TPU v7x, 32 devices: a whole 2x2x4 slice. The times are simulated.
32 devices in a mesh: dp: 8 (over y, x, core), ctx: 4 (over z).
Axes of the slice: x: 2, y: 2, z: 4, core: 2. Of those that a mesh axis runs over, the one named last changes fastest.
Arguments:
- inputs: bfloat16 [8, 512, 2048], P('dp', 'ctx'), may hold values from -6 to 6
- segment: int32 [8, 512], P('dp', 'ctx'), may hold values from 0 to 3, as said below
- w_qkv: bfloat16 [2048, 6144], P(('dp', 'ctx')), may hold values from -0.125 to 0.125
- w_out: bfloat16 [2048, 2048], P(('dp', 'ctx')), may hold values from -0.125 to 0.125
- w_gate: bfloat16 [2048, 8192], P('dp', 'ctx'), may hold values from -0.125 to 0.125
- w_up: bfloat16 [2048, 8192], P('dp', 'ctx'), may hold values from -0.125 to 0.125
- w_down_t: bfloat16 [2048, 8192], P('dp', 'ctx'), may hold values from -0.0625 to 0.0625
- gains: float32 [4, 2048], replicated, may hold values from 0.25 to 1.75
- cotangent: bfloat16 [8, 512, 2048], P('dp', 'ctx'), may hold values from -6 to 6
Outputs:
- output: bfloat16 [8, 512, 2048], P('dp', 'ctx')
- input_grad: float32 [8, 512, 2048], P('dp', 'ctx')
- grad_qkv: float32 [2048, 6144], P(('dp', 'ctx'))
- grad_out: float32 [2048, 2048], P(('dp', 'ctx'))
- grad_gate: float32 [2048, 8192], P('dp', 'ctx')
- grad_up: float32 [2048, 8192], P('dp', 'ctx')
- grad_down_t: float32 [2048, 8192], P('dp', 'ctx')
- grad_gains: float32 [4, 2048], replicated
Inputs may be any that keep to these rules, and one draw needn't show every extreme that they name: `segment`: in every sequence ids 1, 2 and 3 mark three documents in this order, each of one position or more, and 0 marks padding, one position or more at the sequence's end.
All inputs are finite; a program needn't handle non-finite values.
Results may differ from a plain program's by a relative error of at most 0.015.
Values may be sent and summed in bfloat16 or wider, within the bound.
A program may use at most 704 MiB of HBM per device.

v0:
```python
import jax
import jax.numpy as jnp
from jax import lax
from jax.sharding import PartitionSpec as P

HEADS = 16
HEAD_DIM = 128


EPS = 1e-06
ROPE_BASE = 500000.0


def rope_tables(positions):
    half = HEAD_DIM // 2
    frequency = ROPE_BASE ** (-(jnp.arange(half, dtype=jnp.float32) * 2.0 / HEAD_DIM))
    angles = positions[:, None] * frequency[None, :]
    cosine = jnp.cos(angles)
    sine = jnp.sin(angles)
    return (jnp.concatenate([cosine, cosine], 1), jnp.concatenate([sine, sine], 1))


def rotate(values, cosine, sine):
    half = HEAD_DIM // 2
    turned = jnp.concatenate([-values[..., half:], values[..., :half]], -1)
    return values * cosine[:, None, :] + turned * sine[:, None, :]


def norm_rope(values, gain, cosine, sine):
    factor = lax.rsqrt(jnp.mean(values * values, axis=-1, keepdims=True) + EPS)
    normed = (values * factor * gain).reshape(values.shape[0], HEADS, HEAD_DIM)
    return rotate(normed, cosine, sine).reshape(values.shape[0], HEADS * HEAD_DIM)


def post_norm(values, gain):
    return values * lax.rsqrt(jnp.mean(values * values, axis=-1, keepdims=True) + EPS) * gain


def swiglu(gate, up_part):
    return jax.nn.silu(gate) * up_part


def dot_rows(left, right):
    return lax.dot_general(
        left, right, (((1,), (1,)), ((), ())), preferred_element_type=jnp.float32
    )


def dot_first(left, right):
    return lax.dot_general(
        left, right, (((0,), (0,)), ((), ())), preferred_element_type=jnp.float32
    )


def per_device(inputs, segment, w_qkv, w_out, w_gate, w_up, w_down_t, gains, cotangent):
    rows = inputs.shape[1]
    width = inputs.shape[2]
    tokens = inputs[0]
    offset = lax.axis_index("ctx") * rows
    local_place = offset + jnp.arange(rows, dtype=jnp.int32)
    cosine, sine = rope_tables(local_place.astype(jnp.float32))
    qkv_full, out_full = (
        lax.all_gather(w_qkv, ("dp", "ctx"), axis=0, tiled=True),
        lax.all_gather(w_out, ("dp", "ctx"), axis=0, tiled=True),
    )
    mixed = jnp.dot(tokens, qkv_full, preferred_element_type=jnp.float32)
    query_raw = mixed[:, :width]
    key_raw = mixed[:, width : 2 * width]
    query_low = norm_rope(query_raw, gains[0], cosine, sine).astype(jnp.bfloat16)
    key_low = norm_rope(key_raw, gains[1], cosine, sine).astype(jnp.bfloat16)
    value_low = mixed[:, 2 * width :].astype(jnp.bfloat16)
    own_segment = segment[0]
    key_all, value_all, segment_all = (
        lax.all_gather(key_low, "ctx", axis=0, tiled=True),
        lax.all_gather(value_low, "ctx", axis=0, tiled=True),
        lax.all_gather(own_segment.astype(jnp.bfloat16), "ctx", axis=0, tiled=True),
    )
    length = key_all.shape[0]
    key_segment = segment_all.astype(jnp.int32)
    places = jnp.arange(length, dtype=jnp.int32)
    allowed = (
        (own_segment[:, None] == key_segment[None, :])
        & (places[None, :] <= local_place[:, None])
        & ((key_segment[None, :] != 0) | (places[None, :] == local_place[:, None]))
    )
    scale = HEAD_DIM ** (-0.5)
    query_heads = query_low.reshape(rows, HEADS, HEAD_DIM).transpose(1, 0, 2)
    key_heads = key_all.reshape(length, HEADS, HEAD_DIM).transpose(1, 0, 2)
    value_heads = value_all.reshape(length, HEADS, HEAD_DIM).transpose(1, 0, 2)

    def head_forward(item):
        query_head, key_head, value_head = item
        masked = jnp.where(allowed, dot_rows(query_head, key_head) * scale, -1e30)
        row_max = jnp.max(masked, axis=1, keepdims=True)
        weights = jnp.where(allowed, jnp.exp(masked - row_max), 0.0)
        total = jnp.sum(weights, axis=1, keepdims=True)
        shares = (weights / total).astype(jnp.bfloat16)
        result = jnp.dot(shares, value_head, preferred_element_type=jnp.float32)
        return (result, (row_max + jnp.log(total))[:, 0])

    head_out, log_total = lax.map(head_forward, (query_heads, key_heads, value_heads))
    attended_low = head_out.transpose(1, 0, 2).reshape(rows, width).astype(jnp.bfloat16)
    projected = jnp.dot(attended_low, out_full, preferred_element_type=jnp.float32)
    residual = tokens.astype(jnp.float32) + post_norm(projected, gains[2])
    residual_low = residual.astype(jnp.bfloat16)
    gate_rows, up_rows, down_rows = (
        lax.all_gather(w_gate, "dp", axis=0, tiled=True),
        lax.all_gather(w_up, "dp", axis=0, tiled=True),
        lax.all_gather(w_down_t, "dp", axis=0, tiled=True),
    )
    gate_w, up_w, down_w = (gate_rows, up_rows, down_rows)
    ffn_rows = lax.all_gather(residual_low, "ctx", axis=0, tiled=True)
    gate = jnp.dot(ffn_rows, gate_w, preferred_element_type=jnp.float32)
    up_part = jnp.dot(ffn_rows, up_w, preferred_element_type=jnp.float32)
    activated = swiglu(gate, up_part).astype(jnp.bfloat16)
    feed_part = dot_rows(activated, down_w)
    feed = lax.psum_scatter(feed_part, "ctx", scatter_dimension=0, tiled=True)
    output = (residual + post_norm(feed, gains[3])).astype(jnp.bfloat16)
    upstream = cotangent[0].astype(jnp.float32)
    unused_feed, pull_feed = jax.vjp(post_norm, feed, gains[3])
    feed_grad, gain_feed = pull_feed(upstream)
    feed_grad_low = feed_grad.astype(jnp.bfloat16)
    grad_rows = lax.all_gather(feed_grad_low, "ctx", axis=0, tiled=True)
    act_grad = jnp.dot(grad_rows, down_w, preferred_element_type=jnp.float32)
    unused_act, pull_act = jax.vjp(swiglu, gate, up_part)
    gate_grad, up_grad = pull_act(act_grad)
    gate_low = gate_grad.astype(jnp.bfloat16)
    up_low = up_grad.astype(jnp.bfloat16)
    back_part = dot_rows(gate_low, gate_w) + dot_rows(up_low, up_w)
    back_feed = lax.psum_scatter(back_part, "ctx", scatter_dimension=0, tiled=True)
    residual_grad = upstream + back_feed
    left = ffn_rows
    feed_weights = lax.psum_scatter(
        jnp.stack(
            [dot_first(left, gate_low), dot_first(left, up_low), dot_first(grad_rows, activated)], 1
        ),
        "dp",
        scatter_dimension=0,
        tiled=True,
    )
    unused_attn, pull_attn = jax.vjp(post_norm, projected, gains[2])
    projected_grad, gain_attn = pull_attn(residual_grad)
    projected_low = projected_grad.astype(jnp.bfloat16)
    attended_grad = dot_rows(projected_low, out_full)
    grad_heads = (
        attended_grad.astype(jnp.bfloat16).reshape(rows, HEADS, HEAD_DIM).transpose(1, 0, 2)
    )

    def head_backward(item):
        query_head, key_head, value_head, grad_head, log_head = item
        shares = jnp.where(
            allowed, jnp.exp(dot_rows(query_head, key_head) * scale - log_head[:, None]), 0.0
        )
        share_grad = dot_rows(grad_head, value_head)
        inner = jnp.sum(shares * share_grad, axis=1, keepdims=True)
        score_grad = (shares * (share_grad - inner)).astype(jnp.bfloat16)
        query_grad = jnp.dot(score_grad, key_head, preferred_element_type=jnp.float32) * scale
        key_grad = dot_first(score_grad, query_head) * scale
        value_grad = dot_first(shares.astype(jnp.bfloat16), grad_head)
        return (query_grad, key_grad, value_grad)

    query_back, key_back, value_back = lax.map(
        head_backward, (query_heads, key_heads, value_heads, grad_heads, log_total)
    )
    kv_term = jnp.concatenate(
        [
            key_back.transpose(1, 0, 2).reshape(length, width),
            value_back.transpose(1, 0, 2).reshape(length, width),
        ],
        1,
    )
    kv_grad = lax.psum_scatter(kv_term, "ctx", scatter_dimension=0, tiled=True)
    query_grad = query_back.transpose(1, 0, 2).reshape(rows, width)

    def turn_norm(values, gain):
        return norm_rope(values, gain, cosine, sine)

    unused_query, pull_query = jax.vjp(turn_norm, query_raw, gains[0])
    query_raw_grad, gain_query = pull_query(query_grad)
    unused_key, pull_key = jax.vjp(turn_norm, key_raw, gains[1])
    key_raw_grad, gain_key = pull_key(kv_grad[:, :width])
    mixed_grad = jnp.concatenate([query_raw_grad, key_raw_grad, kv_grad[:, width:]], 1).astype(
        jnp.bfloat16
    )
    input_grad = residual_grad + dot_rows(mixed_grad, qkv_full)
    left = tokens
    attention_weights = lax.psum_scatter(
        jnp.concatenate([dot_first(left, mixed_grad), dot_first(attended_low, projected_low)], 1),
        ("dp", "ctx"),
        scatter_dimension=0,
        tiled=True,
    )
    grad_gains = lax.psum(jnp.stack([gain_query, gain_key, gain_attn, gain_feed]), ("dp", "ctx"))
    return (
        output[None],
        input_grad[None],
        attention_weights[:, : 3 * width],
        attention_weights[:, 3 * width :],
        feed_weights[:, 0],
        feed_weights[:, 1],
        feed_weights[:, 2],
        grad_gains,
    )


def solution(mesh):
    in_specs = (
        P("dp", "ctx", None),
        P("dp", "ctx"),
        P(("dp", "ctx"), None),
        P(("dp", "ctx"), None),
        P("dp", "ctx"),
        P("dp", "ctx"),
        P("dp", "ctx"),
        P(),
        P("dp", "ctx", None),
    )
    out_specs = (
        P("dp", "ctx", None),
        P("dp", "ctx", None),
        P(("dp", "ctx"), None),
        P(("dp", "ctx"), None),
        P("dp", "ctx"),
        P("dp", "ctx"),
        P("dp", "ctx"),
        P(),
    )
    return jax.shard_map(
        per_device, mesh=mesh, in_specs=in_specs, out_specs=out_specs, check_vma=False
    )
```

profile of v0, /device:TPU:0, one launch (start us, length us, event | category | flops | bytes accessed | tf_op | source)
XLA Modules:
  0.0 2788.9 jit_solution(4000228823553164613)
XLA Ops:
  8.0 160.3 %all-gather.11.cloned.1.call-done = bf16[2048,6144]{1,0:T(8,128)(2,1)} async-done(((bf16[64,6144]{1,0:T(8,128)(2,1)}), bf16[2048,6144]{1,0:T(8,128)(2,1)}) %all-gather.11.cloned.1.call-update) | async-done | bytes 25165840 | tf_op jit(solution)/shard_map/all_gather | solution.py:63
  196.6 27.0 all-gather.15.cloned.1.call-done
  225.8 44.7 %all-gather.13.cloned.1.call-done = bf16[512,2048]{1,0:T(8,128)(2,1)} async-done(((bf16[128,2048]{1,0:T(8,128)(2,1)}), bf16[512,2048]{1,0:T(8,128)(2,1)}) %all-gather.13.cloned.1.call-update) | async-done | bytes 2097168 | tf_op jit(solution)/shard_map/all_gather | solution.py:74
  274.0 31.0 %while.28 = (s32[]{:T(128)}, bf16[16,128,128]{1,2,0:T(8,128)(2,1)S(1)}, f32[16,128]{1,0:T(8,128)S(1)}, bf16[16,128,128]{2,1,0:T(8,128)(2,1)S(1)}, bf16[16,512,12...) while((s32[]{:T(128)}, ...), condition=%wide.region_5.6_spmd.clone, body=%wide.region_2.5_spmd.clone.sunk | while | flops 35389312 | bytes 1164929 | solution.py:101
  305.0 44.7 %all-gather.17.cloned.1.call-done = bf16[2048,2048]{1,0:T(8,128)(2,1)} async-done(((bf16[64,2048]{1,0:T(8,128)(2,1)}), bf16[2048,2048]{1,0:T(8,128)(2,1)}) %all-gather.17.cloned.1.call-update) | async-done | bytes 8388624 | tf_op jit(solution)/shard_map/all_gather | solution.py:64
  357.6 46.8 %all-gather.21.cloned.1.call-done = bf16[2048,2048]{1,0:T(8,128)(2,1)} async-done(((bf16[256,2048]{1,0:T(8,128)(2,1)}), bf16[2048,2048]{1,0:T(8,128)(2,1)}) %all-gather.21.cloned.1.call-update) | async-done | bytes 8388624 | tf_op jit(solution)/shard_map/all_gather | solution.py:107
  404.4 48.0 %all-gather.19.cloned.1.call-done = bf16[512,2048]{1,0:T(8,128)(2,1)} async-done(((bf16[128,2048]{1,0:T(8,128)(2,1)}), bf16[512,2048]{1,0:T(8,128)(2,1)}) %all-gather.19.cloned.1.call-update) | async-done | bytes 2097168 | tf_op jit(solution)/shard_map/all_gather | solution.py:112
  463.1 44.3 %all-gather.23.cloned.1.call-done = bf16[2048,2048]{1,0:T(8,128)(2,1)} async-done(((bf16[256,2048]{1,0:T(8,128)(2,1)}), bf16[2048,2048]{1,0:T(8,128)(2,1)}) %all-gather.23.cloned.1.call-update) | async-done | bytes 8388624 | tf_op jit(solution)/shard_map/all_gather | solution.py:108
  518.2 45.5 %all-gather.25.cloned.1.call-done = bf16[2048,2048]{1,0:T(8,128)(2,1)} async-done(((bf16[256,2048]{1,0:T(8,128)(2,1)}), bf16[2048,2048]{1,0:T(8,128)(2,1)}) %all-gather.25.cloned.1.call-update) | async-done | bytes 8388624 | tf_op jit(solution)/shard_map/all_gather | solution.py:109
  574.3 76.9 %reduce-scatter.8.cloned.1.call-done = f32[128,2048]{1,0:T(8,128)} async-done(((f32[512,2048]{1,0:T(8,128)}), f32[128,2048]{1,0:T(8,128)}) %reduce-scatter.8.cloned.1.call-update) | async-done | bytes 1048592 | tf_op jit(solution)/shard_map/reduce_scatter | solution.py:117
  657.3 46.4 %all-gather.27.cloned.1.call-done = bf16[512,2048]{1,0:T(8,128)(2,1)} async-done(((bf16[128,2048]{1,0:T(8,128)(2,1)}), bf16[512,2048]{1,0:T(8,128)(2,1)}) %all-gather.27.cloned.1.call-update) | async-done | bytes 2097168 | tf_op jit(solution)/shard_map/all_gather | solution.py:123
  703.7 12.0 multiply_convert_fusion.1
  733.9 75.5 %reduce-scatter.10.cloned.1.call-done = f32[128,2048]{1,0:T(8,128)} async-done(((f32[512,2048]{1,0:T(8,128)}), f32[128,2048]{1,0:T(8,128)}) %reduce-scatter.10.cloned.1.call-update) | async-done | bytes 1048592 | tf_op jit(solution)/shard_map/reduce_scatter | solution.py:130
  821.3 98.8 %while.29 = (s32[]{:T(128)}, f32[16,128,128]{2,1,0:T(8,128)S(1)}, f32[16,512,128]{2,1,0:T(8,128)}, f32[16,512,128]{2,1,0:T(8,128)}, bf16[16,128,128]{2,1,0:T(8,1...) while((s32[]{:T(128)}, f32[16,128,128]{2,1,0:T(8,128)S(1)}, ...), condition=%wide.region_14.15_spmd.clone, body=%wide.region_12.14_spmd.clone.sunk | while | flops 84950912 | bytes 3091601 | solution.py:162
  928.2 12.7 convolution_bitcast_fusion.3
  957.6 35.9 %pad_maximum_fusion.1 = f32[2048,3,2048]{2,0,1:T(8,128)} fusion(f32[2048,1,2048]{2,0,1:T(8,128)} %convolution_bitcast_fusion.3, f32[2048,1,2048]{2,0,1:T(8,128)} %convolution_bitcast_fusion.4, f32[2048,1,2048]{2,0,1:T(8,128)} %convolution_bitcast_fusion.5), kind=kLoop, calls=%fused_computation.70 | loop fusion | flops 25165824 | bytes 100663296 | tf_op jit(solution)/shard_map/stack | solution.py:134
  1003.4 69.6 %reduce-scatter.12.cloned.1.call-done = f32[128,4096]{1,0:T(8,128)} async-done(((f32[512,4096]{1,0:T(8,128)}), f32[128,4096]{1,0:T(8,128)}) %reduce-scatter.12.cloned.1.call-update) | async-done | bytes 2097168 | tf_op jit(solution)/shard_map/reduce_scatter | solution.py:172
  1081.4 34.1 %convolution_bitcast_fusion.2 = f32[2048,6144]{0,1:T(8,128)} fusion(bf16[128,2048]{1,0:T(8,128)(2,1)} %slice.114, bf16[128,2048]{1,0:T(8,128)(2,1)} %get-tuple-element.257, bf16[128,2048]{1,0:T(8,128)(2,1)} %get-tuple-element.256, bf16[1,128,2048]{2,1,0:T(8,128)(2,1)} %param.13), kind=kOutput, calls=%fused_computation.71 | convolution fusion | flops 3225944064 | bytes 52428800 | tf_op jit(solution)/shard_map/dot_general | solution.py:50
  1115.5 50.7 %pad_maximum_fusion = f32[2048,8192]{0,1:T(8,128)} fusion(f32[2048,2048]{0,1:T(8,128)} %fusion.98, f32[2048,6144]{0,1:T(8,128)} %convolution_bitcast_fusion.2), kind=kLoop, calls=%fused_computation.69 | loop fusion | flops 16777216 | bytes 134217728 | tf_op jit(solution)/shard_map/concatenate | solution.py:188
  1166.3 64.5 %copy.46 = f32[2048,8192]{1,0:T(8,128)} copy(f32[2048,8192]{0,1:T(8,128)} %pad_maximum_fusion) | data formatting | bytes 134217728
  1231.5 43.6 %psum.7 = f32[4,2048]{1,0:T(4,128)} all-reduce(f32[4,2048]{1,0:T(4,128)S(1)} %pad_maximum_fusion.8), channel_id=1, replica_groups=mesh['dp'=8,'ctx'=4] {'dp','ctx'}, use_global_device_ids=true, to_apply=%region_24.25 | all-reduce | flops 8192 | bytes 65536 | tf_op jit(solution)/shard_map/psum | solution.py:193
  1275.1 14.5 fusion.60
  1289.6 75.1 %reduce-scatter.14.cloned.1.call-done = f32[256,3,2048]{2,0,1:T(8,128)} async-done(((f32[2048,3,2048]{2,0,1:T(8,128)}), f32[256,3,2048]{2,0,1:T(8,128)}) %reduce-scatter.14.cloned.1.call-update) | async-done | bytes 6291472 | tf_op jit(solution)/shard_map/reduce_scatter | solution.py:133
  1370.5 1407.2 %reduce-scatter.16.cloned.1.call-done = f32[64,8192]{1,0:T(8,128)} async-done(((f32[2048,8192]{1,0:T(8,128)}), f32[64,8192]{1,0:T(8,128)}) %reduce-scatter.16.cloned.1.call-update) | async-done | bytes 2097168
  (377 shorter events, 293.3 us)
Async XLA Ops:
  7.2 161.1 %all-gather.11.cloned.1.call-start = ((), (), s32[]{:S(2)}) async-start(), calls=%async_computation.5 | async-start | bytes 25952256 | tf_op jit(solution)/shard_map/all_gather | solution.py:63
  7.9 215.8 %all-gather.15.cloned.1.call-start = ((), (), s32[]{:S(2)}) async-start(), calls=%async_computation.7 | async-start | bytes 2621440 | tf_op jit(solution)/shard_map/all_gather | solution.py:75
  8.0 172.0 %copy-start.27 = (f32[4,2048]{1,0:T(4,128)S(1)}, f32[4,2048]{1,0:T(4,128)}, u32[]{:S(2)}) copy-start(f32[4,2048]{1,0:T(4,128)} %param.20) | copy-start | bytes 98308
  179.4 91.1 %all-gather.13.cloned.1.call-start = ((), (), s32[]{:S(2)}) async-start(), calls=%async_computation.6 | async-start | bytes 2621440 | tf_op jit(solution)/shard_map/all_gather | solution.py:74
  185.1 164.6 %all-gather.17.cloned.1.call-start = ((), (), s32[]{:S(2)}) async-start(), calls=%async_computation.8 | async-start | bytes 8650752 | tf_op jit(solution)/shard_map/all_gather | solution.py:64
  185.7 218.8 %all-gather.21.cloned.1.call-start = ((), (), s32[]{:S(2)}) async-start(), calls=%async_computation.10 | async-start | bytes 9437184 | tf_op jit(solution)/shard_map/all_gather | solution.py:107
  186.3 266.1 %all-gather.19.cloned.1.call-start = ((), (), s32[]{:S(2)}) async-start(), calls=%async_computation.9 | async-start | bytes 2621440 | tf_op jit(solution)/shard_map/all_gather | solution.py:112
  305.0 44.7 %copy-start.10 = (bf16[16,512,128]{2,1,0:T(8,128)(2,1)}, bf16[16,512,128]{2,1,0:T(8,128)(2,1)S(1)}, u32[]{:S(2)}) copy-start(bf16[16,512,128]{2,1,0:T(8,128)(2,1)S(1)} %get-tuple-element.537) | copy-start | bytes 6291460
  305.0 49.5 %copy-start.11 = (bf16[16,128,128]{1,2,0:T(8,128)(2,1)}, bf16[16,128,128]{1,2,0:T(8,128)(2,1)S(1)}, u32[]{:S(2)}) copy-start(bf16[16,128,128]{1,2,0:T(8,128)(2,1)S(1)} %get-tuple-element.100) | copy-start | bytes 1572868
  305.0 49.5 %copy-start.20 = (bf16[16,128,128]{2,1,0:T(8,128)(2,1)}, bf16[16,128,128]{2,1,0:T(8,128)(2,1)S(1)}, u32[]{:S(2)}) copy-start(bf16[16,128,128]{2,1,0:T(8,128)(2,1)S(1)} %get-tuple-element.557) | copy-start | bytes 1572868
  355.6 151.8 %all-gather.23.cloned.1.call-start = ((), (), s32[]{:S(2)}) async-start(), calls=%async_computation.11 | async-start | bytes 9437184 | tf_op jit(solution)/shard_map/all_gather | solution.py:108
  356.3 207.4 %all-gather.25.cloned.1.call-start = ((), (), s32[]{:S(2)}) async-start(), calls=%async_computation.12 | async-start | bytes 9437184 | tf_op jit(solution)/shard_map/all_gather | solution.py:109
  357.1 294.1 %reduce-scatter.8.cloned.1.call-start = ((), (), s32[]{:S(2)}) async-start(), calls=%async_computation.13 | async-start | bytes 5242880 | tf_op jit(solution)/shard_map/reduce_scatter | solution.py:117
  452.4 55.0 %copy-start.37 = (bf16[512,2048]{1,0:T(8,128)(2,1)S(1)}, bf16[512,2048]{1,0:T(8,128)(2,1)}, u32[]{:S(2)}) copy-start(bf16[512,2048]{1,0:T(8,128)(2,1)} %all-gather.19.cloned.1.call-done) | copy-start | bytes 6291460
  574.3 78.3 %copy-start.4 = (bf16[1,128,2048]{2,1,0:T(8,128)(2,1)S(1)}, bf16[1,128,2048]{2,1,0:T(8,128)(2,1)}, u32[]{:S(2)}) copy-start(bf16[1,128,2048]{2,1,0:T(8,128)(2,1)} %param.21) | copy-start | bytes 1572868
  574.3 129.4 %all-gather.27.cloned.1.call-start = ((), (), s32[]{:S(2)}) async-start(), calls=%async_computation.14 | async-start | bytes 2621440 | tf_op jit(solution)/shard_map/all_gather | solution.py:123
  657.1 152.4 %reduce-scatter.10.cloned.1.call-start = ((), (), s32[]{:S(2)}) async-start(), calls=%async_computation.15 | async-start | bytes 5242880 | tf_op jit(solution)/shard_map/reduce_scatter | solution.py:130
  733.8 77.9 %copy-start.2 = (f32[128,2048]{1,0:T(8,128)S(1)}, f32[128,2048]{1,0:T(8,128)}, u32[]{:S(2)}) copy-start(f32[128,2048]{1,0:T(8,128)} %reduce-scatter.8.cloned.1.call-done) | copy-start | bytes 3145732
  733.8 339.2 %reduce-scatter.12.cloned.1.call-start = ((), (), s32[]{:S(2)}) async-start(), calls=%async_computation.16 | async-start | bytes 10485760 | tf_op jit(solution)/shard_map/reduce_scatter | solution.py:172
  927.9 436.8 %reduce-scatter.14.cloned.1.call-start = ((), (), s32[]{:S(2)}) async-start(), calls=%async_computation.17 | async-start | bytes 56623104 | tf_op jit(solution)/shard_map/reduce_scatter | solution.py:133
  993.5 1784.2 %reduce-scatter.16.cloned.1.call-start = ((), (), s32[]{:S(2)}) async-start(), calls=%async_computation.18 | async-start | bytes 69206016
  1230.8 44.3 %copy-start.5 = (bf16[1,128,2048]{2,1,0:T(8,128)(2,1)S(1)}, bf16[1,128,2048]{2,1,0:T(8,128)(2,1)}, u32[]{:S(2)}) copy-start(bf16[1,128,2048]{2,1,0:T(8,128)(2,1)} %param.21) | copy-start | bytes 1572868
  1230.8 44.3 %copy-start.9 = (f32[128,2048]{1,0:T(8,128)S(1)}, f32[128,2048]{1,0:T(8,128)}, u32[]{:S(2)}) copy-start(f32[128,2048]{1,0:T(8,128)} %reduce-scatter.10.cloned.1.call-done) | copy-start | bytes 3145732
  1230.8 44.3 %copy-start.13 = (bf16[128,2048]{1,0:T(8,128)(2,1)S(1)}, bf16[128,2048]{1,0:T(8,128)(2,1)}, u32[]{:S(2)}) copy-start(bf16[128,2048]{1,0:T(8,128)(2,1)} %get-tuple-element.256) | copy-start | bytes 1572868
  (33 other events, 197.9 us)
Sparse Core Ops, SparseCore 0:
  10.9 157.3 all-gather.10
  179.5 44.1 all-gather.14
  225.8 44.6 all-gather.12
  273.3 76.2 all-gather.16
  351.4 52.9 all-gather.20
  406.4 45.9 all-gather.18
  454.3 53.0 all-gather.22
  509.3 54.3 all-gather.24
  574.4 76.7 reduce-scatter.7
  657.2 46.4 all-gather.26
  734.0 75.4 reduce-scatter.9
  928.0 144.9 reduce-scatter.11
  1076.7 288.0 reduce-scatter.13
  1367.1 1410.5 reduce-scatter.15
where the time goes:
time: 2800 us; the launch traced here: 2790 us
  waiting for transfers between devices  2220 us (79%)
  matrix products  292 us (10%)
  other arithmetic  118 us (4%)
  local copies, waits for them, and re-layouts  94.1 us (3%)
  blocking collectives  52.7 us (2%)
    unnamed x15, waiting for transfers between devices  1410 us
    all_gather x1, waiting for transfers between devices, per_device(): lax.all_gather(w_qkv, ('dp', 'ctx'), axis=0, tiled=True)  160 us
    dot_general x37, matrix products, dot_first(): lax.dot_general(left, right, (((0,), (0,)), ((), ())), preferred_element_...  113 us
    dot_general x53, matrix products, dot_rows(): lax.dot_general(left, right, (((1,), (1,)), ((), ())), preferred_element_...  106 us
    reduce_scatter x1, waiting for transfers between devices, per_device(): feed = lax.psum_scatter(feed_part, 'ctx', scatter_dimension=0, tiled=True)  76.9 us
    reduce_scatter x1, waiting for transfers between devices, per_device(): lax.psum_scatter(back_part, 'ctx', scatter_dimension=0, tiled=True)  75.5 us
    reduce_scatter x1, waiting for transfers between devices, per_device(): lax.psum_scatter(jnp.stack([dot_first(left, gate_low), dot_first(left, up...  75.1 us
    unnamed x91, local copies, waits for them, and re-layouts  69.7 us
  transfers between devices with their start and end apart: 14, of which 14 were waited for; matrix products, arithmetic and copies ran while one was open for 12% of the time, Pallas kernels for 0%

commit v1 on v0

v1 whole, which is shorter than its diff:
```python
import jax
import jax.numpy as jnp
from jax import lax
from jax.sharding import Mesh
from jax.sharding import PartitionSpec as P

HEAD_DIM = 128
EPS = 1e-06
ROPE_BASE = 500000.0
F32 = jnp.float32
BF16 = jnp.bfloat16
GROUP = ("core", "ctx")
ALL = ("chip", "core", "ctx")


def rope_tables(positions):
    half = HEAD_DIM // 2
    frequency = ROPE_BASE ** (-(jnp.arange(half, dtype=F32) * 2.0 / HEAD_DIM))
    angles = positions[:, None] * frequency[None, :]
    cosine = jnp.cos(angles)
    sine = jnp.sin(angles)
    return (jnp.concatenate([cosine, cosine], 1), jnp.concatenate([sine, sine], 1))


def rotate(values, cosine, sine):
    half = HEAD_DIM // 2
    turned = jnp.concatenate([-values[..., half:], values[..., :half]], -1)
    return values * cosine + turned * sine


def rotate_back(values, cosine, sine):
    half = HEAD_DIM // 2
    scaled = values * sine
    turned = jnp.concatenate([scaled[..., half:], -scaled[..., :half]], -1)
    return values * cosine + turned


def dot(left, right):
    return jnp.dot(left, right, preferred_element_type=F32)


def dot_rows(left, right):
    return lax.dot_general(left, right, (((1,), (1,)), ((), ())), preferred_element_type=F32)


def dot_first(left, right):
    return lax.dot_general(left, right, (((0,), (0,)), ((), ())), preferred_element_type=F32)


def gather(values, axes):
    return lax.all_gather(values, axes, axis=0, tiled=True)


def scatter_sum(values, axes):
    return lax.psum_scatter(values, axes, scatter_dimension=0, tiled=True)


def norm_factor(values):
    return lax.rsqrt(jnp.mean(values * values, axis=-1, keepdims=True) + EPS)


def norm_back(values, factor, gain, grad):
    normed = values * factor
    scaled = gain * grad
    back = factor * (scaled - normed * jnp.mean(scaled * normed, axis=-1, keepdims=True))
    return back, jnp.sum(grad * normed, axis=0)


def per_device(inputs, segment, w_qkv, w_out, w_gate, w_up, w_down_t, gains, cotangent):
    rows, width = inputs.shape[1:]
    cores = lax.axis_size("core")
    spans = lax.axis_size("ctx")
    members = cores * spans
    length = rows * spans
    total_rows = cores * length
    part = width // members
    heads = part // HEAD_DIM
    member = lax.axis_index(GROUP)
    tokens = inputs[0]

    qkv_rows = w_qkv.shape[0]
    qkv_cut = w_qkv.reshape(qkv_rows, 3, members, part).transpose(2, 0, 1, 3)
    qkv_cut = qkv_cut.reshape(members, qkv_rows, 3 * part)
    qkv_cut = lax.all_to_all(qkv_cut, GROUP, 0, 0, tiled=True)
    qkv_w = gather(qkv_cut.reshape(members * qkv_rows, 3 * part), "chip")
    tokens_all = gather(tokens, GROUP)
    out_full = gather(w_out, ALL)
    out_w = lax.dynamic_slice_in_dim(out_full, member * part, part, 0)

    hidden = w_gate.shape[1] // cores
    gate_up = jnp.concatenate(
        [w_gate.reshape(-1, cores, 1, hidden), w_up.reshape(-1, cores, 1, hidden)], 2
    ).reshape(-1, cores * 2 * hidden)
    gate_up = lax.all_to_all(gate_up, "core", 1, 0, tiled=True)
    gate_up_w = gather(gate_up, "chip")
    down_w = gather(lax.all_to_all(w_down_t, "core", 1, 0, tiled=True), "chip")

    mixed = dot(tokens_all, qkv_w)
    query_raw = mixed[:, :part]
    key_raw = mixed[:, part : 2 * part]
    value_low = mixed[:, 2 * part :].astype(BF16)
    squares = jnp.stack([jnp.sum(query_raw * query_raw, 1), jnp.sum(key_raw * key_raw, 1)])
    squares = lax.psum(squares, GROUP)
    factors = lax.rsqrt(squares / width + EPS)
    gain_q = lax.dynamic_slice_in_dim(gains[0], member * part, part)
    gain_k = lax.dynamic_slice_in_dim(gains[1], member * part, part)
    places = jnp.arange(length, dtype=jnp.int32)
    cosine, sine = rope_tables(places.astype(F32))
    cosine, sine = cosine[None, :, None, :], sine[None, :, None, :]
    shape = (cores, length, heads, HEAD_DIM)
    query_factor, key_factor = factors[0][:, None], factors[1][:, None]
    query_low = rotate((query_raw * query_factor * gain_q).reshape(shape), cosine, sine).astype(BF16)
    key_low = rotate((key_raw * key_factor * gain_k).reshape(shape), cosine, sine).astype(BF16)
    value_low = value_low.reshape(shape)

    ids = gather(segment[0], GROUP).reshape(cores, length)
    allowed = (
        (ids[:, :, None] == ids[:, None, :])
        & (places[None, None, :] <= places[None, :, None])
        & ((ids[:, None, :] != 0) | (places[None, None, :] == places[None, :, None]))
    )[:, None]
    scale = HEAD_DIM ** (-0.5)
    scores = jnp.einsum("bqhd,bkhd->bhqk", query_low, key_low, preferred_element_type=F32) * scale
    masked = jnp.where(allowed, scores, -1e30)
    row_max = jnp.max(masked, axis=-1, keepdims=True)
    weights = jnp.where(allowed, jnp.exp(masked - row_max), 0.0)
    shares = weights / jnp.sum(weights, axis=-1, keepdims=True)
    shares_low = shares.astype(BF16)
    attended = jnp.einsum("bhqk,bkhd->bqhd", shares_low, value_low, preferred_element_type=F32)
    attended_low = attended.reshape(total_rows, part).astype(BF16)
    projected = scatter_sum(dot(attended_low, out_w).astype(BF16), GROUP).astype(F32)

    tokens_wide = tokens.astype(F32)
    proj_factor = norm_factor(projected)
    residual = tokens_wide + projected * proj_factor * gains[2]
    residual_all = gather(residual.astype(BF16), GROUP)

    gate_up_out = dot(residual_all, gate_up_w)
    gate, up_part = gate_up_out[:, :hidden], gate_up_out[:, hidden:]
    sigmoid = 1.0 / (1.0 + jnp.exp(-gate))
    activated = (gate * sigmoid * up_part).astype(BF16)
    feed = scatter_sum(dot_rows(activated, down_w).astype(BF16), GROUP).astype(F32)
    feed_factor = norm_factor(feed)
    output = (residual + feed * feed_factor * gains[3]).astype(BF16)
    upstream = cotangent[0].astype(F32)
    feed_grad, gain_feed = norm_back(feed, feed_factor, gains[3], upstream)
    feed_grad_all = gather(feed_grad.astype(BF16), GROUP)

    act_grad = dot(feed_grad_all, down_w)
    gate_grad = act_grad * up_part * sigmoid * (1.0 + gate * (1.0 - sigmoid))
    up_grad = act_grad * (gate * sigmoid)
    gate_up_grad = jnp.concatenate([gate_grad.astype(BF16), up_grad.astype(BF16)], 1)
    back_feed = scatter_sum(dot_rows(gate_up_grad, gate_up_w).astype(BF16), GROUP).astype(F32)
    residual_grad = upstream + back_feed

    grad_gate_up = scatter_sum(dot_first(residual_all, gate_up_grad).astype(BF16), "chip")
    grad_gate_up = lax.all_to_all(grad_gate_up, "core", 0, 1, tiled=True)
    grad_gate_up = grad_gate_up.reshape(-1, cores, 2, hidden).astype(F32)
    grad_gate = grad_gate_up[:, :, 0].reshape(-1, cores * hidden)
    grad_up = grad_gate_up[:, :, 1].reshape(-1, cores * hidden)
    grad_down = scatter_sum(dot_first(feed_grad_all, activated).astype(BF16), "chip")
    grad_down = lax.all_to_all(grad_down, "core", 0, 1, tiled=True).astype(F32)

    projected_grad, gain_attn = norm_back(projected, proj_factor, gains[2], residual_grad)
    projected_all = gather(projected_grad.astype(BF16), GROUP)
    attended_grad = dot_rows(projected_all, out_w).astype(BF16).reshape(shape)

    share_grad = jnp.einsum("bqhd,bkhd->bhqk", attended_grad, value_low, preferred_element_type=F32)
    inner = jnp.sum(shares * share_grad, axis=-1, keepdims=True)
    score_grad = (shares * (share_grad - inner)).astype(BF16)
    query_grad = jnp.einsum("bhqk,bkhd->bqhd", score_grad, key_low, preferred_element_type=F32)
    key_grad = jnp.einsum("bhqk,bqhd->bkhd", score_grad, query_low, preferred_element_type=F32)
    value_grad = jnp.einsum("bhqk,bqhd->bkhd", shares_low, attended_grad, preferred_element_type=F32)
    query_turn = rotate_back(query_grad * scale, cosine, sine).reshape(total_rows, part)
    key_turn = rotate_back(key_grad * scale, cosine, sine).reshape(total_rows, part)
    query_norm, key_norm = query_raw * query_factor, key_raw * key_factor
    sums = jnp.stack(
        [jnp.sum(gain_q * query_turn * query_norm, 1), jnp.sum(gain_k * key_turn * key_norm, 1)]
    )
    means = lax.psum(sums, GROUP) / width
    query_mixed = query_factor * (gain_q * query_turn - query_norm * means[0][:, None])
    key_mixed = key_factor * (gain_k * key_turn - key_norm * means[1][:, None])
    gain_query = jnp.sum(query_turn * query_norm, 0)
    gain_key = jnp.sum(key_turn * key_norm, 0)
    mixed_grad = jnp.concatenate(
        [query_mixed, key_mixed, value_grad.reshape(total_rows, part)], 1
    ).astype(BF16)
    input_part = dot_rows(mixed_grad, qkv_w).astype(BF16)
    input_grad = residual_grad + scatter_sum(input_part, GROUP).astype(F32)

    grad_qkv = scatter_sum(dot_first(tokens_all, mixed_grad).astype(BF16), "chip")
    grad_qkv = grad_qkv.reshape(members, qkv_rows, 3 * part)
    grad_qkv = lax.all_to_all(grad_qkv, GROUP, 0, 0, tiled=True)
    grad_qkv = grad_qkv.reshape(members, qkv_rows, 3, part).transpose(1, 2, 0, 3)
    grad_qkv = grad_qkv.reshape(qkv_rows, 3 * width).astype(F32)

    out_part = dot_first(attended_low, projected_all).astype(BF16)
    out_part = lax.dynamic_update_slice_in_dim(
        jnp.zeros((width, width), BF16), out_part, member * part, 0
    )
    grad_out = scatter_sum(out_part, ALL).astype(F32)

    wide = jnp.zeros((2, width), F32)
    wide = lax.dynamic_update_slice(wide, jnp.stack([gain_query, gain_key]), (0, member * part))
    grad_gains = lax.psum(jnp.concatenate([wide, gain_attn[None], gain_feed[None]]), ALL)
    return (
        output[None],
        input_grad[None],
        grad_qkv,
        grad_out,
        grad_gate,
        grad_up,
        grad_down,
        grad_gains,
    )


def solution(mesh):
    cores = 2
    chips = mesh.shape["dp"] // cores
    split = Mesh(mesh.devices.reshape(chips, cores, mesh.shape["ctx"]), ALL)
    dp = ("chip", "core")
    every = P((*dp, "ctx"), None)
    in_specs = (
        P(dp, "ctx", None),
        P(dp, "ctx"),
        every,
        every,
        P(dp, "ctx"),
        P(dp, "ctx"),
        P(dp, "ctx"),
        P(),
        P(dp, "ctx", None),
    )
    out_specs = (
        P(dp, "ctx", None),
        P(dp, "ctx", None),
        every,
        every,
        P(dp, "ctx"),
        P(dp, "ctx"),
        P(dp, "ctx"),
        P(),
    )
    return jax.shard_map(
        per_device, mesh=split, in_specs=in_specs, out_specs=out_specs, check_vma=False
    )
```

time: 2800 us -> 1310 us (0.47)
  waiting for transfers between devices: 2220 us -> 885 us
  matrix products: 292 us -> 116 us
  blocking collectives: 52.7 us -> 153 us
  other arithmetic: 118 us -> 39.9 us
    unnamed x15 -> x16, waiting for transfers between devices: 1410 us -> 1.61 us
    reduce_scatter x4 -> x8, waiting for transfers between devices: 297 us -> 559 us  [scatter_sum(): return lax.psum_scatter(values, axes, scatter_dimension=0, tiled=True)]
    all_gather x9 -> x8, waiting for transfers between devices: 508 us -> 325 us  [gather(): return lax.all_gather(values, axes, axis=0, tiled=True)]
    dot_general x37 -> x4, matrix products: 113 us -> 31.8 us  [dot_first(): lax.dot_general(left, right, (((0,), (0,)), ((), ())), preferred_element_...]
    dot_general x53 -> x4, matrix products: 106 us -> 34.2 us  [dot_rows(): lax.dot_general(left, right, (((1,), (1,)), ((), ())), preferred_element_...]
    concatenate x4 -> x2, other arithmetic: 54.7 us -> 1.84 us  [the longest x1 1.82 us: per_device(): jnp.concatenate([w_gate.reshape(-1, cores, 1, hidden), w_up.reshape(-1, c...]
    psum x1 -> x3, blocking collectives: 43.6 us -> 95 us  [the longest x1 64 us: per_device(): lax.psum(jnp.concatenate([wide, gain_attn[None], gain_feed[None]]), ALL)]
    all_to_all x0 -> x4, blocking collectives: none -> 45.5 us  [the longest x1 26.9 us: per_device(): qkv_cut = lax.all_to_all(qkv_cut, GROUP, 0, 0, tiled=True)]
  transfers between devices with their start and end apart: 14 -> 18, of which waited for: 14 -> 15; matrix products, arithmetic and copies ran while one was open for 12% -> 14% of each run, Pallas kernels for 0% -> 0%
where the time goes in v1:
time: 1310 us; the launch traced here: 1300 us
  waiting for transfers between devices  885 us (68%)
  blocking collectives  153 us (12%)
  matrix products  116 us (9%)
  local copies, waits for them, and re-layouts  83.5 us (6%)
  other arithmetic  39.9 us (3%)
  between operations  14.7 us (1%)
    reduce_scatter x8, waiting for transfers between devices, scatter_sum(): return lax.psum_scatter(values, axes, scatter_dimension=0, tiled=True)  559 us
    all_gather x8, waiting for transfers between devices, gather(): return lax.all_gather(values, axes, axis=0, tiled=True)  325 us
    psum x1, blocking collectives, per_device(): lax.psum(jnp.concatenate([wide, gain_attn[None], gain_feed[None]]), ALL)  64 us
    dot_general x4, matrix products, dot(): return jnp.dot(left, right, preferred_element_type=F32)  34.9 us
    dot_general x4, matrix products, dot_rows(): lax.dot_general(left, right, (((1,), (1,)), ((), ())), preferred_element_...  34.2 us
    dot_general x4, matrix products, dot_first(): lax.dot_general(left, right, (((0,), (0,)), ((), ())), preferred_element_...  31.8 us
    all_to_all x1, blocking collectives, per_device(): qkv_cut = lax.all_to_all(qkv_cut, GROUP, 0, 0, tiled=True)  26.9 us
  transfers between devices with their start and end apart: 18, of which 15 were waited for; matrix products, arithmetic and copies ran while one was open for 14% of the time, Pallas kernels for 0%

profile of v1, /device:TPU:0, one launch (start us, length us, event | category | flops | bytes accessed | tf_op | source)
XLA Modules:
  0.0 1303.1 jit_solution(13197521999439722919)
XLA Ops:
  9.9 26.9 %all_to_all.74 = bf16[8,64,768]{2,1,0:T(8,128)(2,1)} all-to-all(bf16[8,64,768]{2,1,0:T(8,128)(2,1)S(1)} %reshape.177), channel_id=1, replica_groups=mesh['chip'=4,'core'=2,'ctx'=4] {'core','ctx'}, dimensions={0} | all-to-all | bytes 1572864 | tf_op jit(solution)/shard_map/all_to_all | solution.py:84
  38.3 12.7 all-gather.1
  55.5 23.9 %all-gather.11.cloned.1.call-done = bf16[2048,768]{1,0:T(8,128)(2,1)} async-done(((bf16[512,768]{1,0:T(8,128)(2,1)}), bf16[2048,768]{1,0:T(8,128)(2,1)}) %all-gather.11.cloned.1.call-update) | async-done | bytes 3145744 | tf_op jit(solution)/shard_map/all_gather | solution.py:51
  79.3 48.8 %all-gather.25.cloned.1.call-done = bf16[1,1024,2048]{2,1,0:T(8,128)(2,1)} async-done(((bf16[1,128,2048]{2,1,0:T(8,128)(2,1)}), bf16[1,1024,2048]{2,1,0:T(8,128)(2,1)}) %all-gather.25.cloned.1.call-update) | async-done | bytes 4194320 | tf_op jit(solution)/shard_map/all_gather | solution.py:51
  135.4 15.3 %psum.21 = f32[2,1024]{1,0:T(2,128)S(1)} all-reduce(f32[2,1024]{1,0:T(2,128)S(1)} %pad_maximum_fusion.10), channel_id=1, replica_groups=mesh['chip'=4,'core'=2,'ctx'=4] {'core','ctx'}, use_global_device_ids=true, to_apply=%region_2.0 | all-reduce | flops 2048 | bytes 16384 | tf_op jit(solution)/shard_map/psum | solution.py:103
  184.0 23.5 %all-gather.13.cloned.1.call-done = bf16[2048,2048]{1,0:T(8,128)(2,1)} async-done(((bf16[64,2048]{1,0:T(8,128)(2,1)}), bf16[2048,2048]{1,0:T(8,128)(2,1)}) %all-gather.13.cloned.1.call-update) | async-done | bytes 8388624 | tf_op jit(solution)/shard_map/all_gather | solution.py:51
  228.9 71.1 %reduce-scatter.9.cloned.1.call-done = bf16[128,2048]{1,0:T(8,128)(2,1)} async-done(((bf16[1024,2048]{1,0:T(8,128)(2,1)}), bf16[128,2048]{1,0:T(8,128)(2,1)}) %reduce-scatter.9.cloned.1.call-update) | async-done | bytes 524304 | tf_op jit(solution)/shard_map/reduce_scatter | solution.py:55
  315.2 74.4 %all-gather.17.cloned.1.call-done = bf16[2048,2048]{1,0:T(8,128)(2,1)} async-done(((bf16[512,2048]{1,0:T(8,128)(2,1)}), bf16[2048,2048]{1,0:T(8,128)(2,1)}) %all-gather.17.cloned.1.call-update) | async-done | bytes 8388624 | tf_op jit(solution)/shard_map/all_gather | solution.py:51
  389.7 49.2 %all-gather.15.cloned.1.call-done = bf16[1024,2048]{1,0:T(8,128)(2,1)} async-done(((bf16[128,2048]{1,0:T(8,128)(2,1)}), bf16[1024,2048]{1,0:T(8,128)(2,1)}) %all-gather.15.cloned.1.call-update) | async-done | bytes 4194320 | tf_op jit(solution)/shard_map/all_gather | solution.py:51
  438.9 12.5 fusion.74
  457.4 35.4 %all-gather.19.cloned.1.call-done = bf16[2048,1024]{1,0:T(8,128)(2,1)} async-done(((bf16[512,1024]{1,0:T(8,128)(2,1)}), bf16[2048,1024]{1,0:T(8,128)(2,1)}) %all-gather.19.cloned.1.call-update) | async-done | bytes 4194320 | tf_op jit(solution)/shard_map/all_gather | solution.py:51
  502.1 89.1 %reduce-scatter.11.cloned.1.call-done = bf16[128,2048]{1,0:T(8,128)(2,1)} async-done(((bf16[1024,2048]{1,0:T(8,128)(2,1)}), bf16[128,2048]{1,0:T(8,128)(2,1)}) %reduce-scatter.11.cloned.1.call-update) | async-done | bytes 524304 | tf_op jit(solution)/shard_map/reduce_scatter | solution.py:55
  597.0 46.5 %all-gather.21.cloned.1.call-done = bf16[1024,2048]{1,0:T(8,128)(2,1)} async-done(((bf16[128,2048]{1,0:T(8,128)(2,1)}), bf16[1024,2048]{1,0:T(8,128)(2,1)}) %all-gather.21.cloned.1.call-update) | async-done | bytes 4194320 | tf_op jit(solution)/shard_map/all_gather | solution.py:51
  643.5 11.6 multiply_convert_fusion.2
  657.2 12.7 convolution_convert_fusion.1
  669.9 87.8 %reduce-scatter.13.cloned.1.call-done = bf16[128,2048]{1,0:T(8,128)(2,1)} async-done(((bf16[1024,2048]{1,0:T(8,128)(2,1)}), bf16[128,2048]{1,0:T(8,128)(2,1)}) %reduce-scatter.13.cloned.1.call-update) | async-done | bytes 524304 | tf_op jit(solution)/shard_map/reduce_scatter | solution.py:55
  763.0 9.4 convolution_convert_fusion.4
  772.5 14.0 %convolution_convert_fusion = bf16[2048,2048]{1,0:T(8,128)(2,1)} fusion(bf16[1024,2048]{1,0:T(8,128)(2,1)} %all-gather.15.cloned.1.call-done, bf16[1024,1024]{1,0:T(8,128)(2,1)} %copy-done.24, bf16[1024,1024]{1,0:T(8,128)(2,1)} %copy-done.23), kind=kOutput, calls=%fused_computation.1 | convolution fusion | flops 8602517504 | bytes 16777216 | tf_op jit(solution)/shard_map/dot_general | solution.py:47
  786.9 22.9 %all-gather.23.cloned.1.call-done = bf16[1024,2048]{1,0:T(8,128)(2,1)} async-done(((bf16[128,2048]{1,0:T(8,128)(2,1)}), bf16[1024,2048]{1,0:T(8,128)(2,1)}) %all-gather.23.cloned.1.call-update) | async-done | bytes 4194320 | tf_op jit(solution)/shard_map/all_gather | solution.py:51
  830.7 15.6 %psum.22 = f32[2,1024]{1,0:T(2,128)S(1)} all-reduce(f32[2,1024]{1,0:T(2,128)S(1)} %pad_maximum_fusion.11), channel_id=1, replica_groups=mesh['chip'=4,'core'=2,'ctx'=4] {'core','ctx'}, use_global_device_ids=true, to_apply=%region_15.16 | all-reduce | flops 2048 | bytes 16384 | tf_op jit(solution)/shard_map/psum | solution.py:180
  878.0 76.0 %reduce-scatter.21.cloned.1.call-done = bf16[512,2048]{1,0:T(8,128)(2,1)} async-done(((bf16[2048,2048]{1,0:T(8,128)(2,1)}), bf16[512,2048]{1,0:T(8,128)(2,1)}) %reduce-scatter.21.cloned.1.call-update) | async-done | bytes 2097168 | tf_op jit(solution)/shard_map/reduce_scatter | solution.py:55
  957.7 43.0 %reduce-scatter.17.cloned.1.call-done = bf16[512,768]{0,1:T(8,128)(2,1)} async-done(((bf16[2048,768]{0,1:T(8,128)(2,1)}), bf16[512,768]{0,1:T(8,128)(2,1)}) %reduce-scatter.17.cloned.1.call-update) | async-done | bytes 786448 | tf_op jit(solution)/shard_map/reduce_scatter | solution.py:55
  1007.7 64.0 %psum.23 = f32[4,2048]{1,0:T(4,128)} all-reduce(f32[4,2048]{1,0:T(4,128)S(1)} %pad_maximum_fusion.9), channel_id=1, replica_groups=mesh['chip'=4,'core'=2,'ctx'=4] {'chip','core','ctx'}, use_global_device_ids=true, to_apply=%region_25.26 | all-reduce | flops 8192 | bytes 65536 | tf_op jit(solution)/shard_map/psum | solution.py:205
  1108.9 185.7 %reduce-scatter.19.cloned.1.call-done = bf16[64,2048]{1,0:T(8,128)(2,1)} async-done(((bf16[2048,2048]{1,0:T(8,128)(2,1)}), bf16[64,2048]{1,0:T(8,128)(2,1)}) %reduce-scatter.19.cloned.1.call-update) | async-done | bytes 262160 | tf_op jit(solution)/shard_map/reduce_scatter | solution.py:55
  (189 shorter events, 216.3 us)
Async XLA Ops:
  7.2 72.2 %all-gather.11.cloned.1.call-start = ((), (), s32[]{:S(2)}) async-start(), calls=%async_computation.14 | async-start | bytes 3932160 | tf_op jit(solution)/shard_map/all_gather | solution.py:51
  7.2 31.1 %copy-start.21 = (s32[1,128]{1,0:T(1,128)S(1)}, s32[1,128]{1,0:T(1,128)}, u32[]{:S(2)}) copy-start(s32[1,128]{1,0:T(1,128)} %param.10) | copy-start | bytes 1540
  7.2 45.0 %copy-start.20 = (f32[4,2048]{1,0:T(4,128)S(1)}, f32[4,2048]{1,0:T(4,128)}, u32[]{:S(2)}) copy-start(f32[4,2048]{1,0:T(4,128)} %param.16) | copy-start | bytes 98308
  36.8 91.3 %all-gather.25.cloned.1.call-start = ((), (), s32[]{:S(2)}) async-start(), calls=%async_computation.29 | async-start | bytes 4718592 | tf_op jit(solution)/shard_map/all_gather | solution.py:51
  37.5 170.0 %all-gather.13.cloned.1.call-start = ((), (), s32[]{:S(2)}) async-start(), calls=%async_computation.15 | async-start | bytes 8650752 | tf_op jit(solution)/shard_map/all_gather | solution.py:51
  38.3 261.7 %reduce-scatter.9.cloned.1.call-start = ((), (), s32[]{:S(2)}) async-start(), calls=%async_computation.16 | async-start | bytes 4718592 | tf_op jit(solution)/shard_map/reduce_scatter | solution.py:55
  212.2 177.5 %all-gather.17.cloned.1.call-start = ((), (), s32[]{:S(2)}) async-start(), calls=%async_computation.18 | async-start | bytes 10485760 | tf_op jit(solution)/shard_map/all_gather | solution.py:51
  228.8 210.0 %all-gather.15.cloned.1.call-start = ((), (), s32[]{:S(2)}) async-start(), calls=%async_computation.17 | async-start | bytes 4718592 | tf_op jit(solution)/shard_map/all_gather | solution.py:51
  303.5 189.3 %all-gather.19.cloned.1.call-start = ((), (), s32[]{:S(2)}) async-start(), calls=%async_computation.19 | async-start | bytes 5242880 | tf_op jit(solution)/shard_map/all_gather | solution.py:51
  314.9 276.3 %reduce-scatter.11.cloned.1.call-start = ((), (), s32[]{:S(2)}) async-start(), calls=%async_computation.20 | async-start | bytes 4718592 | tf_op jit(solution)/shard_map/reduce_scatter | solution.py:55
  502.1 141.5 %all-gather.21.cloned.1.call-start = ((), (), s32[]{:S(2)}) async-start(), calls=%async_computation.21 | async-start | bytes 4718592 | tf_op jit(solution)/shard_map/all_gather | solution.py:51
  596.5 161.2 %reduce-scatter.13.cloned.1.call-start = ((), (), s32[]{:S(2)}) async-start(), calls=%async_computation.22 | async-start | bytes 4718592 | tf_op jit(solution)/shard_map/reduce_scatter | solution.py:55
  669.8 140.0 %all-gather.23.cloned.1.call-start = ((), (), s32[]{:S(2)}) async-start(), calls=%async_computation.23 | async-start | bytes 4718592 | tf_op jit(solution)/shard_map/all_gather | solution.py:51
  762.8 107.6 %reduce-scatter.23.cloned.1.call-start = ((), (), s32[]{:S(2)}) async-start(), calls=%async_computation.28 | async-start | bytes 5242880 | tf_op jit(solution)/shard_map/reduce_scatter | solution.py:55
  772.4 181.5 %reduce-scatter.21.cloned.1.call-start = ((), (), s32[]{:S(2)}) async-start(), calls=%async_computation.27 | async-start | bytes 10485760 | tf_op jit(solution)/shard_map/reduce_scatter | solution.py:55
  786.5 214.2 %reduce-scatter.17.cloned.1.call-start = ((), (), s32[]{:S(2)}) async-start(), calls=%async_computation.25 | async-start | bytes 3932160 | tf_op jit(solution)/shard_map/reduce_scatter | solution.py:55
  849.5 6.4 copy-start.19
  855.8 250.9 %reduce-scatter.15.cloned.1.call-start = ((), (), s32[]{:S(2)}) async-start(), calls=%async_computation.24 | async-start | bytes 4718592 | tf_op jit(solution)/shard_map/reduce_scatter | solution.py:55
  863.7 4.4 copy-start.6
  863.7 430.9 %reduce-scatter.19.cloned.1.call-start = ((), (), s32[]{:S(2)}) async-start(), calls=%async_computation.26 | async-start | bytes 8650752 | tf_op jit(solution)/shard_map/reduce_scatter | solution.py:55
  953.9 49.1 %all-to-all-start.4 = ((bf16[2,256,2048]{2,1,0:T(8,128)(2,1)}), bf16[2,256,2048]{2,1,0:T(8,128)(2,1)S(1)}, u32[]{:S(2)}, u32[]{:S(2)}) async-start(bf16[2,256,2048]{2,1,0:T(8,128)(2,1)} %bitcast.167), calls=%async_computation.11 | async-start | bytes 4194304 | tf_op jit(solution)/shard_map/all_to_all | solution.py:157
  1003.0 92.6 %all-to-all-start.3 = ((bf16[8,64,768]{2,1,0:T(8,128)(2,1)}), bf16[8,64,768]{2,1,0:T(8,128)(2,1)}, u32[]{:S(2)}, u32[]{:S(2)}) async-start(bf16[8,64,768]{2,1,0:T(8,128)(2,1)} %bitcast.33), calls=%async_computation.8 | async-start | bytes 1572864 | tf_op jit(solution)/shard_map/all_to_all | solution.py:193
  1095.6 11.0 copy-start
  1095.6 11.0 copy-start.8
  (19 other events, 45.8 us)
Sparse Core Ops, SparseCore 0:
  36.9 42.3 all-gather.10
  80.9 47.1 all-gather.24
  131.0 76.4 all-gather.12
  212.3 87.6 reduce-scatter.8
  302.3 87.3 all-gather.16
  391.7 47.1 all-gather.14
  441.3 51.4 all-gather.18
  502.2 88.9 reduce-scatter.10
  596.6 46.8 all-gather.20
  670.0 87.6 reduce-scatter.12
  762.9 46.9 all-gather.22
  812.7 51.4 reduce-scatter.22
  867.5 86.3 reduce-scatter.20
  956.8 43.9 reduce-scatter.16
  1002.9 103.7 reduce-scatter.14
  1108.8 185.7 reduce-scatter.18

commit v2 on v1

--- a/solution.py
+++ b/solution.py
@@ -1,6 +1,8 @@
 import jax
 import jax.numpy as jnp
 from jax import lax
+from jax.experimental import pallas as pl
+from jax.experimental.pallas import tpu as pltpu
 from jax.sharding import Mesh
 from jax.sharding import PartitionSpec as P
 
@@ -13,6 +15,345 @@
 ALL = ("chip", "core", "ctx")
 
 
+PIECE = 32
+LAGB = 1
+LAGJ = 1
+MESH_ID = pl.DeviceIdType.MESH
+
+
+def row_factor(values):
+    return lax.rsqrt(jnp.mean(values * values, axis=-1, keepdims=True) + EPS)
+
+
+def row_norm_back(values, gain, grad):
+    factor = row_factor(values)
+    normed = values * factor
+    scaled = gain * grad
+    back = factor * (scaled - normed * jnp.mean(scaled * normed, axis=-1, keepdims=True))
+    return back, jnp.sum(grad * normed, axis=0, keepdims=True)
+
+
+def after_projected(total, ins, outs, rows):
+    tokens, gains = ins
+    residual_out, projected_out = outs
+    projected_out[rows, :] = total
+    gain = gains[2:3, :]
+    residual = tokens[rows, :].astype(F32) + total * row_factor(total) * gain
+    residual_out[rows, :] = residual
+    return residual
+
+
+def after_feed(total, ins, outs, rows):
+    residual, cotangent, gains = ins
+    output, gain_out = outs
+    gain = gains[3:4, :]
+    normed = total * row_factor(total) * gain
+    output[rows, :] = (residual[rows, :] + normed).astype(BF16)
+    back, term = row_norm_back(total, gain, cotangent[rows, :].astype(F32))
+    gain_out[...] += term
+    return back
+
+
+def after_back(total, ins, outs, rows):
+    projected, cotangent, gains = ins
+    grad_out, gain_out = outs
+    grad = cotangent[rows, :].astype(F32) + total
+    grad_out[rows, :] = grad
+    back, term = row_norm_back(projected[rows, :], gains[2:3, :], grad)
+    gain_out[...] += term
+    return back
+
+
+def after_input(total, ins, outs, rows):
+    (grad,), (result,) = ins, outs
+    result[rows, :] = grad[rows, :] + total
+    return None
+
+
+def pass_tokens(total, ins, outs, rows):
+    return ins[0][rows, :]
+
+
+class Exchange:
+    def __init__(self, spans, rows, width, piece, reduce, spread, row_fn, n_in, n_out, gain):
+        self.spans, self.rows, self.width, self.piece = spans, rows, width, piece
+        self.reduce, self.spread, self.row_fn = reduce, spread, row_fn
+        self.n_in, self.n_out, self.gain = n_in, n_out, gain
+        self.count = rows // piece
+
+    def scratch(self):
+        spans, count = self.spans, self.count
+        block = pltpu.VMEM((spans * self.rows, self.width), BF16)
+        sems = pltpu.SemaphoreType.DMA((spans, count))
+        items = []
+        if self.reduce:
+            items += [block] * 4 + [pltpu.SemaphoreType.DMA] + [sems] * 6
+        if self.spread:
+            items += [pltpu.VMEM((2 * spans * self.rows, self.width), BF16)]
+            items += [sems] * 7 + [pltpu.SemaphoreType.DMA]
+        return items
+
+    def body(self, *refs):
+        spans, rows, piece, count = self.spans, self.rows, self.piece, self.count
+        refs = list(refs)
+        take = lambda n: [refs.pop(0) for _ in range(n)]
+        partial = take(1)[0] if self.reduce else None
+        ins = take(self.n_in)
+        outs = take(self.n_out)
+        gathered = take(1)[0] if self.spread else None
+        if self.reduce:
+            own, near, from_left, from_right = take(4)
+            (load_sem,) = take(1)
+            near_send, near_recv, right_send, right_recv, left_send, left_recv = take(6)
+        if self.spread:
+            (held,) = take(1)
+            fwd_send, fwd_recv, bwd_send, bwd_recv, own_send, side_send, side_recv = take(7)
+            (store_sem,) = take(1)
+        core = lax.axis_index("core")
+        place = lax.axis_index("ctx")
+        other = 1 - core
+        has_left = place > 0
+        has_right = place < spans - 1
+
+        def at(block, k):
+            return pl.ds(pl.multiple_of(block * rows + k * piece, piece), piece)
+
+        def held_at(seq, block, k):
+            return pl.ds(pl.multiple_of((seq * spans + block) * rows + k * piece, piece), piece)
+
+        def remote(src, dst, send, recv, **device):
+            return pltpu.make_async_remote_copy(
+                src_ref=src, dst_ref=dst, send_sem=send, recv_sem=recv,
+                device_id=device, device_id_type=MESH_ID,
+            )
+
+        barrier = pltpu.get_barrier_semaphore()
+        pl.semaphore_signal(barrier, 1, device_id={"core": other}, device_id_type=MESH_ID)
+
+        @pl.when(has_left)
+        def _():
+            pl.semaphore_signal(barrier, 1, device_id={"ctx": place - 1}, device_id_type=MESH_ID)
+
+        @pl.when(has_right)
+        def _():
+            pl.semaphore_signal(barrier, 1, device_id={"ctx": place + 1}, device_id_type=MESH_ID)
+
+        pl.semaphore_wait(barrier, 1 + has_left.astype(jnp.int32) + has_right.astype(jnp.int32))
+
+        if self.gain is not None:
+            outs[self.gain][...] = jnp.zeros_like(outs[self.gain])
+
+        def near_copy(d, k):
+            return remote(
+                partial.at[held_at(other, d, k)], near.at[at(d, k)],
+                near_send.at[d, k], near_recv.at[d, k], core=other,
+            )
+
+        def right_copy(d, k):
+            return remote(
+                own.at[at(d, k)], from_left.at[at(d, k)],
+                right_send.at[d, k], right_recv.at[d, k], ctx=place + 1,
+            )
+
+        def left_copy(d, k):
+            return remote(
+                own.at[at(d, k)], from_right.at[at(d, k)],
+                left_send.at[d, k], left_recv.at[d, k], ctx=place - 1,
+            )
+
+        def fwd_copy(o, k, send):
+            where = held_at(core, o, k)
+            return remote(held.at[where], held.at[where], send, fwd_recv.at[o, k], ctx=place + 1)
+
+        def bwd_copy(o, k, send):
+            where = held_at(core, o, k)
+            return remote(held.at[where], held.at[where], send, bwd_recv.at[o, k], ctx=place - 1)
+
+        def side_copy(o, k):
+            where = held_at(core, o, k)
+            return remote(held.at[where], held.at[where], side_send.at[o, k], side_recv.at[o, k], core=other)
+
+        if self.reduce:
+            load = pltpu.make_async_copy(
+                partial.at[pl.ds(pl.multiple_of(core * spans * rows, rows), spans * rows)], own, load_sem
+            )
+            load.start()
+
+            @pl.loop(0, count)
+            def _(k):
+                for j in range(spans):
+                    near_copy(j, k).start()
+
+            load.wait()
+
+        def base(d, k):
+            near_copy(d, k).wait_recv()
+            return own[at(d, k), :].astype(F32) + near[at(d, k), :].astype(F32)
+
+        def reduce_step(k):
+            for j in range(spans - 1):
+                right, left = spans - 1 - j, j
+
+                @pl.when(jnp.logical_and(right > place, has_left))
+                def _():
+                    value = base(right, k)
+                    right_copy(right, k).wait_recv()
+                    own[at(right, k), :] = (value + from_left[at(right, k), :].astype(F32)).astype(BF16)
+                    right_copy(right, k).start()
+
+                @pl.when(jnp.logical_and(right > place, jnp.logical_not(has_left)))
+                def _():
+                    own[at(right, k), :] = base(right, k).astype(BF16)
+                    right_copy(right, k).start()
+
+                @pl.when(jnp.logical_and(left < place, has_right))
+                def _():
+                    value = base(left, k)
+                    left_copy(left, k).wait_recv()
+                    own[at(left, k), :] = (value + from_right[at(left, k), :].astype(F32)).astype(BF16)
+                    left_copy(left, k).start()
+
+                @pl.when(jnp.logical_and(left < place, jnp.logical_not(has_right)))
+                def _():
+                    own[at(left, k), :] = base(left, k).astype(BF16)
+                    left_copy(left, k).start()
+
+        def finish_step(k):
+            total = None
+            if self.reduce:
+                total = base(place, k)
+
+                @pl.when(has_left)
+                def _():
+                    right_copy(place, k).wait_recv()
+
+                @pl.when(has_right)
+                def _():
+                    left_copy(place, k).wait_recv()
+
+                zero = jnp.zeros_like(total)
+                total = total + jnp.where(has_left, from_left[at(place, k), :].astype(F32), zero)
+                total = total + jnp.where(has_right, from_right[at(place, k), :].astype(F32), zero)
+            own_rows = pl.ds(pl.multiple_of(k * piece, piece), piece)
+            result = self.row_fn(total, ins, outs, own_rows)
+            if self.spread:
+                held[held_at(core, place, k), :] = result.astype(BF16)
+
+                @pl.when(has_right)
+                def _():
+                    fwd_copy(place, k, fwd_send.at[place, k]).start()
+
+                @pl.when(has_left)
+                def _():
+                    bwd_copy(place, k, bwd_send.at[place, k]).start()
+
+                side_copy(place, k).start()
+
+        def relay_step(k, j):
+            if True:
+
+                @pl.when(place - j >= 0)
+                def _():
+                    fwd_copy(place - j, k, fwd_send.at[place - j, k]).wait_recv()
+
+                    @pl.when(has_right)
+                    def _():
+                        fwd_copy(place - j, k, fwd_send.at[place - j, k]).start()
+
+                    side_copy(place - j, k).start()
+
+                @pl.when(place + j < spans)
+                def _():
+                    bwd_copy(place + j, k, bwd_send.at[place + j, k]).wait_recv()
+
+                    @pl.when(has_left)
+                    def _():
+                        bwd_copy(place + j, k, bwd_send.at[place + j, k]).start()
+
+                    side_copy(place + j, k).start()
+
+        lag = LAGB if self.reduce else 0
+
+        @pl.loop(0, count + lag + (LAGJ * (spans - 1) if self.spread else 0))
+        def _(t):
+            if self.reduce:
+
+                @pl.when(t < count)
+                def _():
+                    reduce_step(t)
+
+            @pl.when(jnp.logical_and(t >= lag, t < count + lag))
+            def _():
+                finish_step(t - lag)
+
+            if self.spread:
+                for j in range(1, spans):
+                    after = t - lag - j * LAGJ
+
+                    @pl.when(jnp.logical_and(after >= 0, after < count))
+                    def _():
+                        relay_step(after, j)
+
+        if self.spread:
+
+            @pl.loop(0, count)
+            def _(k):
+                for o in range(spans):
+                    side_copy(o, k).wait_recv()
+
+            store = pltpu.make_async_copy(held, gathered, store_sem)
+            store.start()
+
+        @pl.loop(0, count)
+        def _(k):
+            for d in range(spans):
+                if self.reduce:
+                    near_copy(d, k).wait_send()
+
+                    @pl.when(d > place)
+                    def _():
+                        right_copy(d, k).wait_send()
+
+                    @pl.when(d < place)
+                    def _():
+                        left_copy(d, k).wait_send()
+
+                if self.spread:
+                    side_copy(d, k).wait_send()
+
+                    @pl.when(jnp.logical_and(d <= place, has_right))
+                    def _():
+                        fwd_copy(d, k, fwd_send.at[d, k]).wait_send()
+
+                    @pl.when(jnp.logical_and(d >= place, has_left))
+                    def _():
+                        bwd_copy(d, k, bwd_send.at[d, k]).wait_send()
+
+        if self.spread:
+            store.wait()
+
+    def call(self, name, collective_id, partial, ins, outs):
+        vmem = pl.BlockSpec(memory_space=pltpu.VMEM)
+        hbm = pl.BlockSpec(memory_space=pl.ANY)
+        shapes = list(outs)
+        specs = [vmem] * len(outs)
+        if self.spread:
+            shapes.append(jax.ShapeDtypeStruct((2 * self.spans * self.rows, self.width), BF16))
+            specs.append(hbm)
+        operands = ([partial] if self.reduce else []) + list(ins)
+        return pl.pallas_call(
+            self.body,
+            out_shape=shapes,
+            in_specs=([hbm] if self.reduce else []) + [vmem] * len(ins),
+            out_specs=specs,
+            scratch_shapes=self.scratch(),
+            compiler_params=pltpu.CompilerParams(
+                collective_id=collective_id, has_side_effects=True, vmem_limit_bytes=40 << 20
+            ),
+            name=name,
+        )(*operands)
+
+
 def rope_tables(positions):
     half = HEAD_DIM // 2
     frequency = ROPE_BASE ** (-(jnp.arange(half, dtype=F32) * 2.0 / HEAD_DIM))
@@ -53,17 +394,6 @@
 
 def scatter_sum(values, axes):
     return lax.psum_scatter(values, axes, scatter_dimension=0, tiled=True)
-
-
-def norm_factor(values):
-    return lax.rsqrt(jnp.mean(values * values, axis=-1, keepdims=True) + EPS)
-
-
-def norm_back(values, factor, gain, grad):
-    normed = values * factor
-    scaled = gain * grad
-    back = factor * (scaled - normed * jnp.mean(scaled * normed, axis=-1, keepdims=True))
-    return back, jnp.sum(grad * normed, axis=0)
 
 
 def per_device(inputs, segment, w_qkv, w_out, w_gate, w_up, w_down_t, gains, cotangent):
@@ -83,7 +413,13 @@
     qkv_cut = qkv_cut.reshape(members, qkv_rows, 3 * part)
     qkv_cut = lax.all_to_all(qkv_cut, GROUP, 0, 0, tiled=True)
     qkv_w = gather(qkv_cut.reshape(members * qkv_rows, 3 * part), "chip")
-    tokens_all = gather(tokens, GROUP)
+    spread = lambda reduce, row_fn, n_in, n_out, gain: Exchange(
+        spans, rows, width, PIECE, reduce, True, row_fn, n_in, n_out, gain
+    )
+    own = jax.ShapeDtypeStruct((rows, width), F32)
+    own_low = jax.ShapeDtypeStruct((rows, width), BF16)
+    one = jax.ShapeDtypeStruct((1, width), F32)
+    (tokens_all,) = spread(False, pass_tokens, 1, 0, None).call("gather_tokens", 1, None, [tokens], [])
     out_full = gather(w_out, ALL)
     out_w = lax.dynamic_slice_in_dim(out_full, member * part, part, 0)
 
@@ -128,30 +464,33 @@
     shares_low = shares.astype(BF16)
     attended = jnp.einsum("bhqk,bkhd->bqhd", shares_low, value_low, preferred_element_type=F32)
     attended_low = attended.reshape(total_rows, part).astype(BF16)
-    projected = scatter_sum(dot(attended_low, out_w).astype(BF16), GROUP).astype(F32)
-
-    tokens_wide = tokens.astype(F32)
-    proj_factor = norm_factor(projected)
-    residual = tokens_wide + projected * proj_factor * gains[2]
-    residual_all = gather(residual.astype(BF16), GROUP)
+    residual, projected, residual_all = spread(True, after_projected, 2, 2, None).call(
+        "sum_projected", 2, dot(attended_low, out_w).astype(BF16), [tokens, gains], [own, own]
+    )
 
     gate_up_out = dot(residual_all, gate_up_w)
     gate, up_part = gate_up_out[:, :hidden], gate_up_out[:, hidden:]
     sigmoid = 1.0 / (1.0 + jnp.exp(-gate))
     activated = (gate * sigmoid * up_part).astype(BF16)
-    feed = scatter_sum(dot_rows(activated, down_w).astype(BF16), GROUP).astype(F32)
-    feed_factor = norm_factor(feed)
-    output = (residual + feed * feed_factor * gains[3]).astype(BF16)
-    upstream = cotangent[0].astype(F32)
-    feed_grad, gain_feed = norm_back(feed, feed_factor, gains[3], upstream)
-    feed_grad_all = gather(feed_grad.astype(BF16), GROUP)
+    output, gain_feed, feed_grad_all = spread(True, after_feed, 3, 2, 1).call(
+        "sum_feed",
+        3,
+        dot_rows(activated, down_w).astype(BF16),
+        [residual, cotangent[0], gains],
+        [own_low, one],
+    )
 
     act_grad = dot(feed_grad_all, down_w)
     gate_grad = act_grad * up_part * sigmoid * (1.0 + gate * (1.0 - sigmoid))
     up_grad = act_grad * (gate * sigmoid)
     gate_up_grad = jnp.concatenate([gate_grad.astype(BF16), up_grad.astype(BF16)], 1)
-    back_feed = scatter_sum(dot_rows(gate_up_grad, gate_up_w).astype(BF16), GROUP).astype(F32)
-    residual_grad = upstream + back_feed
+    residual_grad, gain_attn, projected_all = spread(True, after_back, 3, 2, 1).call(
+        "sum_back",
+        4,
+        dot_rows(gate_up_grad, gate_up_w).astype(BF16),
+        [projected, cotangent[0], gains],
+        [own, one],
+    )
 
     grad_gate_up = scatter_sum(dot_first(residual_all, gate_up_grad).astype(BF16), "chip")
     grad_gate_up = lax.all_to_all(grad_gate_up, "core", 0, 1, tiled=True)
@@ -161,8 +500,6 @@
     grad_down = scatter_sum(dot_first(feed_grad_all, activated).astype(BF16), "chip")
     grad_down = lax.all_to_all(grad_down, "core", 0, 1, tiled=True).astype(F32)
 
-    projected_grad, gain_attn = norm_back(projected, proj_factor, gains[2], residual_grad)
-    projected_all = gather(projected_grad.astype(BF16), GROUP)
     attended_grad = dot_rows(projected_all, out_w).astype(BF16).reshape(shape)
 
     share_grad = jnp.einsum("bqhd,bkhd->bhqk", attended_grad, value_low, preferred_element_type=F32)
@@ -186,7 +523,9 @@
         [query_mixed, key_mixed, value_grad.reshape(total_rows, part)], 1
     ).astype(BF16)
     input_part = dot_rows(mixed_grad, qkv_w).astype(BF16)
-    input_grad = residual_grad + scatter_sum(input_part, GROUP).astype(F32)
+    (input_grad,) = Exchange(
+        spans, rows, width, PIECE, True, False, after_input, 1, 1, None
+    ).call("sum_input", 5, input_part, [residual_grad], [own])
 
     grad_qkv = scatter_sum(dot_first(tokens_all, mixed_grad).astype(BF16), "chip")
     grad_qkv = grad_qkv.reshape(members, qkv_rows, 3 * part)
@@ -202,7 +541,7 @@
 
     wide = jnp.zeros((2, width), F32)
     wide = lax.dynamic_update_slice(wide, jnp.stack([gain_query, gain_key]), (0, member * part))
-    grad_gains = lax.psum(jnp.concatenate([wide, gain_attn[None], gain_feed[None]]), ALL)
+    grad_gains = lax.psum(jnp.concatenate([wide, gain_attn, gain_feed]), ALL)
     return (
         output[None],
         input_grad[None],

time: 1310 us -> 929 us (0.71)
  waiting for transfers between devices: 885 us -> 233 us
  Pallas kernels: 0 us -> 329 us
  blocking collectives: 153 us -> 134 us
  other arithmetic: 39.9 us -> 26.1 us
    reduce_scatter x8 -> x4, waiting for transfers between devices: 559 us -> 196 us  [scatter_sum(): return lax.psum_scatter(values, axes, scatter_dimension=0, tiled=True)]
    pallas_call x0 -> x5, Pallas kernels: none -> 329 us  [call(): pl.pallas_call(self.body, out_shape=shapes, in_specs=([hbm] if self.reduc...]
    all_gather x8 -> x4, waiting for transfers between devices: 325 us -> 36.3 us  [gather(): return lax.all_gather(values, axes, axis=0, tiled=True)]
    psum x1, blocking collectives: 64 us -> 39.7 us  [per_device(): grad_gains = lax.psum(jnp.concatenate([wide, gain_attn, gain_feed]), ALL)]
    unnamed x62 -> x80, local copies, waits for them, and re-layouts: 25.5 us -> 28 us
  transfers between devices with their start and end apart: 18 -> 9, of which waited for: 15 -> 4; matrix products, arithmetic and copies ran while one was open for 14% -> 15% of each run, Pallas kernels for 0% -> 19%
where the time goes in v2:
time: 929 us; the launch traced here: 921 us
  Pallas kernels  329 us (35%)
  waiting for transfers between devices  233 us (25%)
  blocking collectives  134 us (14%)
  matrix products  106 us (11%)
  local copies, waits for them, and re-layouts  73.2 us (8%)
  other arithmetic  26.1 us (3%)
  between operations  15.1 us (2%)
    pallas_call x5, Pallas kernels, call(): pl.pallas_call(self.body, out_shape=shapes, in_specs=([hbm] if self.reduc...  329 us
    reduce_scatter x4, waiting for transfers between devices, scatter_sum(): return lax.psum_scatter(values, axes, scatter_dimension=0, tiled=True)  196 us
    psum x1, blocking collectives, per_device(): grad_gains = lax.psum(jnp.concatenate([wide, gain_attn, gain_feed]), ALL)  39.7 us
    all_gather x4, waiting for transfers between devices, gather(): return lax.all_gather(values, axes, axis=0, tiled=True)  36.3 us
    dot_general x4, matrix products, dot_first(): lax.dot_general(left, right, (((0,), (0,)), ((), ())), preferred_element_...  32 us
    dot_general x4, matrix products, dot(): return jnp.dot(left, right, preferred_element_type=F32)  30.8 us
    dot_general x4, matrix products, dot_rows(): lax.dot_general(left, right, (((1,), (1,)), ((), ())), preferred_element_...  28.3 us
    unnamed x80, local copies, waits for them, and re-layouts  28 us
  transfers between devices with their start and end apart: 9, of which 4 were waited for; matrix products, arithmetic and copies ran while one was open for 15% of the time, Pallas kernels for 19%

profile of v2, /device:TPU:0, one launch (start us, length us, event | category | flops | bytes accessed | tf_op | source)
XLA Modules:
  0.0 920.9 jit_solution(4296311332126470048)
XLA Ops:
  10.0 26.9 %all_to_all.74 = bf16[8,64,768]{2,1,0:T(8,128)(2,1)} all-to-all(bf16[8,64,768]{2,1,0:T(8,128)(2,1)S(1)} %reshape.151), channel_id=1, replica_groups=mesh['chip'=4,'core'=2,'ctx'=4] {'core','ctx'}, dimensions={0} | all-to-all | bytes 1572864 | tf_op jit(solution)/shard_map/all_to_all | solution.py:414
  55.5 38.5 %gather_tokens.1 = bf16[1024,2048]{1,0:T(8,128)(2,1)S(1)} custom-call(bf16[128,2048]{1,0:T(8,128)(2,1)S(1)} %bitcast.121), custom_call_target="tpu_custom_call" | custom-call | tf_op jit(solution)/shard_map/gather_tokens/pallas_call | solution.py:344
  96.0 13.8 %all-gather = s32[1,1024]{1,0:T(1,128)S(1)} all-gather(s32[1,128]{1,0:T(1,128)S(1)} %copy-done.31), channel_id=2, replica_groups=mesh['chip'=4,'core'=2,'ctx'=4] {'core','ctx'}, dimensions={1}, use_global_device_ids=true | all-gather | bytes 4608 | tf_op jit(solution)/shard_map/all_gather | solution.py:392
  113.9 8.3 fusion.41
  125.2 16.2 %psum.21 = f32[2,1024]{1,0:T(2,128)S(1)} all-reduce(f32[2,1024]{1,0:T(2,128)S(1)} %pad_maximum_fusion.10), channel_id=1, replica_groups=mesh['chip'=4,'core'=2,'ctx'=4] {'core','ctx'}, use_global_device_ids=true, to_apply=%region_2.0 | all-reduce | flops 2048 | bytes 16384 | tf_op jit(solution)/shard_map/psum | solution.py:439
  169.5 77.2 %sum_projected.1 = (f32[128,2048]{1,0:T(8,128)S(1)}, f32[128,2048]{1,0:T(8,128)S(1)}, bf16[1024,2048]{1,0:T(8,128)(2,1)S(1)}) custom-call(bf16[1024,2048]{1,0:T(8,128)(2,1)S(1)} %convolution_convert_fusion.2.refs_0_, bf16[128,2048]{1,0:T(8,128)(2,1)S(1)} %bitcast.122, f32[4,2048]{1,0:T(4,128)S(1)} %copy-done.8), custom_call_target="tpu_custom_call" | custom-call | tf_op jit(solution)/shard_map/sum_projected/pallas_call | solution.py:344
  248.7 12.5 %fusion.42 = f32[1024,2048]{1,0:T(8,128)S(1)} fusion(bf16[1024,2048]{1,0:T(8,128)(2,1)} %copy-done.9, bf16[2048,2048]{1,0:T(8,128)(2,1)} %all-gather.10.cloned.1.call-done), kind=kOutput, calls=%fused_computation.110 | convolution fusion | flops 8589934592 | bytes 20971520 | tf_op jit(solution)/shard_map/dot_general | solution.py:380
  267.2 36.3 %all-gather.12.cloned.1.call-done = bf16[2048,1024]{1,0:T(8,128)(2,1)} async-done(((bf16[512,1024]{1,0:T(8,128)(2,1)}), bf16[2048,1024]{1,0:T(8,128)(2,1)}) %all-gather.12.cloned.1.call-update) | async-done | bytes 4194320 | tf_op jit(solution)/shard_map/all_gather | solution.py:392
  303.4 7.5 convolution_convert_fusion.5.refs_0_
  311.0 80.4 %sum_feed.1 = (bf16[128,2048]{1,0:T(8,128)(2,1)S(1)}, f32[1,2048]{1,0:T(1,128)S(1)}, bf16[1024,2048]{1,0:T(8,128)(2,1)S(1)}) custom-call(bf16[1024,2048]{1,0:T(8,128)(2,1)S(1)} %convolution_convert_fusion.5.refs_0_, f32[128,2048]{1,0:T(8,128)S(1)} %get-tuple-element.18.refs_1_, bf16[128,2048]{1,0:T(8,128)(2,1)S(1)} %bitcast.123, f32[4,2048]{1,0:T(4,128)S(1)} %copy-done.8), custom_call_target="tpu_custom_call" | custom-call | tf_op jit(solution)/shard_map/sum_feed/pallas_call | solution.py:344
  391.4 7.5 multiply_convert_fusion.2
  398.8 12.6 %convolution_convert_fusion.1.refs_0_ = bf16[1024,2048]{1,0:T(8,128)(2,1)S(1)} fusion(bf16[2048,2048]{1,0:T(8,128)(2,1)} %all-gather.10.cloned.1.call-done, bf16[1024,1024]{1,0:T(8,128)(2,1)} %get-tuple-element.35, bf16[1024,1024]{1,0:T(8,128)(2,1)} %get-tuple-element.34), kind=kOutput, calls=%fused_computation.13 | convolution fusion | flops 8600420352 | bytes 16777216 | tf_op jit(solution)/shard_map/dot_general | solution.py:384
  411.4 76.4 %sum_back.1 = (f32[128,2048]{1,0:T(8,128)S(1)}, f32[1,2048]{1,0:T(1,128)S(1)}, bf16[1024,2048]{1,0:T(8,128)(2,1)S(1)}) custom-call(bf16[1024,2048]{1,0:T(8,128)(2,1)S(1)} %convolution_convert_fusion.1.refs_0_, f32[128,2048]{1,0:T(8,128)S(1)} %get-tuple-element.21.refs_1_, bf16[128,2048]{1,0:T(8,128)(2,1)S(1)} %bitcast.124, f32[4,2048]{1,0:T(4,128)S(1)} %copy-done.8), custom_call_target="tpu_custom_call" | custom-call | tf_op jit(solution)/shard_map/sum_back/pallas_call | solution.py:344
  505.8 14.6 %psum.22 = f32[2,1024]{1,0:T(2,128)S(1)} all-reduce(f32[2,1024]{1,0:T(2,128)S(1)} %pad_maximum_fusion.11), channel_id=1, replica_groups=mesh['chip'=4,'core'=2,'ctx'=4] {'core','ctx'}, use_global_device_ids=true, to_apply=%region_8.9 | all-reduce | flops 2048 | bytes 16384 | tf_op jit(solution)/shard_map/psum | solution.py:517
  531.7 9.4 %convolution_convert_fusion.4 = bf16[2048,1024]{1,0:T(8,128)(2,1)} fusion(bf16[1024,2048]{1,0:T(8,128)(2,1)} %copy-done.10, bf16[1024,1024]{1,0:T(8,128)(2,1)} %multiply_convert_fusion.3), kind=kOutput, calls=%fused_computation.16 | convolution fusion | flops 4297064448 | bytes 10485760 | tf_op jit(solution)/shard_map/dot_general | solution.py:388
  541.2 14.1 %convolution_convert_fusion = bf16[2048,2048]{1,0:T(8,128)(2,1)} fusion(bf16[1024,2048]{1,0:T(8,128)(2,1)} %copy-done.9, bf16[1024,1024]{1,0:T(8,128)(2,1)} %get-tuple-element.35, bf16[1024,1024]{1,0:T(8,128)(2,1)} %get-tuple-element.34), kind=kOutput, calls=%fused_computation.1 | convolution fusion | flops 8602517504 | bytes 16777216 | tf_op jit(solution)/shard_map/dot_general | solution.py:388
  562.5 13.0 %reduce-scatter.5.cloned.1.call-done = bf16[512,768]{0,1:T(8,128)(2,1)} async-done(((bf16[2048,768]{0,1:T(8,128)(2,1)}), bf16[512,768]{0,1:T(8,128)(2,1)}) %reduce-scatter.5.cloned.1.call-update) | async-done | bytes 786448 | tf_op jit(solution)/shard_map/reduce_scatter | solution.py:396
  588.0 56.2 %sum_input.1 = f32[128,2048]{1,0:T(8,128)S(1)} custom-call(bf16[1024,2048]{1,0:T(8,128)(2,1)S(1)} %convolution_convert_fusion.3.refs_0_, f32[128,2048]{1,0:T(8,128)S(1)} %get-tuple-element.23.refs_1_), custom_call_target="tpu_custom_call" | custom-call | tf_op jit(solution)/shard_map/sum_input/pallas_call | solution.py:344
  644.3 39.7 %psum.23 = f32[4,2048]{1,0:T(4,128)} all-reduce(f32[4,2048]{1,0:T(4,128)S(1)} %pad_maximum_fusion.9), channel_id=1, replica_groups=mesh['chip'=4,'core'=2,'ctx'=4] {'chip','core','ctx'}, use_global_device_ids=true, to_apply=%region_15.16 | all-reduce | flops 8192 | bytes 65536 | tf_op jit(solution)/shard_map/psum | solution.py:544
  696.5 25.7 %reduce-scatter.9.cloned.1.call-done = bf16[512,2048]{1,0:T(8,128)(2,1)} async-done(((bf16[2048,2048]{1,0:T(8,128)(2,1)}), bf16[512,2048]{1,0:T(8,128)(2,1)}) %reduce-scatter.9.cloned.1.call-update) | async-done | bytes 2097168 | tf_op jit(solution)/shard_map/reduce_scatter | solution.py:396
  722.2 6.8 all_to_all.78
  731.4 6.7 reshape.164
  738.1 7.3 fusion.34
  753.1 157.3 %reduce-scatter.7.cloned.1.call-done = bf16[64,2048]{1,0:T(8,128)(2,1)} async-done(((bf16[2048,2048]{1,0:T(8,128)(2,1)}), bf16[64,2048]{1,0:T(8,128)(2,1)}) %reduce-scatter.7.cloned.1.call-update) | async-done | bytes 262160 | tf_op jit(solution)/shard_map/reduce_scatter | solution.py:396
  (175 shorter events, 141.1 us)
Async XLA Ops:
  7.2 30.5 %copy-start.22 = (bf16[256,2048]{1,0:T(8,128)(2,1)S(1)}, bf16[256,2048]{1,0:T(8,128)(2,1)}, u32[]{:S(2)}) copy-start(bf16[256,2048]{1,0:T(8,128)(2,1)} %param.13) | copy-start | bytes 3145732
  7.2 106.7 %all-gather.6.cloned.1.call-start = ((), (), s32[]{:S(2)}) async-start(), calls=%async_computation.10 | async-start | bytes 3932160 | tf_op jit(solution)/shard_map/all_gather | solution.py:392
  36.8 129.2 %all-gather.8.cloned.1.call-start = ((), (), s32[]{:S(2)}) async-start(), calls=%async_computation.11 | async-start | bytes 8650752 | tf_op jit(solution)/shard_map/all_gather | solution.py:392
  37.6 211.1 %all-gather.10.cloned.1.call-start = ((), (), s32[]{:S(2)}) async-start(), calls=%async_computation.12 | async-start | bytes 10485760 | tf_op jit(solution)/shard_map/all_gather | solution.py:392
  47.7 7.8 copy-start.8
  47.7 7.8 copy-start.4
  47.7 255.7 %all-gather.12.cloned.1.call-start = ((), (), s32[]{:S(2)}) async-start(), calls=%async_computation.13 | async-start | bytes 5242880 | tf_op jit(solution)/shard_map/all_gather | solution.py:392
  53.9 42.1 %copy-start.31 = (s32[1,128]{1,0:T(1,128)S(1)}, s32[1,128]{1,0:T(1,128)}, u32[]{:S(2)}) copy-start(s32[1,128]{1,0:T(1,128)} %param.10) | copy-start | bytes 1540
  55.2 520.3 %reduce-scatter.5.cloned.1.call-start = ((), (), s32[]{:S(2)}) async-start(), calls=%async_computation.14 | async-start | bytes 3932160 | tf_op jit(solution)/shard_map/reduce_scatter | solution.py:396
  156.9 5.9 copy-start.16
  156.9 5.9 copy-start.27
  267.2 43.8 %copy-start.5 = (bf16[1,128,2048]{2,1,0:T(8,128)(2,1)S(1)}, bf16[1,128,2048]{2,1,0:T(8,128)(2,1)}, u32[]{:S(2)}) copy-start(bf16[1,128,2048]{2,1,0:T(8,128)(2,1)} %param.17) | copy-start | bytes 1572868
  303.4 87.9 %copy-start.14 = (f32[1024,2048]{1,0:T(8,128)S(1)}, f32[1024,2048]{1,0:T(8,128)}, u32[]{:S(2)}) copy-start(f32[1024,2048]{1,0:T(8,128)} %copy-done.13) | copy-start | bytes 25165828
  310.9 80.4 %copy-start.32 = (bf16[2048,1024]{1,0:T(8,128)(2,1)S(1)}, bf16[2048,1024]{1,0:T(8,128)(2,1)}, u32[]{:S(2)}) copy-start(bf16[2048,1024]{1,0:T(8,128)(2,1)} %all-gather.12.cloned.1.call-done) | copy-start | bytes 12582916
  391.3 7.5 copy-start.6
  391.3 7.5 copy-start.10
  531.7 157.4 %reduce-scatter.11.cloned.1.call-start = ((), (), s32[]{:S(2)}) async-start(), calls=%async_computation.17 | async-start | bytes 5242880 | tf_op jit(solution)/shard_map/reduce_scatter | solution.py:396
  541.1 181.1 %reduce-scatter.9.cloned.1.call-start = ((), (), s32[]{:S(2)}) async-start(), calls=%async_computation.16 | async-start | bytes 10485760 | tf_op jit(solution)/shard_map/reduce_scatter | solution.py:396
  555.3 355.0 %reduce-scatter.7.cloned.1.call-start = ((), (), s32[]{:S(2)}) async-start(), calls=%async_computation.15 | async-start | bytes 8650752 | tf_op jit(solution)/shard_map/reduce_scatter | solution.py:396
  562.4 19.9 %copy-start.24 = (bf16[1024,256]{0,1:T(8,128)(2,1)S(1)}, bf16[1024,256]{0,1:T(8,128)(2,1)}, u32[]{:S(2)}) copy-start(bf16[1024,256]{0,1:T(8,128)(2,1)} %copy-done.23) | copy-start | bytes 1572868
  562.4 19.9 %copy-start.26 = (bf16[1024,256]{0,1:T(8,128)(2,1)S(1)}, bf16[1024,256]{0,1:T(8,128)(2,1)}, u32[]{:S(2)}) copy-start(bf16[1024,256]{0,1:T(8,128)(2,1)} %copy-done.25) | copy-start | bytes 1572868
  562.4 19.9 %copy-start.30 = (bf16[32,8,2,512]{3,1,2,0:T(8,128)(2,1)S(1)}, bf16[32,8,2,512]{3,1,2,0:T(8,128)(2,1)}, u32[]{:S(2)}) copy-start(bf16[32,8,2,512]{3,1,2,0:T(8,128)(2,1)} %copy-done.29) | copy-start | bytes 1572868
  577.8 106.3 %all-to-all-start.3 = ((bf16[8,64,768]{2,1,0:T(8,128)(2,1)}), bf16[8,64,768]{2,1,0:T(8,128)(2,1)}, u32[]{:S(2)}, u32[]{:S(2)}) async-start(bf16[8,64,768]{2,1,0:T(8,128)(2,1)} %bitcast.29), calls=%async_computation.4 | async-start | bytes 1572864 | tf_op jit(solution)/shard_map/all_to_all | solution.py:532
  749.2 162.9 %copy-start.7 = (bf16[128,2048]{1,0:T(8,128)(2,1)S(1)}, bf16[128,2048]{1,0:T(8,128)(2,1)}, u32[]{:S(2)}) copy-start(bf16[128,2048]{1,0:T(8,128)(2,1)} %copy-done.6) | copy-start | bytes 1572868
  (18 other events, 44.4 us)
Sparse Core Ops, SparseCore 0:
  37.0 42.3 all-gather.5
  82.3 77.3 all-gather.7
  162.2 86.1 all-gather.9
  250.7 52.6 all-gather.11
  531.8 43.6 reduce-scatter.4
  578.3 52.6 reduce-scatter.10
  634.4 87.7 reduce-scatter.8
  724.5 185.8 reduce-scatter.6

commit v3 on v2

--- a/solution.py
+++ b/solution.py
@@ -75,7 +75,8 @@
 
 
 class Exchange:
-    def __init__(self, spans, rows, width, piece, reduce, spread, row_fn, n_in, n_out, gain):
+    def __init__(self, spans, rows, width, piece, reduce, spread, row_fn, n_in, n_out, gain, extra=None):
+        self.extra = extra
         self.spans, self.rows, self.width, self.piece = spans, rows, width, piece
         self.reduce, self.spread, self.row_fn = reduce, spread, row_fn
         self.n_in, self.n_out, self.gain = n_in, n_out, gain
@@ -91,6 +92,8 @@
         if self.spread:
             items += [pltpu.VMEM((2 * spans * self.rows, self.width), BF16)]
             items += [sems] * 7 + [pltpu.SemaphoreType.DMA]
+        if self.extra is not None:
+            items += self.extra.scratch()
         return items
 
     def body(self, *refs):
@@ -99,7 +102,12 @@
         take = lambda n: [refs.pop(0) for _ in range(n)]
         partial = take(1)[0] if self.reduce else None
         ins = take(self.n_in)
+        extra = self.extra
+        if extra is not None:
+            extra.ins = take(extra.n_in)
         outs = take(self.n_out)
+        if extra is not None:
+            extra.outs = take(extra.n_out)
         gathered = take(1)[0] if self.spread else None
         if self.reduce:
             own, near, from_left, from_right = take(4)
@@ -109,6 +117,8 @@
             (held,) = take(1)
             fwd_send, fwd_recv, bwd_send, bwd_recv, own_send, side_send, side_recv = take(7)
             (store_sem,) = take(1)
+        if extra is not None:
+            extra.held = refs
         core = lax.axis_index("core")
         place = lax.axis_index("ctx")
         other = 1 - core
@@ -128,17 +138,20 @@
             )
 
         barrier = pltpu.get_barrier_semaphore()
-        pl.semaphore_signal(barrier, 1, device_id={"core": other}, device_id_type=MESH_ID)
-
-        @pl.when(has_left)
-        def _():
-            pl.semaphore_signal(barrier, 1, device_id={"ctx": place - 1}, device_id_type=MESH_ID)
-
-        @pl.when(has_right)
-        def _():
-            pl.semaphore_signal(barrier, 1, device_id={"ctx": place + 1}, device_id_type=MESH_ID)
-
-        pl.semaphore_wait(barrier, 1 + has_left.astype(jnp.int32) + has_right.astype(jnp.int32))
+        if extra is not None:
+            meet_all(spans)
+        else:
+            pl.semaphore_signal(barrier, 1, device_id={"core": other}, device_id_type=MESH_ID)
+
+            @pl.when(has_left)
+            def _():
+                pl.semaphore_signal(barrier, 1, device_id={"ctx": place - 1}, device_id_type=MESH_ID)
+
+            @pl.when(has_right)
+            def _():
+                pl.semaphore_signal(barrier, 1, device_id={"ctx": place + 1}, device_id_type=MESH_ID)
+
+            pl.semaphore_wait(barrier, 1 + has_left.astype(jnp.int32) + has_right.astype(jnp.int32))
 
         if self.gain is not None:
             outs[self.gain][...] = jnp.zeros_like(outs[self.gain])
@@ -173,6 +186,8 @@
             where = held_at(core, o, k)
             return remote(held.at[where], held.at[where], side_send.at[o, k], side_recv.at[o, k], core=other)
 
+        if extra is not None:
+            extra.start()
         if self.reduce:
             load = pltpu.make_async_copy(
                 partial.at[pl.ds(pl.multiple_of(core * spans * rows, rows), spans * rows)], own, load_sem
@@ -282,9 +297,17 @@
                 def _():
                     reduce_step(t)
 
-            @pl.when(jnp.logical_and(t >= lag, t < count + lag))
-            def _():
-                finish_step(t - lag)
+            if self.reduce:
+
+                @pl.when(jnp.logical_and(t >= lag, t < count + lag))
+                def _():
+                    finish_step(t - lag)
+            else:
+
+                @pl.when(t == 0)
+                def _():
+                    for k in range(count):
+                        finish_step(k)
 
             if self.spread:
                 for j in range(1, spans):
@@ -293,7 +316,11 @@
                     @pl.when(jnp.logical_and(after >= 0, after < count))
                     def _():
                         relay_step(after, j)
-
+            if extra is not None:
+                extra.tick(t)
+
+        if extra is not None:
+            extra.finish(count + lag + (LAGJ * (spans - 1) if self.spread else 0))
         if self.spread:
 
             @pl.loop(0, count)
@@ -335,23 +362,301 @@
     def call(self, name, collective_id, partial, ins, outs):
         vmem = pl.BlockSpec(memory_space=pltpu.VMEM)
         hbm = pl.BlockSpec(memory_space=pl.ANY)
+        operands = ([partial] if self.reduce else []) + list(ins)
+        in_specs = ([hbm] if self.reduce else []) + [vmem] * len(ins)
         shapes = list(outs)
         specs = [vmem] * len(outs)
+        if self.extra is not None:
+            operands += self.extra.operands
+            in_specs += self.extra.in_specs
+            shapes += self.extra.out_shapes
+            specs += self.extra.out_specs
         if self.spread:
             shapes.append(jax.ShapeDtypeStruct((2 * self.spans * self.rows, self.width), BF16))
             specs.append(hbm)
-        operands = ([partial] if self.reduce else []) + list(ins)
         return pl.pallas_call(
             self.body,
             out_shape=shapes,
-            in_specs=([hbm] if self.reduce else []) + [vmem] * len(ins),
+            in_specs=in_specs,
             out_specs=specs,
             scratch_shapes=self.scratch(),
             compiler_params=pltpu.CompilerParams(
-                collective_id=collective_id, has_side_effects=True, vmem_limit_bytes=40 << 20
+                collective_id=collective_id, has_side_effects=True, vmem_limit_bytes=48 << 20
+            ),
+            cost_estimate=pl.CostEstimate(
+                flops=0,
+                bytes_accessed=(50 if self.reduce else 30) * self.width * self.width,
+                transcendentals=0,
             ),
             name=name,
         )(*operands)
+
+
+def meet_all(spans):
+    chips = lax.axis_size("chip")
+    barrier = pltpu.get_barrier_semaphore()
+    chip = lax.axis_index("chip")
+    core = lax.axis_index("core")
+    place = lax.axis_index("ctx")
+    for s in range(1, chips):
+        pl.semaphore_signal(
+            barrier, 1, device_id={"chip": lax.rem(chip + s, chips)}, device_id_type=MESH_ID
+        )
+    for s in range(1, 2 * spans):
+        to_core, to_place = step_member(core, place, s, spans)
+        pl.semaphore_signal(
+            barrier, 1, device_id={"core": to_core, "ctx": to_place}, device_id_type=MESH_ID
+        )
+    pl.semaphore_wait(barrier, chips - 1 + 2 * spans - 1)
+
+
+def step_member(core, place, s, spans):
+    return lax.rem(core + s % 2, 2), lax.rem(place + s // 2, spans)
+
+
+class Extra:
+    def remote(self, src, dst, send, recv, **device):
+        return pltpu.make_async_remote_copy(
+            src_ref=src, dst_ref=dst, send_sem=send, recv_sem=recv,
+            device_id=device, device_id_type=MESH_ID,
+        )
+
+    def locate(self):
+        self.chip = lax.axis_index("chip")
+        self.core = lax.axis_index("core")
+        self.place = lax.axis_index("ctx")
+        self.me = self.core * self.spans + self.place
+
+
+class QkvWeights(Extra):
+    n_in, n_out = 2, 2
+
+    def __init__(self, spans, chips, cut, ids):
+        self.spans, self.chips = spans, chips
+        self.members, self.block, self.columns = cut.shape
+        self.operands = [cut, ids]
+        self.ids_shape = ids.shape
+        vmem = pl.BlockSpec(memory_space=pltpu.VMEM)
+        self.in_specs = [vmem, vmem]
+        self.out_shapes = [
+            jax.ShapeDtypeStruct((chips * self.members * self.block, self.columns), BF16),
+            jax.ShapeDtypeStruct((self.members * ids.shape[0], ids.shape[1]), jnp.int32),
+        ]
+        self.out_specs = [vmem, vmem]
+
+    def scratch(self):
+        rows = self.chips * self.members * self.block
+        sems = pltpu.SemaphoreType.DMA((self.members,))
+        cross = pltpu.SemaphoreType.DMA((self.chips, self.members))
+        ids = (self.members * self.ids_shape[0], self.ids_shape[1])
+        return [pltpu.VMEM((rows, self.columns), BF16), pltpu.VMEM(ids, jnp.int32)] + [sems] * 4 + [cross] * 2
+
+    def at(self, chip, m):
+        return pl.ds(pl.multiple_of((chip * self.members + m) * self.block, self.block), self.block)
+
+    def ids_at(self, m):
+        return pl.ds(pl.multiple_of(m * self.ids_shape[0], self.ids_shape[0]), self.ids_shape[0])
+
+    def block_copy(self, s):
+        full, _, send, recv = self.held[:4]
+        core, place = step_member(self.core, self.place, s, self.spans)
+        return self.remote(
+            self.ins[0].at[core * self.spans + place], full.at[self.at(self.chip, self.me)],
+            send.at[s], recv.at[s], core=core, ctx=place,
+        )
+
+    def ids_copy(self, s):
+        all_ids, send, recv = self.held[1], self.held[4], self.held[5]
+        core, place = step_member(self.core, self.place, s, self.spans)
+        return self.remote(
+            self.ins[1], all_ids.at[self.ids_at(self.me)], send.at[s], recv.at[s], core=core, ctx=place
+        )
+
+    def source(self, s):
+        core = lax.rem(self.core + s % 2, 2)
+        return core * self.spans + lax.rem(self.place + self.spans - s // 2, self.spans)
+
+    def chip_copy(self, s, m):
+        full, _, _, _, _, _, send, recv = self.held
+        where = self.at(self.chip, m)
+        return self.remote(
+            full.at[where], full.at[where], send.at[s, m], recv.at[s, m], chip=lax.rem(self.chip + s, self.chips)
+        )
+
+    def start(self):
+        self.locate()
+        cut, ids = self.ins
+        full, all_ids = self.held[:2]
+        for s in range(1, self.members):
+            self.block_copy(s).start()
+        for s in range(1, self.members):
+            self.ids_copy(s).start()
+        full[self.at(self.chip, self.me), :] = cut[self.me]
+        all_ids[self.ids_at(self.me), :] = ids[...]
+
+    def send_block(self, s):
+        m = self.me if s == 0 else self.source(s)
+        if s > 0:
+            self.block_copy(s).wait_recv()
+        for step in range(1, self.chips):
+            self.chip_copy(step, m).start()
+
+    def tick(self, t):
+        @pl.when(t == 0)
+        def _():
+            for s in range(self.members):
+                self.send_block(s)
+
+    def finish(self, ticks):
+        full, all_ids = self.held[:2]
+        for s in range(1, self.members):
+            self.ids_copy(s).wait_recv()
+            self.block_copy(s).wait_send()
+            self.ids_copy(s).wait_send()
+
+        @pl.loop(0, self.members)
+        def _(m):
+            for s in range(1, self.chips):
+                self.chip_copy(s, m).wait()
+
+        self.outs[0][...] = full[...]
+        self.outs[1][...] = all_ids[...]
+
+
+class QkvGrads(Extra):
+    n_in, n_out = 2, 2
+
+    def __init__(self, spans, chips, members, grads, sums):
+        self.spans, self.chips, self.members = spans, chips, members
+        self.block, self.columns = grads.shape[0] // (chips * members), grads.shape[1]
+        self.part = self.columns // 3
+        self.width = self.part * members
+        self.own_rows = self.part // 128
+        self.sum_rows = sums.shape[0]
+        self.operands = [grads, sums]
+        vmem = pl.BlockSpec(memory_space=pltpu.VMEM)
+        self.in_specs = [vmem, vmem]
+        self.out_shapes = [
+            jax.ShapeDtypeStruct((self.block, 3 * self.width), F32),
+            jax.ShapeDtypeStruct((4, self.width // 128, 128), F32),
+        ]
+        self.out_specs = [vmem, vmem]
+
+    def scratch(self):
+        sems = pltpu.SemaphoreType.DMA((self.members,))
+        chip_sems = pltpu.SemaphoreType.DMA((self.chips,))
+        cross = pltpu.SemaphoreType.DMA((self.chips, self.members))
+        return [
+            pltpu.VMEM((self.chips, self.members, self.block, self.columns), BF16),
+            pltpu.VMEM((self.members, self.block, self.columns), BF16),
+            pltpu.VMEM((self.members, self.block, self.columns), BF16),
+            pltpu.VMEM((self.chips, self.sum_rows, 128), F32),
+            pltpu.VMEM((self.sum_rows, 128), F32),
+            pltpu.VMEM((self.members, self.sum_rows, 128), F32),
+        ] + [cross] * 2 + [sems] * 2 + [chip_sems] * 2 + [sems] * 2
+
+    def at(self, chip, m):
+        return pl.ds(pl.multiple_of((chip * self.members + m) * self.block, self.block), self.block)
+
+    def chip_copy(self, s, m):
+        other = lax.rem(self.chip + s, self.chips)
+        return self.remote(
+            self.ins[0].at[self.at(other, m)], self.arrived.at[s, m],
+            self.cross_send.at[s, m], self.cross_recv.at[s, m], chip=other,
+        )
+
+    def member_copy(self, s):
+        core, place = step_member(self.core, self.place, s, self.spans)
+        return self.remote(
+            self.summed.at[core * self.spans + place], self.columns_in.at[self.me],
+            self.member_send.at[s], self.member_recv.at[s], core=core, ctx=place,
+        )
+
+    def sums_chip(self, s):
+        return self.remote(
+            self.ins[1], self.sums_in.at[s], self.sums_send.at[s], self.sums_recv.at[s],
+            chip=lax.rem(self.chip + s, self.chips),
+        )
+
+    def sums_member(self, s):
+        core, place = step_member(self.core, self.place, s, self.spans)
+        return self.remote(
+            self.sums_chips, self.sums_members.at[self.me], self.last_send.at[s], self.last_recv.at[s],
+            core=core, ctx=place,
+        )
+
+    def start(self):
+        self.locate()
+        (
+            self.arrived, self.summed, self.columns_in, self.sums_in, self.sums_chips, self.sums_members,
+            self.cross_send, self.cross_recv, self.member_send, self.member_recv,
+            self.sums_send, self.sums_recv, self.last_send, self.last_recv,
+        ) = self.held
+        for s in range(1, self.chips):
+            self.sums_chip(s).start()
+
+        @pl.loop(0, self.members)
+        def _(i):
+            m = lax.rem(self.me + 1 + i, self.members)
+            for s in range(1, self.chips):
+                self.chip_copy(s, m).start()
+
+    def add_block(self, m):
+        total = self.ins[0][self.at(self.chip, m), :].astype(F32)
+        for s in range(1, self.chips):
+            self.chip_copy(s, m).wait_recv()
+            total = total + self.arrived[s, m].astype(F32)
+        self.summed[m] = total.astype(BF16)
+
+    def send_blocks(self, first, last):
+        for s in range(first, last):
+            core, place = step_member(self.core, self.place, s, self.spans)
+            self.add_block(core * self.spans + place)
+            self.member_copy(s).start()
+
+    def tick(self, t):
+        @pl.when(t == 1)
+        def _():
+            total = self.ins[1][...]
+            for s in range(1, self.chips):
+                self.sums_chip(s).wait_recv()
+                total = total + self.sums_in[s]
+            self.sums_chips[...] = total
+            self.sums_members[self.me] = total
+            for s in range(1, self.members):
+                self.sums_member(s).start()
+
+    def finish(self, ticks):
+        self.send_blocks(1, self.members)
+        self.add_block(self.me)
+        self.columns_in[self.me] = self.summed[self.me]
+        for s in range(1, self.members):
+            self.sums_member(s).wait()
+        wide = self.width // 128
+        for i in range(2):
+            total = self.sums_members[0, i * wide : (i + 1) * wide, :]
+            for m in range(1, self.members):
+                total = total + self.sums_members[m, i * wide : (i + 1) * wide, :]
+            self.outs[1][2 + i] = total
+            base = 2 * wide + i * self.own_rows
+            for m in range(self.members):
+                self.outs[1][i, m * self.own_rows : (m + 1) * self.own_rows, :] = self.sums_members[
+                    m, base : base + self.own_rows, :
+                ]
+        for s in range(1, self.members):
+            self.member_copy(s).wait()
+        for m in range(self.members):
+            for i in range(3):
+                self.outs[0][:, i * self.width + m * self.part : i * self.width + (m + 1) * self.part] = (
+                    self.columns_in[m, :, i * self.part : (i + 1) * self.part].astype(F32)
+                )
+        for s in range(1, self.chips):
+            self.sums_chip(s).wait_send()
+
+        @pl.loop(0, self.members)
+        def _(m):
+            for s in range(1, self.chips):
+                self.chip_copy(s, m).wait_send()
 
 
 def rope_tables(positions):
@@ -411,17 +716,22 @@
     qkv_rows = w_qkv.shape[0]
     qkv_cut = w_qkv.reshape(qkv_rows, 3, members, part).transpose(2, 0, 1, 3)
     qkv_cut = qkv_cut.reshape(members, qkv_rows, 3 * part)
-    qkv_cut = lax.all_to_all(qkv_cut, GROUP, 0, 0, tiled=True)
-    qkv_w = gather(qkv_cut.reshape(members * qkv_rows, 3 * part), "chip")
+    chips = lax.axis_size("chip")
+    assert chips == spans
     spread = lambda reduce, row_fn, n_in, n_out, gain: Exchange(
         spans, rows, width, PIECE, reduce, True, row_fn, n_in, n_out, gain
     )
     own = jax.ShapeDtypeStruct((rows, width), F32)
     own_low = jax.ShapeDtypeStruct((rows, width), BF16)
     one = jax.ShapeDtypeStruct((1, width), F32)
-    (tokens_all,) = spread(False, pass_tokens, 1, 0, None).call("gather_tokens", 1, None, [tokens], [])
-    out_full = gather(w_out, ALL)
-    out_w = lax.dynamic_slice_in_dim(out_full, member * part, part, 0)
+    qkv_w, ids, tokens_all = Exchange(
+        spans, rows, width, PIECE, False, True, pass_tokens, 1, 0, None,
+        QkvWeights(spans, chips, qkv_cut, jnp.broadcast_to(segment, (8, rows))),
+    ).call("gather_tokens", 1, None, [tokens], [])
+    swaps = [
+        (m * spans + a, a * members + m) for m in range(members) for a in range(chips)
+    ]
+    out_w = gather(lax.ppermute(w_out, ALL, swaps), "chip")
 
     hidden = w_gate.shape[1] // cores
     gate_up = jnp.concatenate(
@@ -449,7 +759,7 @@
     key_low = rotate((key_raw * key_factor * gain_k).reshape(shape), cosine, sine).astype(BF16)
     value_low = value_low.reshape(shape)
 
-    ids = gather(segment[0], GROUP).reshape(cores, length)
+    ids = ids.reshape(members, 8, rows)[:, 0].reshape(cores, length)
     allowed = (
         (ids[:, :, None] == ids[:, None, :])
         & (places[None, None, :] <= places[None, :, None])
@@ -484,21 +794,25 @@
     gate_grad = act_grad * up_part * sigmoid * (1.0 + gate * (1.0 - sigmoid))
     up_grad = act_grad * (gate * sigmoid)
     gate_up_grad = jnp.concatenate([gate_grad.astype(BF16), up_grad.astype(BF16)], 1)
-    residual_grad, gain_attn, projected_all = spread(True, after_back, 3, 2, 1).call(
-        "sum_back",
-        4,
-        dot_rows(gate_up_grad, gate_up_w).astype(BF16),
-        [projected, cotangent[0], gains],
-        [own, one],
-    )
-
-    grad_gate_up = scatter_sum(dot_first(residual_all, gate_up_grad).astype(BF16), "chip")
+    back_part = dot_rows(gate_up_grad, gate_up_w).astype(BF16)
+    down_part = dot_first(feed_grad_all, activated).astype(BF16)
+    gate_up_part = dot_first(residual_all, gate_up_grad).astype(BF16)
+    back_part, down_part, gate_up_part = lax.optimization_barrier((back_part, down_part, gate_up_part))
+    grad_gate_up = scatter_sum(gate_up_part, "chip")
     grad_gate_up = lax.all_to_all(grad_gate_up, "core", 0, 1, tiled=True)
     grad_gate_up = grad_gate_up.reshape(-1, cores, 2, hidden).astype(F32)
     grad_gate = grad_gate_up[:, :, 0].reshape(-1, cores * hidden)
     grad_up = grad_gate_up[:, :, 1].reshape(-1, cores * hidden)
-    grad_down = scatter_sum(dot_first(feed_grad_all, activated).astype(BF16), "chip")
+    grad_down = scatter_sum(down_part, "chip")
     grad_down = lax.all_to_all(grad_down, "core", 0, 1, tiled=True).astype(F32)
+
+    residual_grad, gain_attn, projected_all = spread(True, after_back, 3, 2, 1).call(
+        "sum_back",
+        4,
+        back_part,
+        [projected, cotangent[0], gains],
+        [own, one],
+    )
 
     attended_grad = dot_rows(projected_all, out_w).astype(BF16).reshape(shape)
 
@@ -523,25 +837,18 @@
         [query_mixed, key_mixed, value_grad.reshape(total_rows, part)], 1
     ).astype(BF16)
     input_part = dot_rows(mixed_grad, qkv_w).astype(BF16)
-    (input_grad,) = Exchange(
-        spans, rows, width, PIECE, True, False, after_input, 1, 1, None
+    sums = jnp.concatenate(
+        [a.reshape(-1, 128) for a in (gain_attn, gain_feed, gain_query, gain_key)]
+        + [jnp.zeros((-2 * part // 128 % 8, 128), F32)]
+    )
+    input_grad, grad_qkv, grad_gains = Exchange(
+        spans, rows, width, PIECE, True, False, after_input, 1, 1, None,
+        QkvGrads(spans, chips, members, dot_first(tokens_all, mixed_grad).astype(BF16), sums),
     ).call("sum_input", 5, input_part, [residual_grad], [own])
 
-    grad_qkv = scatter_sum(dot_first(tokens_all, mixed_grad).astype(BF16), "chip")
-    grad_qkv = grad_qkv.reshape(members, qkv_rows, 3 * part)
-    grad_qkv = lax.all_to_all(grad_qkv, GROUP, 0, 0, tiled=True)
-    grad_qkv = grad_qkv.reshape(members, qkv_rows, 3, part).transpose(1, 2, 0, 3)
-    grad_qkv = grad_qkv.reshape(qkv_rows, 3 * width).astype(F32)
-
-    out_part = dot_first(attended_low, projected_all).astype(BF16)
-    out_part = lax.dynamic_update_slice_in_dim(
-        jnp.zeros((width, width), BF16), out_part, member * part, 0
-    )
-    grad_out = scatter_sum(out_part, ALL).astype(F32)
-
-    wide = jnp.zeros((2, width), F32)
-    wide = lax.dynamic_update_slice(wide, jnp.stack([gain_query, gain_key]), (0, member * part))
-    grad_gains = lax.psum(jnp.concatenate([wide, gain_attn, gain_feed]), ALL)
+    out_part = scatter_sum(dot_first(attended_low, projected_all).astype(BF16), "chip")
+    grad_out = lax.ppermute(out_part, ALL, [(b, a) for a, b in swaps]).astype(F32)
+
     return (
         output[None],
         input_grad[None],
@@ -550,7 +857,7 @@
         grad_gate,
         grad_up,
         grad_down,
-        grad_gains,
+        grad_gains.reshape(4, width),
     )
 
 

time: 929 us -> 735 us (0.79)
  waiting for transfers between devices: 233 us -> 65.2 us
  blocking collectives: 134 us -> 60.7 us
  Pallas kernels: 329 us -> 379 us
    reduce_scatter x4 -> x3, waiting for transfers between devices: 196 us -> 64.5 us  [scatter_sum(): return lax.psum_scatter(values, axes, scatter_dimension=0, tiled=True)]
    pallas_call x5, Pallas kernels: 329 us -> 379 us  [call(): pl.pallas_call(self.body, out_shape=shapes, in_specs=in_specs, out_specs=...]
    psum x1 -> x0, blocking collectives: 39.7 us -> none  [per_device(): grad_gains = lax.psum(jnp.concatenate([wide, gain_attn, gain_feed]), ALL)]
    all_gather x4 -> x3, waiting for transfers between devices: 36.3 us -> 0.04 us  [gather(): return lax.all_gather(values, axes, axis=0, tiled=True)]
    all_to_all x1 -> x0, blocking collectives: 26.9 us -> none  [per_device(): qkv_cut = lax.all_to_all(qkv_cut, GROUP, 0, 0, tiled=True)]
    all_gather x1 -> x0, blocking collectives: 13.8 us -> none  [gather(): return lax.all_gather(values, axes, axis=0, tiled=True)]
    unnamed x80 -> x79, local copies, waits for them, and re-layouts: 28 us -> 29.4 us
  transfers between devices with their start and end apart: 9 -> 8, of which waited for: 4 -> 1; matrix products, arithmetic and copies ran while one was open for 15% -> 14% of each run, Pallas kernels for 19% -> 31%
where the time goes in v3:
time: 735 us; the launch traced here: 727 us
  Pallas kernels  379 us (52%)
  matrix products  115 us (16%)
  waiting for transfers between devices  65.2 us (9%)
  local copies, waits for them, and re-layouts  64.6 us (9%)
  blocking collectives  60.7 us (8%)
  other arithmetic  23.5 us (3%)
  between operations  15 us (2%)
    pallas_call x5, Pallas kernels, call(): pl.pallas_call(self.body, out_shape=shapes, in_specs=in_specs, out_specs=...  379 us
    reduce_scatter x3, waiting for transfers between devices, scatter_sum(): return lax.psum_scatter(values, axes, scatter_dimension=0, tiled=True)  64.5 us
    dot_general x4, matrix products, dot(): return jnp.dot(left, right, preferred_element_type=F32)  36.3 us
    dot_general x4, matrix products, dot_rows(): lax.dot_general(left, right, (((1,), (1,)), ((), ())), preferred_element_...  34.4 us
    dot_general x4, matrix products, dot_first(): lax.dot_general(left, right, (((0,), (0,)), ((), ())), preferred_element_...  30.8 us
    unnamed x79, local copies, waits for them, and re-layouts  29.4 us
    psum x1, blocking collectives, per_device(): squares = lax.psum(squares, GROUP)  16.1 us
    psum x1, blocking collectives, per_device(): means = lax.psum(sums, GROUP) / width  15.2 us
  transfers between devices with their start and end apart: 8, of which 1 were waited for; matrix products, arithmetic and copies ran while one was open for 14% of the time, Pallas kernels for 31%

profile of v3, /device:TPU:0, one launch (start us, length us, event | category | flops | bytes accessed | tf_op | source)
XLA Modules:
  0.0 727.2 jit_solution(3294139185692286071)
XLA Ops:
  12.8 12.6 %all_to_all.64 = bf16[256,2,2048]{0,2,1:T(8,128)(2,1)S(1)} all-to-all(bf16[256,2,2048]{0,2,1:T(8,128)(2,1)S(1)} %bitcast.137), channel_id=1, replica_groups=mesh['chip'=4,'core'=2,'ctx'=4] {'core'}, dimensions={1} | all-to-all | bytes 4194304 | tf_op jit(solution)/shard_map/all_to_all | solution.py:740
  37.0 68.4 %gather_tokens.1 = (bf16[2048,768]{1,0:T(8,128)(2,1)S(1)}, s32[64,128]{1,0:T(8,128)S(1)}, bf16[1024,2048]{1,0:T(8,128)(2,1)}) custom-call(bf16[128,2048]{1,0:T(8,128)(2,1)S(1)} %bitcast.122, bf16[8,64,768]{2,1,0:T(8,128)(2,1)S(1)} %reshape.157.refs_1_, s32[8,128]{1,0:T(8,128)S(1)} %broadcast_in_dim.29.refs_2_), custom_call_target="tpu_custom_call" | custom-call | bytes 125829120 | tf_op jit(solution)/shard_map/gather_tokens/pallas_call | solution.py:377
  107.0 7.4 %fusion.35 = f32[1024,768]{0,1:T(8,128)} fusion(bf16[1024,2048]{1,0:T(8,128)(2,1)} %get-tuple-element.26, bf16[2048,768]{1,0:T(8,128)(2,1)S(1)} %get-tuple-element.27), kind=kOutput, calls=%fused_computation.103 | convolution fusion | flops 3221225472 | bytes 10485760 | tf_op jit(solution)/shard_map/dot_general | solution.py:685
  116.8 16.1 %psum.14 = f32[2,1024]{1,0:T(2,128)S(1)} all-reduce(f32[2,1024]{1,0:T(2,128)S(1)} %pad_maximum_fusion.9), channel_id=1, replica_groups=mesh['chip'=4,'core'=2,'ctx'=4] {'core','ctx'}, use_global_device_ids=true, to_apply=%region_2.0 | all-reduce | flops 2048 | bytes 16384 | tf_op jit(solution)/shard_map/psum | solution.py:749
  152.9 5.8 fusion.34
  162.0 4.7 convolution_convert_fusion.2.refs_0_
  166.6 78.2 %sum_projected.1 = (f32[128,2048]{1,0:T(8,128)S(1)}, f32[128,2048]{1,0:T(8,128)S(1)}, bf16[1024,2048]{1,0:T(8,128)(2,1)}) custom-call(bf16[1024,2048]{1,0:T(8,128)(2,1)} %convolution_convert_fusion.2.refs_0_, bf16[128,2048]{1,0:T(8,128)(2,1)S(1)} %bitcast.123, f32[4,2048]{1,0:T(4,128)S(1)} %copy-done.6), custom_call_target="tpu_custom_call" | custom-call | bytes 209715200 | tf_op jit(solution)/shard_map/sum_projected/pallas_call | solution.py:377
  244.9 12.5 %fusion.36 = f32[1024,2048]{1,0:T(8,128)S(1)} fusion(bf16[1024,2048]{1,0:T(8,128)(2,1)} %get-tuple-element.29, bf16[2048,2048]{1,0:T(8,128)(2,1)} %all-gather.6.cloned.1.call-done), kind=kOutput, calls=%fused_computation.104 | convolution fusion | flops 8589934592 | bytes 20971520 | tf_op jit(solution)/shard_map/dot_general | solution.py:685
  263.4 9.4 %convolution_convert_fusion.5.refs_0_ = bf16[1024,2048]{1,0:T(8,128)(2,1)} fusion(bf16[1024,1024]{1,0:T(8,128)(2,1)} %multiply_convert_fusion.3, bf16[2048,1024]{1,0:T(8,128)(2,1)} %all-gather.8.cloned.1.call-done), kind=kOutput, calls=%fused_computation.17 | convolution fusion | flops 4297064448 | bytes 10485760 | tf_op jit(solution)/shard_map/dot_general | solution.py:689
  272.8 77.9 %sum_feed.1 = (bf16[128,2048]{1,0:T(8,128)(2,1)S(1)}, f32[1,2048]{1,0:T(1,128)S(1)}, bf16[1024,2048]{1,0:T(8,128)(2,1)}) custom-call(bf16[1024,2048]{1,0:T(8,128)(2,1)} %convolution_convert_fusion.5.refs_0_, f32[128,2048]{1,0:T(8,128)S(1)} %get-tuple-element.30.refs_1_, bf16[128,2048]{1,0:T(8,128)(2,1)S(1)} %bitcast.124, f32[4,2048]{1,0:T(4,128)S(1)} %copy-done.6), custom_call_target="tpu_custom_call" | custom-call | bytes 209715200 | tf_op jit(solution)/shard_map/sum_feed/pallas_call | solution.py:377
  350.7 8.5 %convolution_convert_fusion.4 = bf16[2048,1024]{1,0:T(8,128)(2,1)} fusion(bf16[1024,2048]{1,0:T(8,128)(2,1)} %get-tuple-element.32, bf16[1024,1024]{1,0:T(8,128)(2,1)S(1)} %copy-done.15), kind=kOutput, calls=%fused_computation.16 | convolution fusion | flops 4297064448 | bytes 10485760 | tf_op jit(solution)/shard_map/dot_general | solution.py:693
  359.3 11.7 %multiply_convert_fusion.2 = (bf16[1024,1024]{1,0:T(8,128)(2,1)S(1)}, bf16[1024,1024]{1,0:T(8,128)(2,1)S(1)}) fusion(f32[1024,2048]{1,0:T(8,128)} %copy-done.9, bf16[1024,2048]{1,0:T(8,128)(2,1)} %get-tuple-element.32, bf16[2048,1024]{1,0:T(8,128)(2,1)} %all-gather.8.cloned.1.call-done), kind=kOutput, calls=%fused_computation.7 | convolution fusion | flops 4308598784 | bytes 20971520 | tf_op jit(solution)/shard_map/dot_general | solution.py:685
  373.0 11.8 %convolution_convert_fusion = bf16[2048,2048]{1,0:T(8,128)(2,1)} fusion(bf16[1024,2048]{1,0:T(8,128)(2,1)S(1)} %copy-done.29, bf16[1024,1024]{1,0:T(8,128)(2,1)S(1)} %get-tuple-element.53, bf16[1024,1024]{1,0:T(8,128)(2,1)S(1)} %get-tuple-element.52), kind=kOutput, calls=%fused_computation.1 | convolution fusion | flops 8602517504 | bytes 16777216 | tf_op jit(solution)/shard_map/dot_general | solution.py:693
  384.8 14.4 %convolution_convert_fusion.1.refs_0_ = bf16[1024,2048]{1,0:T(8,128)(2,1)} fusion(bf16[2048,2048]{1,0:T(8,128)(2,1)} %all-gather.6.cloned.1.call-done, bf16[1024,1024]{1,0:T(8,128)(2,1)} %copy-done.31, bf16[1024,1024]{1,0:T(8,128)(2,1)} %copy-done.30), kind=kOutput, calls=%fused_computation.13 | convolution fusion | flops 8600420352 | bytes 16777216 | tf_op jit(solution)/shard_map/dot_general | solution.py:689
  399.3 78.3 %sum_back.1 = (f32[128,2048]{1,0:T(8,128)S(1)}, f32[1,2048]{1,0:T(1,128)S(1)}, bf16[1024,2048]{1,0:T(8,128)(2,1)}) custom-call(bf16[1024,2048]{1,0:T(8,128)(2,1)} %convolution_convert_fusion.1.refs_0_, f32[128,2048]{1,0:T(8,128)S(1)} %get-tuple-element.34.refs_1_, bf16[128,2048]{1,0:T(8,128)(2,1)S(1)} %bitcast.125, f32[4,2048]{1,0:T(4,128)S(1)} %copy-done.6), custom_call_target="tpu_custom_call" | custom-call | bytes 209715200 | tf_op jit(solution)/shard_map/sum_back/pallas_call | solution.py:377
  502.3 15.2 %psum.15 = f32[2,1024]{1,0:T(2,128)S(1)} all-reduce(f32[2,1024]{1,0:T(2,128)S(1)} %pad_maximum_fusion.10), channel_id=1, replica_groups=mesh['chip'=4,'core'=2,'ctx'=4] {'core','ctx'}, use_global_device_ids=true, to_apply=%region_8.9 | all-reduce | flops 2048 | bytes 16384 | tf_op jit(solution)/shard_map/psum | solution.py:831
  521.0 6.0 convolution_convert_fusion.6.refs_2_
  528.8 7.0 convolution_convert_fusion.3.refs_0_
  537.1 76.2 %sum_input.1 = (f32[128,2048]{1,0:T(8,128)S(1)}, f32[64,6144]{1,0:T(8,128)S(1)}, f32[4,16,128]{2,1,0:T(8,128)S(1)}) custom-call(bf16[1024,2048]{1,0:T(8,128)(2,1)} %convolution_convert_fusion.3.refs_0_, f32[128,2048]{1,0:T(8,128)S(1)} %copy-done.3, bf16[2048,768]{1,0:T(8,128)(2,1)} %convolution_convert_fusion.6.refs_2_, f32[40,128]{1,0:T(8,128)S(1)} %concatenate.40.refs_3_), custom_call_target="tpu_custom_call" | custom-call | bytes 209715200 | tf_op jit(solution)/shard_map/sum_input/pallas_call | solution.py:377
  614.8 5.7 all_to_all.66
  622.2 64.5 %reduce-scatter.6.cloned.1.call-done = bf16[512,2048]{1,0:T(8,128)(2,1)} async-done(((bf16[2048,2048]{1,0:T(8,128)(2,1)}), bf16[512,2048]{1,0:T(8,128)(2,1)}) %reduce-scatter.6.cloned.1.call-update) | async-done | bytes 2097168 | tf_op jit(solution)/shard_map/reduce_scatter | solution.py:701
  686.6 6.6 all_to_all.67
  695.8 6.7 reshape.173
  702.4 7.2 fusion.28
  (162 shorter events, 99.4 us)
Async XLA Ops:
  7.2 154.8 %all-gather.4.cloned.1.call-start = ((), (), s32[]{:S(2)}) async-start(), calls=%async_computation.7 | async-start | bytes 1310720 | tf_op jit(solution)/shard_map/all_gather | solution.py:697
  7.2 1.6 collective-permute-start
  9.5 235.3 %all-gather.6.cloned.1.call-start = ((), (), s32[]{:S(2)}) async-start(), calls=%async_computation.8 | async-start | bytes 10485760 | tf_op jit(solution)/shard_map/all_gather | solution.py:697
  27.7 235.7 %all-gather.8.cloned.1.call-start = ((), (), s32[]{:S(2)}) async-start(), calls=%async_computation.9 | async-start | bytes 5242880 | tf_op jit(solution)/shard_map/all_gather | solution.py:697
  32.9 4.1 copy-start.27
  32.9 4.1 copy-start
  34.2 492.8 %reduce-scatter.4.cloned.1.call-start = ((), (), s32[]{:S(2)}) async-start(), calls=%async_computation.10 | async-start | bytes 1310720 | tf_op jit(solution)/shard_map/reduce_scatter | solution.py:701
  107.0 25.9 %copy-start.6 = (f32[4,2048]{1,0:T(4,128)S(1)}, f32[4,2048]{1,0:T(4,128)}, u32[]{:S(2)}) copy-start(f32[4,2048]{1,0:T(4,128)} %refs_3_.3) | copy-start | bytes 98308
  147.7 4.5 copy-start.8
  152.9 5.9 copy-start.16
  152.9 5.9 copy-start.18
  152.9 5.9 copy-start.23
  161.9 82.9 %copy-start.12 = (bf16[2,512,2,128]{3,2,1,0:T(2,128)(2,1)}, bf16[2,512,2,128]{3,2,1,0:T(2,128)(2,1)S(1)}, u32[]{:S(2)}) copy-start(bf16[2,512,2,128]{3,2,1,0:T(2,128)(2,1)S(1)} %copy.82) | copy-start | bytes 1572868
  263.4 9.4 %copy-start.1 = (bf16[1,128,2048]{2,1,0:T(8,128)(2,1)S(1)}, bf16[1,128,2048]{2,1,0:T(8,128)(2,1)}, u32[]{:S(2)}) copy-start(bf16[1,128,2048]{2,1,0:T(8,128)(2,1)} %param.17) | copy-start | bytes 1572868
  272.8 77.9 %copy-start.15 = (bf16[1024,1024]{1,0:T(8,128)(2,1)S(1)}, bf16[1024,1024]{1,0:T(8,128)(2,1)}, u32[]{:S(2)}) copy-start(bf16[1024,1024]{1,0:T(8,128)(2,1)} %multiply_convert_fusion.3) | copy-start | bytes 6291460
  350.7 8.6 %copy-start.4 = (bf16[128,2048]{1,0:T(8,128)(2,1)}, bf16[128,2048]{1,0:T(8,128)(2,1)S(1)}, u32[]{:S(2)}) copy-start(bf16[128,2048]{1,0:T(8,128)(2,1)S(1)} %get-tuple-element.31) | copy-start | bytes 1572868
  359.3 13.8 %copy-start.29 = (bf16[1024,2048]{1,0:T(8,128)(2,1)S(1)}, bf16[1024,2048]{1,0:T(8,128)(2,1)}, u32[]{:S(2)}) copy-start(bf16[1024,2048]{1,0:T(8,128)(2,1)} %get-tuple-element.29) | copy-start | bytes 12582916
  399.3 79.3 %copy-start.13 = (bf16[2,512,2,128]{3,2,1,0:T(2,128)(2,1)S(1)}, bf16[2,512,2,128]{3,2,1,0:T(2,128)(2,1)}, u32[]{:S(2)}) copy-start(bf16[2,512,2,128]{3,2,1,0:T(2,128)(2,1)} %copy-done.12) | copy-start | bytes 1572868
  483.0 131.8 %reduce-scatter.8.cloned.1.call-start = ((), (), s32[]{:S(2)}) async-start(), calls=%async_computation.12 | async-start | bytes 5242880 | tf_op jit(solution)/shard_map/reduce_scatter | solution.py:701
  483.6 203.0 %reduce-scatter.6.cloned.1.call-start = ((), (), s32[]{:S(2)}) async-start(), calls=%async_computation.11 | async-start | bytes 10485760 | tf_op jit(solution)/shard_map/reduce_scatter | solution.py:701
  484.8 4.1 copy-start.24
  521.0 7.8 %copy-start.25 = (bf16[32,8,2,512]{3,1,2,0:T(8,128)(2,1)S(1)}, bf16[32,8,2,512]{3,1,2,0:T(8,128)(2,1)}, u32[]{:S(2)}) copy-start(bf16[32,8,2,512]{3,1,2,0:T(8,128)(2,1)} %copy.116) | copy-start | bytes 1572868
  527.1 86.9 %collective-permute-start.1 = (bf16[64,2048]{1,0:T(8,128)(2,1)}, bf16[64,2048]{1,0:T(8,128)(2,1)S(1)}, u32[]{:S(2)}, u32[]{:S(2)}) collective-permute-start(bf16[64,2048]{1,0:T(8,128)(2,1)} %reduce-scatter.4.cloned.1.call-done), channel_id=1, source_target_pairs={{0,0},{8,1},{16,2},{24,3},{1,4},{9,5},{17,6},{25,7},{2,8},{10,9},{... | collective-permute-start | bytes 786440 | tf_op jit(solution)/shard_map/ppermute | solution.py:850
  713.5 3.8 copy-start.5
  (16 other events, 30.9 us)
Sparse Core Ops, SparseCore 0:
  9.8 47.3 all-gather.3
  59.7 102.5 all-gather.5
  164.6 52.6 all-gather.7
  483.1 26.2 reduce-scatter.3
  512.5 81.4 reduce-scatter.7
  596.9 89.6 reduce-scatter.5

commit v4 on v3

--- a/solution.py
+++ b/solution.py
@@ -139,7 +139,7 @@
 
         barrier = pltpu.get_barrier_semaphore()
         if extra is not None:
-            meet_all(spans)
+            meet_all(spans, getattr(extra, "moves", False))
         else:
             pl.semaphore_signal(barrier, 1, device_id={"core": other}, device_id_type=MESH_ID)
 
@@ -392,7 +392,22 @@
         )(*operands)
 
 
-def meet_all(spans):
+def owner_of(chip, core, place, spans):
+    member = core * spans + place
+    return member // 2, lax.rem(member, 2), chip
+
+
+def summer_of(chip, core, place, spans):
+    member = chip * 2 + core
+    return place, member // spans, lax.rem(member, spans)
+
+
+def stays(chip, core, place, spans):
+    to_chip, to_core, to_place = owner_of(chip, core, place, spans)
+    return jnp.logical_and(to_chip == chip, jnp.logical_and(to_core == core, to_place == place))
+
+
+def meet_all(spans, moves):
     chips = lax.axis_size("chip")
     barrier = pltpu.get_barrier_semaphore()
     chip = lax.axis_index("chip")
@@ -407,11 +422,138 @@
         pl.semaphore_signal(
             barrier, 1, device_id={"core": to_core, "ctx": to_place}, device_id_type=MESH_ID
         )
-    pl.semaphore_wait(barrier, chips - 1 + 2 * spans - 1)
+    count = chips - 1 + 2 * spans - 1
+    if moves:
+        away = jnp.logical_not(stays(chip, core, place, spans))
+
+        @pl.when(away)
+        def _():
+            for find in (owner_of, summer_of):
+                to_chip, to_core, to_place = find(chip, core, place, spans)
+                pl.semaphore_signal(
+                    barrier, 1, device_id={"chip": to_chip, "core": to_core, "ctx": to_place}, device_id_type=MESH_ID
+                )
+
+        count = count + 2 * away.astype(jnp.int32)
+    pl.semaphore_wait(barrier, count)
 
 
 def step_member(core, place, s, spans):
     return lax.rem(core + s % 2, 2), lax.rem(place + s // 2, spans)
+
+
+def meet_other_core():
+    barrier = pltpu.get_barrier_semaphore()
+    other = 1 - lax.axis_index("core")
+    pl.semaphore_signal(barrier, 1, device_id={"core": other}, device_id_type=MESH_ID)
+    pl.semaphore_wait(barrier, 1)
+
+
+def split_body(gate, up, down, gate_up_out, down_out, held, load_sem, store_sem, send_sem, recv_sem):
+    core = lax.axis_index("core")
+    other = 1 - core
+    rows, width = gate.shape
+    half = width // 2
+    where = pl.ds(pl.multiple_of(core * rows, rows), rows)
+    places = [gate_up_out.at[where, :half], gate_up_out.at[where, half:], down_out.at[where, :]]
+    mine = pl.ds(pl.multiple_of(core * half, half), half)
+    theirs = pl.ds(pl.multiple_of(other * half, half), half)
+    loads = [
+        pltpu.make_async_copy(a.at[:, mine], held.at[i], load_sem.at[i]) for i, a in enumerate((gate, up, down))
+    ]
+    for load in loads:
+        load.start()
+    meet_other_core()
+    sends = [
+        pltpu.make_async_remote_copy(
+            src_ref=a.at[:, theirs], dst_ref=places[i], send_sem=send_sem.at[i], recv_sem=recv_sem.at[i],
+            device_id={"core": other}, device_id_type=MESH_ID,
+        )
+        for i, a in enumerate((gate, up, down))
+    ]
+    for send in sends:
+        send.start()
+    stores = [pltpu.make_async_copy(held.at[i], places[i], store_sem.at[i]) for i in range(3)]
+    for load, store in zip(loads, stores):
+        load.wait()
+        store.start()
+    for store, send in zip(stores, sends):
+        store.wait()
+        send.wait()
+
+
+def split_columns(gate, up, down):
+    rows, width = gate.shape
+    hbm = pl.BlockSpec(memory_space=pl.ANY)
+    three = pltpu.SemaphoreType.DMA((3,))
+    return pl.pallas_call(
+        split_body,
+        out_shape=[
+            jax.ShapeDtypeStruct((2 * rows, width), BF16),
+            jax.ShapeDtypeStruct((2 * rows, width // 2), BF16),
+        ],
+        in_specs=[hbm] * 3,
+        out_specs=[hbm] * 2,
+        scratch_shapes=[pltpu.VMEM((3, rows, width // 2), BF16)] + [three] * 4,
+        compiler_params=pltpu.CompilerParams(collective_id=6, has_side_effects=True, vmem_limit_bytes=8 << 20),
+        name="split_columns",
+    )(gate, up, down)
+
+
+def join_body(gate_up, down, gate_out, up_out, down_out, gate_up_in, down_in, send_sem, recv_sem):
+    core = lax.axis_index("core")
+    other = 1 - core
+    rows, width = gate_out.shape
+    half = width // 2
+    meet_other_core()
+    theirs = pl.ds(pl.multiple_of(other * rows, rows), rows)
+    sends = [
+        pltpu.make_async_remote_copy(
+            src_ref=a.at[theirs], dst_ref=b, send_sem=send_sem.at[i], recv_sem=recv_sem.at[i],
+            device_id={"core": other}, device_id_type=MESH_ID,
+        )
+        for i, (a, b) in enumerate(((gate_up, gate_up_in), (down, down_in)))
+    ]
+    for send in sends:
+        send.start()
+    mine = pl.ds(pl.multiple_of(core * half, half), half)
+    far = pl.ds(pl.multiple_of(other * half, half), half)
+    step = 16
+
+    def rows_at(i, base):
+        return pl.ds(pl.multiple_of(base + i * step, step), step)
+
+    @pl.loop(0, rows // step)
+    def _(i):
+        here, there = rows_at(i, core * rows), rows_at(i, 0)
+        gate_out[there, mine] = gate_up[here, :half].astype(F32)
+        up_out[there, mine] = gate_up[here, half:].astype(F32)
+        down_out[there, mine] = down[here, :].astype(F32)
+
+    for send in sends:
+        send.wait()
+
+    @pl.loop(0, rows // step)
+    def _(i):
+        there = rows_at(i, 0)
+        gate_out[there, far] = gate_up_in[there, :half].astype(F32)
+        up_out[there, far] = gate_up_in[there, half:].astype(F32)
+        down_out[there, far] = down_in[there, :].astype(F32)
+
+
+def join_columns(gate_up, down):
+    rows, width = gate_up.shape[0] // 2, gate_up.shape[1]
+    vmem = pl.BlockSpec(memory_space=pltpu.VMEM)
+    two = pltpu.SemaphoreType.DMA((2,))
+    return pl.pallas_call(
+        join_body,
+        out_shape=[jax.ShapeDtypeStruct((rows, width), F32)] * 3,
+        in_specs=[vmem] * 2,
+        out_specs=[vmem] * 3,
+        scratch_shapes=[pltpu.VMEM((rows, width), BF16), pltpu.VMEM((rows, width // 2), BF16), two, two],
+        compiler_params=pltpu.CompilerParams(collective_id=7, has_side_effects=True, vmem_limit_bytes=32 << 20),
+        name="join_columns",
+    )(gate_up, down)
 
 
 class Extra:
@@ -524,23 +666,26 @@
 
 
 class QkvGrads(Extra):
-    n_in, n_out = 2, 2
-
-    def __init__(self, spans, chips, members, grads, sums):
+    n_in, n_out = 3, 3
+    moves = True
+
+    def __init__(self, spans, chips, members, grads, sums, out_grads):
         self.spans, self.chips, self.members = spans, chips, members
+        self.out_rows = out_grads.shape[0] // chips
         self.block, self.columns = grads.shape[0] // (chips * members), grads.shape[1]
         self.part = self.columns // 3
         self.width = self.part * members
         self.own_rows = self.part // 128
         self.sum_rows = sums.shape[0]
-        self.operands = [grads, sums]
+        self.operands = [grads, sums, out_grads]
         vmem = pl.BlockSpec(memory_space=pltpu.VMEM)
-        self.in_specs = [vmem, vmem]
+        self.in_specs = [vmem] * 3
         self.out_shapes = [
             jax.ShapeDtypeStruct((self.block, 3 * self.width), F32),
             jax.ShapeDtypeStruct((4, self.width // 128, 128), F32),
+            jax.ShapeDtypeStruct((self.out_rows, self.width), F32),
         ]
-        self.out_specs = [vmem, vmem]
+        self.out_specs = [vmem] * 3
 
     def scratch(self):
         sems = pltpu.SemaphoreType.DMA((self.members,))
@@ -553,7 +698,10 @@
             pltpu.VMEM((self.chips, self.sum_rows, 128), F32),
             pltpu.VMEM((self.sum_rows, 128), F32),
             pltpu.VMEM((self.members, self.sum_rows, 128), F32),
-        ] + [cross] * 2 + [sems] * 2 + [chip_sems] * 2 + [sems] * 2
+            pltpu.VMEM((self.chips, self.out_rows, self.width), BF16),
+            pltpu.VMEM((self.out_rows, self.width), BF16),
+            pltpu.VMEM((self.out_rows, self.width), BF16),
+        ] + [cross] * 2 + [sems] * 2 + [chip_sems] * 2 + [sems] * 2 + [chip_sems] * 2 + [pltpu.SemaphoreType.DMA] * 2
 
     def at(self, chip, m):
         return pl.ds(pl.multiple_of((chip * self.members + m) * self.block, self.block), self.block)
@@ -585,15 +733,31 @@
             core=core, ctx=place,
         )
 
+    def out_copy(self, s):
+        other = lax.rem(self.chip + s, self.chips)
+        rows = pl.ds(pl.multiple_of(other * self.out_rows, self.out_rows), self.out_rows)
+        return self.remote(
+            self.ins[2].at[rows], self.out_in.at[s], self.out_send.at[s], self.out_recv.at[s], chip=other
+        )
+
+    def move_copy(self):
+        chip, core, place = owner_of(self.chip, self.core, self.place, self.spans)
+        return self.remote(
+            self.out_sum, self.out_final, self.move_send, self.move_recv, chip=chip, core=core, ctx=place
+        )
+
     def start(self):
         self.locate()
         (
             self.arrived, self.summed, self.columns_in, self.sums_in, self.sums_chips, self.sums_members,
+            self.out_in, self.out_sum, self.out_final,
             self.cross_send, self.cross_recv, self.member_send, self.member_recv,
             self.sums_send, self.sums_recv, self.last_send, self.last_recv,
+            self.out_send, self.out_recv, self.move_send, self.move_recv,
         ) = self.held
         for s in range(1, self.chips):
             self.sums_chip(s).start()
+            self.out_copy(s).start()
 
         @pl.loop(0, self.members)
         def _(i):
@@ -625,6 +789,23 @@
             self.sums_members[self.me] = total
             for s in range(1, self.members):
                 self.sums_member(s).start()
+
+        @pl.when(t == 2)
+        def _():
+            rows = pl.ds(pl.multiple_of(self.chip * self.out_rows, self.out_rows), self.out_rows)
+            total = self.ins[2][rows, :].astype(F32)
+            for s in range(1, self.chips):
+                self.out_copy(s).wait_recv()
+                total = total + self.out_in[s].astype(F32)
+            self.out_sum[...] = total.astype(BF16)
+
+            @pl.when(stays(self.chip, self.core, self.place, self.spans))
+            def _():
+                self.out_final[...] = total.astype(BF16)
+
+            @pl.when(jnp.logical_not(stays(self.chip, self.core, self.place, self.spans)))
+            def _():
+                self.move_copy().start()
 
     def finish(self, ticks):
         self.send_blocks(1, self.members)
@@ -650,8 +831,14 @@
                 self.outs[0][:, i * self.width + m * self.part : i * self.width + (m + 1) * self.part] = (
                     self.columns_in[m, :, i * self.part : (i + 1) * self.part].astype(F32)
                 )
+        @pl.when(jnp.logical_not(stays(self.chip, self.core, self.place, self.spans)))
+        def _():
+            self.move_copy().wait()
+
+        self.outs[2][...] = self.out_final[...].astype(F32)
         for s in range(1, self.chips):
             self.sums_chip(s).wait_send()
+            self.out_copy(s).wait_send()
 
         @pl.loop(0, self.members)
         def _(m):
@@ -734,12 +921,8 @@
     out_w = gather(lax.ppermute(w_out, ALL, swaps), "chip")
 
     hidden = w_gate.shape[1] // cores
-    gate_up = jnp.concatenate(
-        [w_gate.reshape(-1, cores, 1, hidden), w_up.reshape(-1, cores, 1, hidden)], 2
-    ).reshape(-1, cores * 2 * hidden)
-    gate_up = lax.all_to_all(gate_up, "core", 1, 0, tiled=True)
-    gate_up_w = gather(gate_up, "chip")
-    down_w = gather(lax.all_to_all(w_down_t, "core", 1, 0, tiled=True), "chip")
+    gate_up, down = split_columns(w_gate, w_up, w_down_t)
+    gate_up_w, down_w = gather(gate_up, "chip"), gather(down, "chip")
 
     mixed = dot(tokens_all, qkv_w)
     query_raw = mixed[:, :part]
@@ -798,14 +981,7 @@
     down_part = dot_first(feed_grad_all, activated).astype(BF16)
     gate_up_part = dot_first(residual_all, gate_up_grad).astype(BF16)
     back_part, down_part, gate_up_part = lax.optimization_barrier((back_part, down_part, gate_up_part))
-    grad_gate_up = scatter_sum(gate_up_part, "chip")
-    grad_gate_up = lax.all_to_all(grad_gate_up, "core", 0, 1, tiled=True)
-    grad_gate_up = grad_gate_up.reshape(-1, cores, 2, hidden).astype(F32)
-    grad_gate = grad_gate_up[:, :, 0].reshape(-1, cores * hidden)
-    grad_up = grad_gate_up[:, :, 1].reshape(-1, cores * hidden)
-    grad_down = scatter_sum(down_part, "chip")
-    grad_down = lax.all_to_all(grad_down, "core", 0, 1, tiled=True).astype(F32)
-
+    gate_up_sum, down_sum = scatter_sum(gate_up_part, "chip"), scatter_sum(down_part, "chip")
     residual_grad, gain_attn, projected_all = spread(True, after_back, 3, 2, 1).call(
         "sum_back",
         4,
@@ -841,14 +1017,15 @@
         [a.reshape(-1, 128) for a in (gain_attn, gain_feed, gain_query, gain_key)]
         + [jnp.zeros((-2 * part // 128 % 8, 128), F32)]
     )
-    input_grad, grad_qkv, grad_gains = Exchange(
+    input_grad, grad_qkv, grad_gains, grad_out = Exchange(
         spans, rows, width, PIECE, True, False, after_input, 1, 1, None,
-        QkvGrads(spans, chips, members, dot_first(tokens_all, mixed_grad).astype(BF16), sums),
+        QkvGrads(
+            spans, chips, members, dot_first(tokens_all, mixed_grad).astype(BF16), sums,
+            dot_first(attended_low, projected_all).astype(BF16),
+        ),
     ).call("sum_input", 5, input_part, [residual_grad], [own])
 
-    out_part = scatter_sum(dot_first(attended_low, projected_all).astype(BF16), "chip")
-    grad_out = lax.ppermute(out_part, ALL, [(b, a) for a, b in swaps]).astype(F32)
-
+    grad_gate, grad_up, grad_down = join_columns(gate_up_sum, down_sum)
     return (
         output[None],
         input_grad[None],

time: 735 us -> 624 us (0.85)
  waiting for transfers between devices: 65.2 us -> 1.29 us
  blocking collectives: 60.7 us -> 32 us
  Pallas kernels: 379 us -> 399 us
  local copies, waits for them, and re-layouts: 64.6 us -> 44.8 us
    reduce_scatter x3 -> x2, waiting for transfers between devices: 64.5 us -> 0.01 us  [scatter_sum(): return lax.psum_scatter(values, axes, scatter_dimension=0, tiled=True)]
    all_to_all x4 -> x0, blocking collectives: 29.4 us -> none  [the longest x1 12.6 us: per_device(): gate_up = lax.all_to_all(gate_up, 'core', 1, 0, tiled=True)]
    pallas_call x0 -> x2, Pallas kernels: none -> 14.8 us  [the longest x1 11.1 us: split_columns(): pl.pallas_call(split_body, out_shape=[jax.ShapeDtypeStruct((2 * rows, wid...]
    convert_element_type x2 -> x0, local copies, waits for them, and re-layouts: 8.13 us -> none  [the longest x1 6.67 us: per_device(): grad_gate_up = grad_gate_up.reshape(-1, cores, 2, hidden).astype(F32)]
    unnamed x79 -> x92, local copies, waits for them, and re-layouts: 29.4 us -> 30.4 us
  transfers between devices with their start and end apart: 8 -> 6, of which waited for: 1 -> 0; matrix products, arithmetic and copies ran while one was open for 14% -> 14% of each run, Pallas kernels for 31% -> 51%
where the time goes in v4:
time: 624 us; the launch traced here: 618 us
  Pallas kernels  399 us (64%)
  matrix products  108 us (17%)
  local copies, waits for them, and re-layouts  44.8 us (7%)
  blocking collectives  32 us (5%)
  other arithmetic  16.6 us (3%)
  between operations  14.7 us (2%)
    pallas_call x5, Pallas kernels, call(): pl.pallas_call(self.body, out_shape=shapes, in_specs=in_specs, out_specs=...  384 us
    dot_general x4, matrix products, dot(): return jnp.dot(left, right, preferred_element_type=F32)  35.1 us
    dot_general x4, matrix products, dot_rows(): lax.dot_general(left, right, (((1,), (1,)), ((), ())), preferred_element_...  32.5 us
    unnamed x92, local copies, waits for them, and re-layouts  30.4 us
    dot_general x4, matrix products, dot_first(): lax.dot_general(left, right, (((0,), (0,)), ((), ())), preferred_element_...  26.6 us
    psum x1, blocking collectives, per_device(): squares = lax.psum(squares, GROUP)  16.7 us
    psum x1, blocking collectives, per_device(): means = lax.psum(sums, GROUP) / width  15.3 us
  transfers between devices with their start and end apart: 6, of which 0 were waited for; matrix products, arithmetic and copies ran while one was open for 14% of the time, Pallas kernels for 51%

profile of v4, /device:TPU:0, one launch (start us, length us, event | category | flops | bytes accessed | tf_op | source)
XLA Modules:
  0.0 618.1 jit_solution(5839929087373135154)
XLA Ops:
  13.3 11.1 %split_columns.1 = (bf16[512,2048]{1,0:T(8,128)(2,1)}, bf16[512,1024]{1,0:T(8,128)(2,1)}) custom-call(bf16[256,2048]{1,0:T(8,128)(2,1)S(1)} %copy-done.3, bf16[256,2048]{1,0:T(8,128)(2,1)S(1)} %copy-done.4, bf16[256,2048]{1,0:T(8,128)(2,1)S(1)} %copy-done.5), custom_call_target="tpu_custom_call" | custom-call | tf_op jit(solution)/shard_map/split_columns/pallas_call | solution.py:489
  26.8 67.5 %gather_tokens.1 = (bf16[2048,768]{1,0:T(8,128)(2,1)S(1)}, s32[64,128]{1,0:T(8,128)S(1)}, bf16[1024,2048]{1,0:T(8,128)(2,1)}) custom-call(bf16[128,2048]{1,0:T(8,128)(2,1)S(1)} %bitcast.96, bf16[8,64,768]{2,1,0:T(8,128)(2,1)S(1)} %reshape.131.refs_1_, s32[8,128]{1,0:T(8,128)S(1)} %broadcast_in_dim.29.refs_2_), custom_call_target="tpu_custom_call" | custom-call | bytes 125829120 | tf_op jit(solution)/shard_map/gather_tokens/pallas_call | solution.py:377
  94.3 6.4 %fusion.34 = f32[1024,768]{0,1:T(8,128)S(1)} fusion(bf16[1024,2048]{1,0:T(8,128)(2,1)} %get-tuple-element.32, bf16[2048,768]{1,0:T(8,128)(2,1)S(1)} %get-tuple-element.33), kind=kOutput, calls=%fused_computation.99 | convolution fusion | flops 3221225472 | bytes 10485760 | tf_op jit(solution)/shard_map/dot_general | solution.py:872
  102.4 16.7 %psum.14 = f32[2,1024]{1,0:T(2,128)S(1)} all-reduce(f32[2,1024]{1,0:T(2,128)S(1)} %pad_maximum_fusion.8), channel_id=1, replica_groups=mesh['chip'=4,'core'=2,'ctx'=4] {'core','ctx'}, use_global_device_ids=true, to_apply=%region_2.0 | all-reduce | flops 2048 | bytes 16384 | tf_op jit(solution)/shard_map/psum | solution.py:932
  137.8 5.9 fusion.33
  147.6 4.5 convolution_convert_fusion.2.refs_0_
  152.1 77.3 %sum_projected.1 = (f32[128,2048]{1,0:T(8,128)S(1)}, f32[128,2048]{1,0:T(8,128)S(1)}, bf16[1024,2048]{1,0:T(8,128)(2,1)}) custom-call(bf16[1024,2048]{1,0:T(8,128)(2,1)} %convolution_convert_fusion.2.refs_0_, bf16[128,2048]{1,0:T(8,128)(2,1)S(1)} %bitcast.97, f32[4,2048]{1,0:T(4,128)S(1)} %copy-done.13), custom_call_target="tpu_custom_call" | custom-call | bytes 209715200 | tf_op jit(solution)/shard_map/sum_projected/pallas_call | solution.py:377
  230.4 12.5 %fusion.35 = f32[1024,2048]{1,0:T(8,128)S(1)} fusion(bf16[1024,2048]{1,0:T(8,128)(2,1)} %get-tuple-element.35, bf16[2048,2048]{1,0:T(8,128)(2,1)} %all-gather.6.cloned.1.call-done), kind=kOutput, calls=%fused_computation.100 | convolution fusion | flops 8589934592 | bytes 20971520 | tf_op jit(solution)/shard_map/dot_general | solution.py:872
  242.9 3.2 copy-done.19
  246.1 2.7 multiply_convert_fusion.3
  248.9 9.4 %convolution_convert_fusion.5.refs_0_ = bf16[1024,2048]{1,0:T(8,128)(2,1)} fusion(bf16[1024,1024]{1,0:T(8,128)(2,1)} %multiply_convert_fusion.3, bf16[2048,1024]{1,0:T(8,128)(2,1)} %all-gather.8.cloned.1.call-done), kind=kOutput, calls=%fused_computation.16 | convolution fusion | flops 4297064448 | bytes 10485760 | tf_op jit(solution)/shard_map/dot_general | solution.py:876
  258.3 78.0 %sum_feed.1 = (bf16[128,2048]{1,0:T(8,128)(2,1)S(1)}, f32[1,2048]{1,0:T(1,128)S(1)}, bf16[1024,2048]{1,0:T(8,128)(2,1)}) custom-call(bf16[1024,2048]{1,0:T(8,128)(2,1)} %convolution_convert_fusion.5.refs_0_, f32[128,2048]{1,0:T(8,128)S(1)} %get-tuple-element.38.refs_1_, bf16[128,2048]{1,0:T(8,128)(2,1)S(1)} %bitcast.98, f32[4,2048]{1,0:T(4,128)S(1)} %copy-done.13), custom_call_target="tpu_custom_call" | custom-call | bytes 209715200 | tf_op jit(solution)/shard_map/sum_feed/pallas_call | solution.py:377
  336.4 8.4 %convolution_convert_fusion.4 = bf16[2048,1024]{1,0:T(8,128)(2,1)} fusion(bf16[1024,2048]{1,0:T(8,128)(2,1)} %get-tuple-element.40, bf16[1024,1024]{1,0:T(8,128)(2,1)S(1)} %copy-done.24), kind=kOutput, calls=%fused_computation.15 | convolution fusion | flops 4297064448 | bytes 10485760 | tf_op jit(solution)/shard_map/dot_general | solution.py:880
  344.7 11.7 %multiply_convert_fusion.2 = (bf16[1024,1024]{1,0:T(8,128)(2,1)S(1)}, bf16[1024,1024]{1,0:T(8,128)(2,1)S(1)}) fusion(f32[1024,2048]{1,0:T(8,128)} %copy-done.19, bf16[1024,2048]{1,0:T(8,128)(2,1)} %get-tuple-element.40, bf16[2048,1024]{1,0:T(8,128)(2,1)} %all-gather.8.cloned.1.call-done), kind=kOutput, calls=%fused_computation.6 | convolution fusion | flops 4308598784 | bytes 20971520 | tf_op jit(solution)/shard_map/dot_general | solution.py:872
  358.5 12.0 %convolution_convert_fusion = bf16[2048,2048]{1,0:T(8,128)(2,1)} fusion(bf16[1024,2048]{1,0:T(8,128)(2,1)S(1)} %copy-done.37, bf16[1024,1024]{1,0:T(8,128)(2,1)S(1)} %get-tuple-element.65, bf16[1024,1024]{1,0:T(8,128)(2,1)S(1)} %get-tuple-element.64), kind=kOutput, calls=%fused_computation.1 | convolution fusion | flops 8602517504 | bytes 16777216 | tf_op jit(solution)/shard_map/dot_general | solution.py:880
  370.5 14.4 %convolution_convert_fusion.1.refs_0_ = bf16[1024,2048]{1,0:T(8,128)(2,1)} fusion(bf16[2048,2048]{1,0:T(8,128)(2,1)} %all-gather.6.cloned.1.call-done, bf16[1024,1024]{1,0:T(8,128)(2,1)} %copy-done.39, bf16[1024,1024]{1,0:T(8,128)(2,1)} %copy-done.38), kind=kOutput, calls=%fused_computation.12 | convolution fusion | flops 8600420352 | bytes 16777216 | tf_op jit(solution)/shard_map/dot_general | solution.py:876
  386.2 79.4 %sum_back.1 = (f32[128,2048]{1,0:T(8,128)S(1)}, f32[1,2048]{1,0:T(1,128)S(1)}, bf16[1024,2048]{1,0:T(8,128)(2,1)}) custom-call(bf16[1024,2048]{1,0:T(8,128)(2,1)} %convolution_convert_fusion.1.refs_0_, f32[128,2048]{1,0:T(8,128)S(1)} %copy-done.10, bf16[128,2048]{1,0:T(8,128)(2,1)S(1)} %bitcast.99, f32[4,2048]{1,0:T(4,128)S(1)} %copy-done.13), custom_call_target="tpu_custom_call" | custom-call | bytes 209715200 | tf_op jit(solution)/shard_map/sum_back/pallas_call | solution.py:377
  465.7 3.5 convolution_convert_fusion.10
  469.8 3.3 multiply_reduce_fusion
  482.0 15.3 %psum.15 = f32[2,1024]{1,0:T(2,128)S(1)} all-reduce(f32[2,1024]{1,0:T(2,128)S(1)} %pad_maximum_fusion.9), channel_id=1, replica_groups=mesh['chip'=4,'core'=2,'ctx'=4] {'core','ctx'}, use_global_device_ids=true, to_apply=%region_8.9 | all-reduce | flops 2048 | bytes 16384 | tf_op jit(solution)/shard_map/psum | solution.py:1007
  503.1 5.1 convolution_convert_fusion.3.refs_0_
  508.2 4.9 convolution_convert_fusion.6.refs_2_
  513.2 81.5 %sum_input.1 = (f32[128,2048]{1,0:T(8,128)S(1)}, f32[64,6144]{1,0:T(8,128)S(1)}, f32[4,16,128]{2,1,0:T(8,128)S(1)}, f32[64,2048]{1,0:T(8,128)S(1)}) custom-call(bf16[1024,2048]{1,0:T(8,128)(2,1)} %convolution_convert_fusion.3.refs_0_, f32[128,2048]{1,0:T(8,128)S(1)} %get-tuple-element.44.refs_1_, bf16[2048,768]{1,0:T(8,128)(2,1)} %convolution_convert_fusion.6.refs_2_, ...), custom_call_target="tpu_custom_call" | custom-call | bytes 209715200 | tf_op jit(solution)/shard_map/sum_input/pallas_call | solution.py:377
  599.9 3.7 join_columns.1
  (159 shorter events, 64.7 us)
Async XLA Ops:
  7.2 139.7 %all-gather.4.cloned.1.call-start = ((), (), s32[]{:S(2)}) async-start(), calls=%async_computation.2 | async-start | bytes 1310720 | tf_op jit(solution)/shard_map/all_gather | solution.py:884
  7.2 1.6 collective-permute-start
  9.6 220.9 %all-gather.6.cloned.1.call-start = ((), (), s32[]{:S(2)}) async-start(), calls=%async_computation.3 | async-start | bytes 10485760 | tf_op jit(solution)/shard_map/all_gather | solution.py:884
  13.3 11.9 %copy-start.29 = (bf16[64,6144]{1,0:T(8,128)(2,1)S(1)}, bf16[64,6144]{1,0:T(8,128)(2,1)}, u32[]{:S(2)}) copy-start(bf16[64,6144]{1,0:T(8,128)(2,1)} %param.11) | copy-start | bytes 2359300
  24.4 224.5 %all-gather.8.cloned.1.call-start = ((), (), s32[]{:S(2)}) async-start(), calls=%async_computation.4 | async-start | bytes 5242880 | tf_op jit(solution)/shard_map/all_gather | solution.py:884
  25.1 572.0 %reduce-scatter.5.cloned.1.call-start = ((), (), s32[]{:S(2)}) async-start(), calls=%async_computation.6 | async-start | bytes 5242880 | tf_op jit(solution)/shard_map/reduce_scatter | solution.py:888
  94.3 6.5 %copy-start.14 = (bf16[2048,768]{1,0:T(8,128)(2,1)}, bf16[2048,768]{1,0:T(8,128)(2,1)S(1)}, u32[]{:S(2)}) copy-start(bf16[2048,768]{1,0:T(8,128)(2,1)S(1)} %get-tuple-element.33) | copy-start | bytes 9437188
  94.3 24.9 %copy-start.13 = (f32[4,2048]{1,0:T(4,128)S(1)}, f32[4,2048]{1,0:T(4,128)}, u32[]{:S(2)}) copy-start(f32[4,2048]{1,0:T(4,128)} %refs_3_.3) | copy-start | bytes 98308
  131.8 2.9 copy-start.21
  137.8 5.9 copy-start.30
  242.9 3.2 copy-start.19
  248.9 9.4 %copy-start.2 = (bf16[1,128,2048]{2,1,0:T(8,128)(2,1)S(1)}, bf16[1,128,2048]{2,1,0:T(8,128)(2,1)}, u32[]{:S(2)}) copy-start(bf16[1,128,2048]{2,1,0:T(8,128)(2,1)} %param.17) | copy-start | bytes 1572868
  258.3 78.0 %copy-start.24 = (bf16[1024,1024]{1,0:T(8,128)(2,1)S(1)}, bf16[1024,1024]{1,0:T(8,128)(2,1)}, u32[]{:S(2)}) copy-start(bf16[1024,1024]{1,0:T(8,128)(2,1)} %multiply_convert_fusion.3) | copy-start | bytes 6291460
  344.7 13.8 %copy-start.37 = (bf16[1024,2048]{1,0:T(8,128)(2,1)S(1)}, bf16[1024,2048]{1,0:T(8,128)(2,1)}, u32[]{:S(2)}) copy-start(bf16[1024,2048]{1,0:T(8,128)(2,1)} %get-tuple-element.35) | copy-start | bytes 12582916
  385.0 212.1 %reduce-scatter.3.cloned.1.call-start = ((), (), s32[]{:S(2)}) async-start(), calls=%async_computation.5 | async-start | bytes 10485760 | tf_op jit(solution)/shard_map/reduce_scatter | solution.py:888
  385.6 80.1 %copy-start.28 = (bf16[256,2048]{1,0:T(8,128)(2,1)S(1)}, bf16[256,2048]{1,0:T(8,128)(2,1)}, u32[]{:S(2)}) copy-start(bf16[256,2048]{1,0:T(8,128)(2,1)} %all-gather.4.cloned.1.call-done) | copy-start | bytes 3145732
  465.7 4.1 copy-start.31
  469.8 3.7 copy-start.20
  481.3 18.5 %copy-start.23 = (bf16[2,512,2,128]{3,2,1,0:T(2,128)(2,1)S(1)}, bf16[2,512,2,128]{3,2,1,0:T(2,128)(2,1)}, u32[]{:S(2)}) copy-start(bf16[2,512,2,128]{3,2,1,0:T(2,128)(2,1)} %copy-done.22) | copy-start | bytes 1572868
  497.3 3.1 copy-start.36
  500.4 2.7 copy-start.32
  503.1 5.1 copy-start.35
  599.9 4.5 copy-start.8
  599.9 6.6 %copy-start.12 = (f32[64,2048]{1,0:T(8,128)S(1)}, f32[64,2048]{1,0:T(8,128)}, u32[]{:S(2)}) copy-start(f32[64,2048]{1,0:T(8,128)} %copy-done.11) | copy-start | bytes 1572868
  (22 other events, 33.0 us)
Sparse Core Ops, SparseCore 0:
  10.4 53.9 all-gather.3
  66.3 89.7 all-gather.5
  157.9 52.6 all-gather.7
  385.1 52.6 reduce-scatter.4
  441.0 96.8 reduce-scatter.2

commit v5 on v4

--- a/solution.py
+++ b/solution.py
@@ -1,3 +1,5 @@
+import functools
+
 import jax
 import jax.numpy as jnp
 from jax import lax
@@ -855,19 +857,6 @@
     return (jnp.concatenate([cosine, cosine], 1), jnp.concatenate([sine, sine], 1))
 
 
-def rotate(values, cosine, sine):
-    half = HEAD_DIM // 2
-    turned = jnp.concatenate([-values[..., half:], values[..., :half]], -1)
-    return values * cosine + turned * sine
-
-
-def rotate_back(values, cosine, sine):
-    half = HEAD_DIM // 2
-    scaled = values * sine
-    turned = jnp.concatenate([scaled[..., half:], -scaled[..., :half]], -1)
-    return values * cosine + turned
-
-
 def dot(left, right):
     return jnp.dot(left, right, preferred_element_type=F32)
 
@@ -886,6 +875,364 @@
 
 def scatter_sum(values, axes):
     return lax.psum_scatter(values, axes, scatter_dimension=0, tiled=True)
+
+
+def turn(values, cosine, sine):
+    return values * cosine + pltpu.roll(values, HEAD_DIM // 2, 1) * sine
+
+
+def member_rows(part):
+    row = lax.broadcasted_iota(jnp.int32, (8, 2 * part), 0)
+    column = lax.broadcasted_iota(jnp.int32, (8, 2 * part), 1)
+    return jnp.where(row == column // part, 1.0, 0.0).astype(F32)
+
+
+def row_sums(pick, values):
+    return lax.dot_general(
+        pick, values, (((1,), (1,)), ((), ())), precision=lax.Precision.HIGHEST, preferred_element_type=F32
+    )
+
+
+def over_columns(pick, sums):
+    return lax.dot_general(
+        sums, pick, (((0,), (0,)), ((), ())), precision=lax.Precision.HIGHEST, preferred_element_type=F32
+    )
+
+
+class Stats:
+    def __init__(self, spans, own, arrived, send, recv):
+        self.spans, self.own, self.arrived, self.send, self.recv = spans, own, arrived, send, recv
+        self.core, self.place = lax.axis_index("core"), lax.axis_index("ctx")
+        self.me = self.core * spans + self.place
+
+    def member(self, s):
+        core, place = step_member(self.core, self.place, s, self.spans)
+        return {"core": core, "ctx": place}
+
+    def greet(self):
+        for s in range(1, 2 * self.spans):
+            pl.semaphore_signal(
+                pltpu.get_barrier_semaphore(), 1, device_id=self.member(s), device_id_type=MESH_ID
+            )
+
+    def meet(self):
+        pl.semaphore_wait(pltpu.get_barrier_semaphore(), 2 * self.spans - 1)
+
+    def copy(self, s):
+        return pltpu.make_async_remote_copy(
+            src_ref=self.own, dst_ref=self.arrived.at[s], send_sem=self.send.at[s], recv_sem=self.recv.at[s],
+            device_id=self.member(s), device_id_type=MESH_ID,
+        )
+
+    def start(self):
+        for s in range(1, 2 * self.spans):
+            self.copy(s).start()
+
+    def total(self):
+        total = self.own[...]
+        for s in range(1, 2 * self.spans):
+            self.copy(s).wait()
+            total = total + self.arrived[s]
+        return total
+
+
+def stats_scratch(spans, total_rows):
+    sems = pltpu.SemaphoreType.DMA((2 * spans,))
+    return [
+        pltpu.VMEM((8, total_rows), F32),
+        pltpu.VMEM((2 * spans, 8, total_rows), F32),
+        sems,
+        sems,
+    ]
+
+
+def allowed_at(ids, seq, block, count, spans):
+    rows = ids.shape[1]
+    per = block // rows
+    ids_of = lambda z: ids[(seq * spans + z) * 8 : (seq * spans + z) * 8 + 8, :].astype(F32)
+    first = count * per
+    keys = jnp.concatenate([ids_of(z)[:1] for z in range(first + per)], 1)
+    queries = jnp.concatenate([jnp.transpose(ids_of(z))[:, :1] for z in range(first, first + per)], 0)
+    shape = (block, (count + 1) * block)
+    query_at = lax.broadcasted_iota(jnp.int32, shape, 0) + count * block
+    key_at = lax.broadcasted_iota(jnp.int32, shape, 1)
+    same = queries == keys
+    seen = jnp.logical_and(same, key_at <= query_at)
+    return jnp.logical_and(seen, jnp.logical_or(keys != 0.0, key_at == query_at))
+
+
+def softmax_parts(query, key, allowed):
+    scores = jnp.where(allowed, dot_rows(query, key) * HEAD_DIM ** (-0.5), -1e30)
+    weights = jnp.exp(scores - jnp.max(scores, axis=1, keepdims=True))
+    return weights / jnp.sum(weights, axis=1, keepdims=True)
+
+
+QUERY_BLOCK = 256
+ROW_TILE = 256
+
+
+def attend_body(
+    spans, tokens, weights, out_w, gains, ids, cosine, sine,
+    partial_out, query_out, key_out, value_out, normed_out, factor_out, attended_out,
+    held, held_w, raw, given, own, arrived, load_sem, store_sem, send, recv,
+):
+    part = out_w.shape[0]
+    total_rows = raw.shape[0]
+    length = total_rows // 2
+    width = tokens.shape[1]
+    tiles = total_rows // ROW_TILE
+    stats = Stats(spans, own, arrived, send, recv)
+    stats.greet()
+
+    def at(i):
+        return pl.ds(pl.multiple_of(i * ROW_TILE, ROW_TILE), ROW_TILE)
+
+    def load_rows(i):
+        return pltpu.make_async_copy(tokens.at[at(i)], held.at[at(i)], load_sem.at[i])
+
+    load_w = pltpu.make_async_copy(weights, held_w, load_sem.at[tiles])
+    load_w.start()
+
+    @pl.loop(0, tiles)
+    def _(i):
+        load_rows(i).start()
+
+    pick = member_rows(part)
+    load_w.wait()
+
+    @pl.loop(0, tiles)
+    def _(i):
+        load_rows(i).wait()
+        values = dot(held[at(i), :], held_w[...])
+        raw[at(i), :] = values
+        both = values[:, : 2 * part]
+        own[:, at(i)] = row_sums(pick, both * both)
+
+    stats.meet()
+    stats.start()
+
+    @pl.loop(0, tiles)
+    def _(i):
+        value_out[at(i), :] = raw[at(i), 2 * part :].astype(BF16)
+
+    factor_out[...] = lax.rsqrt(stats.total() / width + EPS)
+    me = stats.me
+    columns = pl.ds(pl.multiple_of(me * part, part), part)
+    gain = jnp.concatenate([gains[0:1, columns], gains[1:2, columns]], 1)
+
+    @pl.loop(0, tiles)
+    def _(i):
+        normed = raw[at(i), : 2 * part] * over_columns(pick, factor_out[:, at(i)])
+        normed_out[at(i), :] = normed
+        scaled = normed * gain
+        place = pl.ds(pl.multiple_of(lax.rem(i, length // ROW_TILE) * ROW_TILE, ROW_TILE), ROW_TILE)
+        for h in range(part // HEAD_DIM):
+            head = slice(h * HEAD_DIM, (h + 1) * HEAD_DIM)
+            low = slice(part + h * HEAD_DIM, part + (h + 1) * HEAD_DIM)
+            query_out[at(i), head] = turn(scaled[:, head], cosine[place, :], sine[place, :]).astype(BF16)
+            key_out[at(i), head] = turn(scaled[:, low], cosine[place, :], sine[place, :]).astype(BF16)
+
+    block = QUERY_BLOCK
+    for seq in range(2):
+        for count in range(length // block):
+            allowed = allowed_at(ids, seq, block, count, spans)
+            rows = slice(seq * length + count * block, seq * length + (count + 1) * block)
+            keys = slice(seq * length, seq * length + (count + 1) * block)
+            for h in range(part // HEAD_DIM):
+                head = slice(h * HEAD_DIM, (h + 1) * HEAD_DIM)
+                shares = softmax_parts(query_out[rows, head], key_out[keys, head], allowed)
+                attended_out[rows, head] = dot(shares.astype(BF16), value_out[keys, head]).astype(BF16)
+            i = rows.start // ROW_TILE
+            if i >= 2:
+                pltpu.make_async_copy(given.at[i % 2], partial_out.at[at(i - 2)], store_sem.at[i - 2]).wait()
+            given[i % 2] = dot(attended_out[rows, :], out_w[...]).astype(BF16)
+            pltpu.make_async_copy(given.at[i % 2], partial_out.at[at(i)], store_sem.at[i]).start()
+    for i in range(tiles - 2, tiles):
+        pltpu.make_async_copy(given.at[i % 2], partial_out.at[at(i)], store_sem.at[i]).wait()
+
+
+def attend(spans, tokens, weights, out_w, gains, ids, cosine, sine):
+    total_rows, width = tokens.shape
+    part = out_w.shape[0]
+    tiles = total_rows // ROW_TILE
+    vmem = pl.BlockSpec(memory_space=pltpu.VMEM)
+    hbm = pl.BlockSpec(memory_space=pl.ANY)
+    shape = jax.ShapeDtypeStruct
+    return pl.pallas_call(
+        functools.partial(attend_body, spans),
+        out_shape=[
+            shape((total_rows, width), BF16),
+            shape((total_rows, part), BF16),
+            shape((total_rows, part), BF16),
+            shape((total_rows, part), BF16),
+            shape((total_rows, 2 * part), F32),
+            shape((8, total_rows), F32),
+            shape((total_rows, part), BF16),
+        ],
+        in_specs=[hbm, hbm] + [vmem] * 5,
+        out_specs=[hbm] + [vmem] * 6,
+        scratch_shapes=[
+            pltpu.VMEM((total_rows, width), BF16),
+            pltpu.VMEM(weights.shape, BF16),
+            pltpu.VMEM((total_rows, 3 * part), F32),
+            pltpu.VMEM((2, ROW_TILE, width), BF16),
+            *stats_scratch(spans, total_rows)[:2],
+            pltpu.SemaphoreType.DMA((tiles + 1,)),
+            pltpu.SemaphoreType.DMA((tiles,)),
+            *stats_scratch(spans, total_rows)[2:],
+        ],
+        compiler_params=pltpu.CompilerParams(collective_id=8, has_side_effects=True, vmem_limit_bytes=56 << 20),
+        cost_estimate=pl.CostEstimate(flops=2 * total_rows * width * 5 * part, bytes_accessed=0, transcendentals=0),
+        name="attend",
+    )(tokens, weights, out_w, gains, ids, cosine, sine)
+
+
+def attend_back_body(
+    spans, grads, tokens, weights, out_w, gains, ids, cosine, sine,
+    query, key, value, normed, factor, attended,
+    input_out, qkv_out, out_out, gains_out,
+    held, held_tokens, held_w, raw, mixed, attended_grad, given, own, arrived, load_sem, store_sem, send, recv,
+):
+    part = out_w.shape[0]
+    total_rows = raw.shape[0]
+    length = total_rows // 2
+    width = grads.shape[1]
+    tiles = total_rows // ROW_TILE
+    scale = HEAD_DIM ** (-0.5)
+    stats = Stats(spans, own, arrived, send, recv)
+    stats.greet()
+
+    def at(i):
+        return pl.ds(pl.multiple_of(i * ROW_TILE, ROW_TILE), ROW_TILE)
+
+    def load_rows(i):
+        return pltpu.make_async_copy(grads.at[at(i)], held.at[at(i)], load_sem.at[i])
+
+    @pl.loop(0, tiles)
+    def _(i):
+        load_rows(i).start()
+
+    load_w = pltpu.make_async_copy(weights, held_w, load_sem.at[tiles])
+    load_tokens = pltpu.make_async_copy(tokens, held_tokens, load_sem.at[tiles + 1])
+    load_w.start()
+    load_tokens.start()
+    pick = member_rows(part)
+    me = stats.me
+    columns = pl.ds(pl.multiple_of(me * part, part), part)
+    gain = jnp.concatenate([gains[0:1, columns], gains[1:2, columns]], 1)
+
+    @pl.loop(0, tiles)
+    def _(i):
+        load_rows(i).wait()
+        attended_grad[at(i), :] = dot_rows(held[at(i), :], out_w[...]).astype(BF16)
+
+    block = QUERY_BLOCK
+    blocks = length // block
+    for seq in range(2):
+        for h in range(part // HEAD_DIM):
+            head = slice(h * HEAD_DIM, (h + 1) * HEAD_DIM)
+            key_at = slice(part + h * HEAD_DIM, part + (h + 1) * HEAD_DIM)
+            value_at = slice(2 * part + h * HEAD_DIM, 2 * part + (h + 1) * HEAD_DIM)
+            for count in reversed(range(blocks)):
+                allowed = allowed_at(ids, seq, block, count, spans)
+                rows = slice(seq * length + count * block, seq * length + (count + 1) * block)
+                keys = slice(seq * length, seq * length + (count + 1) * block)
+                shares = softmax_parts(query[rows, head], key[keys, head], allowed)
+                share_grad = dot_rows(attended_grad[rows, head], value[keys, head])
+                inner = jnp.sum(shares * share_grad, axis=1, keepdims=True)
+                score_grad = (shares * (share_grad - inner)).astype(BF16)
+                raw[rows, head] = dot(score_grad, key[keys, head]) * scale
+                key_grad = dot_first(score_grad, query[rows, head]) * scale
+                value_grad = dot_first(shares.astype(BF16), attended_grad[rows, head])
+                if count == blocks - 1:
+                    raw[keys, key_at] = key_grad
+                    raw[keys, value_at] = value_grad
+                else:
+                    raw[keys, key_at] += key_grad
+                    raw[keys, value_at] += value_grad
+
+    gains_out[...] = jnp.zeros_like(gains_out)
+
+    @pl.loop(0, tiles)
+    def _(i):
+        place = pl.ds(pl.multiple_of(lax.rem(i, length // ROW_TILE) * ROW_TILE, ROW_TILE), ROW_TILE)
+        for h in range(2 * part // HEAD_DIM):
+            head = slice(h * HEAD_DIM, (h + 1) * HEAD_DIM)
+            raw[at(i), head] = turn(raw[at(i), head], cosine[place, :], -sine[place, :])
+        terms = raw[at(i), : 2 * part] * normed[at(i), :]
+        gains_out[0:1, :] += jnp.sum(terms, axis=0, keepdims=True)
+        own[:, at(i)] = row_sums(pick, terms * gain)
+        mixed[at(i), 2 * part :] = raw[at(i), 2 * part :].astype(BF16)
+
+    stats.meet()
+    stats.start()
+    out_out[...] = dot_first(attended[...], held[...]).astype(BF16)
+    own[...] = stats.total() / width
+
+    @pl.loop(0, tiles)
+    def _(i):
+        mean = over_columns(pick, own[:, at(i)])
+        back = gain * raw[at(i), : 2 * part] - normed[at(i), :] * mean
+        mixed[at(i), : 2 * part] = (over_columns(pick, factor[:, at(i)]) * back).astype(BF16)
+
+    load_w.wait()
+
+    def store(i):
+        return pltpu.make_async_copy(given.at[lax.rem(i, 2)], input_out.at[at(i)], store_sem.at[lax.rem(i, 2)])
+
+    @pl.loop(0, tiles)
+    def _(i):
+        @pl.when(i >= 2)
+        def _():
+            store(i - 2).wait()
+
+        given[lax.rem(i, 2)] = dot_rows(mixed[at(i), :], held_w[...]).astype(BF16)
+        store(i).start()
+
+    load_tokens.wait()
+
+    @pl.loop(0, width // ROW_TILE)
+    def _(i):
+        qkv_out[at(i), :] = dot_first(held_tokens[:, at(i)], mixed[...]).astype(BF16)
+
+    for i in range(tiles - 2, tiles):
+        store(i).wait()
+
+
+def attend_back(spans, grads, tokens, weights, out_w, gains, ids, cosine, sine, saved):
+    total_rows, width = tokens.shape
+    part = out_w.shape[0]
+    tiles = total_rows // ROW_TILE
+    vmem = pl.BlockSpec(memory_space=pltpu.VMEM)
+    hbm = pl.BlockSpec(memory_space=pl.ANY)
+    shape = jax.ShapeDtypeStruct
+    return pl.pallas_call(
+        functools.partial(attend_back_body, spans),
+        out_shape=[
+            shape((total_rows, width), BF16),
+            shape((width, 3 * part), BF16),
+            shape((part, width), BF16),
+            shape((8, 2 * part), F32),
+        ],
+        in_specs=[hbm] * 3 + [vmem] * (5 + len(saved)),
+        out_specs=[hbm] + [vmem] * 3,
+        scratch_shapes=[
+            pltpu.VMEM((total_rows, width), BF16),
+            pltpu.VMEM((total_rows, width), BF16),
+            pltpu.VMEM(weights.shape, BF16),
+            pltpu.VMEM((total_rows, 3 * part), F32),
+            pltpu.VMEM((total_rows, 3 * part), BF16),
+            pltpu.VMEM((total_rows, part), BF16),
+            pltpu.VMEM((2, ROW_TILE, width), BF16),
+            *stats_scratch(spans, total_rows)[:2],
+            pltpu.SemaphoreType.DMA((tiles + 2,)),
+            pltpu.SemaphoreType.DMA((2,)),
+            *stats_scratch(spans, total_rows)[2:],
+        ],
+        compiler_params=pltpu.CompilerParams(collective_id=9, has_side_effects=True, vmem_limit_bytes=58 << 20),
+        cost_estimate=pl.CostEstimate(flops=2 * total_rows * width * 8 * part, bytes_accessed=0, transcendentals=0),
+        name="attend_back",
+    )(grads, tokens, weights, out_w, gains, ids, cosine, sine, *saved)
 
 
 def per_device(inputs, segment, w_qkv, w_out, w_gate, w_up, w_down_t, gains, cotangent):
@@ -894,10 +1241,7 @@
     spans = lax.axis_size("ctx")
     members = cores * spans
     length = rows * spans
-    total_rows = cores * length
     part = width // members
-    heads = part // HEAD_DIM
-    member = lax.axis_index(GROUP)
     tokens = inputs[0]
 
     qkv_rows = w_qkv.shape[0]
@@ -924,41 +1268,12 @@
     gate_up, down = split_columns(w_gate, w_up, w_down_t)
     gate_up_w, down_w = gather(gate_up, "chip"), gather(down, "chip")
 
-    mixed = dot(tokens_all, qkv_w)
-    query_raw = mixed[:, :part]
-    key_raw = mixed[:, part : 2 * part]
-    value_low = mixed[:, 2 * part :].astype(BF16)
-    squares = jnp.stack([jnp.sum(query_raw * query_raw, 1), jnp.sum(key_raw * key_raw, 1)])
-    squares = lax.psum(squares, GROUP)
-    factors = lax.rsqrt(squares / width + EPS)
-    gain_q = lax.dynamic_slice_in_dim(gains[0], member * part, part)
-    gain_k = lax.dynamic_slice_in_dim(gains[1], member * part, part)
-    places = jnp.arange(length, dtype=jnp.int32)
-    cosine, sine = rope_tables(places.astype(F32))
-    cosine, sine = cosine[None, :, None, :], sine[None, :, None, :]
-    shape = (cores, length, heads, HEAD_DIM)
-    query_factor, key_factor = factors[0][:, None], factors[1][:, None]
-    query_low = rotate((query_raw * query_factor * gain_q).reshape(shape), cosine, sine).astype(BF16)
-    key_low = rotate((key_raw * key_factor * gain_k).reshape(shape), cosine, sine).astype(BF16)
-    value_low = value_low.reshape(shape)
-
-    ids = ids.reshape(members, 8, rows)[:, 0].reshape(cores, length)
-    allowed = (
-        (ids[:, :, None] == ids[:, None, :])
-        & (places[None, None, :] <= places[None, :, None])
-        & ((ids[:, None, :] != 0) | (places[None, None, :] == places[None, :, None]))
-    )[:, None]
-    scale = HEAD_DIM ** (-0.5)
-    scores = jnp.einsum("bqhd,bkhd->bhqk", query_low, key_low, preferred_element_type=F32) * scale
-    masked = jnp.where(allowed, scores, -1e30)
-    row_max = jnp.max(masked, axis=-1, keepdims=True)
-    weights = jnp.where(allowed, jnp.exp(masked - row_max), 0.0)
-    shares = weights / jnp.sum(weights, axis=-1, keepdims=True)
-    shares_low = shares.astype(BF16)
-    attended = jnp.einsum("bhqk,bkhd->bqhd", shares_low, value_low, preferred_element_type=F32)
-    attended_low = attended.reshape(total_rows, part).astype(BF16)
+    cosine, sine = rope_tables(jnp.arange(length, dtype=F32))
+    half = jnp.arange(HEAD_DIM) < HEAD_DIM // 2
+    sine = jnp.where(half[None, :], -sine, sine)
+    out_part, *saved = attend(spans, tokens_all, qkv_w, out_w, gains, ids, cosine, sine)
     residual, projected, residual_all = spread(True, after_projected, 2, 2, None).call(
-        "sum_projected", 2, dot(attended_low, out_w).astype(BF16), [tokens, gains], [own, own]
+        "sum_projected", 2, out_part, [tokens, gains], [own, own]
     )
 
     gate_up_out = dot(residual_all, gate_up_w)
@@ -990,29 +1305,10 @@
         [own, one],
     )
 
-    attended_grad = dot_rows(projected_all, out_w).astype(BF16).reshape(shape)
-
-    share_grad = jnp.einsum("bqhd,bkhd->bhqk", attended_grad, value_low, preferred_element_type=F32)
-    inner = jnp.sum(shares * share_grad, axis=-1, keepdims=True)
-    score_grad = (shares * (share_grad - inner)).astype(BF16)
-    query_grad = jnp.einsum("bhqk,bkhd->bqhd", score_grad, key_low, preferred_element_type=F32)
-    key_grad = jnp.einsum("bhqk,bqhd->bkhd", score_grad, query_low, preferred_element_type=F32)
-    value_grad = jnp.einsum("bhqk,bqhd->bkhd", shares_low, attended_grad, preferred_element_type=F32)
-    query_turn = rotate_back(query_grad * scale, cosine, sine).reshape(total_rows, part)
-    key_turn = rotate_back(key_grad * scale, cosine, sine).reshape(total_rows, part)
-    query_norm, key_norm = query_raw * query_factor, key_raw * key_factor
-    sums = jnp.stack(
-        [jnp.sum(gain_q * query_turn * query_norm, 1), jnp.sum(gain_k * key_turn * key_norm, 1)]
+    input_part, qkv_part, out_grads, gain_sums = attend_back(
+        spans, projected_all, tokens_all, qkv_w, out_w, gains, ids, cosine, sine, saved
     )
-    means = lax.psum(sums, GROUP) / width
-    query_mixed = query_factor * (gain_q * query_turn - query_norm * means[0][:, None])
-    key_mixed = key_factor * (gain_k * key_turn - key_norm * means[1][:, None])
-    gain_query = jnp.sum(query_turn * query_norm, 0)
-    gain_key = jnp.sum(key_turn * key_norm, 0)
-    mixed_grad = jnp.concatenate(
-        [query_mixed, key_mixed, value_grad.reshape(total_rows, part)], 1
-    ).astype(BF16)
-    input_part = dot_rows(mixed_grad, qkv_w).astype(BF16)
+    gain_query, gain_key = gain_sums[0, :part], gain_sums[0, part:]
     sums = jnp.concatenate(
         [a.reshape(-1, 128) for a in (gain_attn, gain_feed, gain_query, gain_key)]
         + [jnp.zeros((-2 * part // 128 % 8, 128), F32)]
@@ -1020,8 +1316,7 @@
     input_grad, grad_qkv, grad_gains, grad_out = Exchange(
         spans, rows, width, PIECE, True, False, after_input, 1, 1, None,
         QkvGrads(
-            spans, chips, members, dot_first(tokens_all, mixed_grad).astype(BF16), sums,
-            dot_first(attended_low, projected_all).astype(BF16),
+            spans, chips, members, qkv_part, sums, out_grads,
         ),
     ).call("sum_input", 5, input_part, [residual_grad], [own])
 

time: 624 us -> 597 us (0.957)
  Pallas kernels: 399 us -> 466 us
  matrix products: 108 us -> 69.2 us
  blocking collectives: 32 us -> 0 us
  local copies, waits for them, and re-layouts: 44.8 us -> 25.9 us
  other arithmetic: 16.6 us -> 8.11 us
    pallas_call x0 -> x2, Pallas kernels: none -> 60.8 us  [the longest x1 34.7 us: attend_back(): pl.pallas_call(functools.partial(attend_back_body, spans), out_shape=[sha...]
    psum x2 -> x0, blocking collectives: 32 us -> none  [the longest x1 16.7 us: per_device(): squares = lax.psum(squares, GROUP)]
    dot_general x4 -> x2, matrix products: 32.5 us -> 22.8 us  [dot_rows(): lax.dot_general(left, right, (((1,), (1,)), ((), ())), preferred_element_...]
    reshape x8 -> x0, local copies, waits for them, and re-layouts: 9.04 us -> none  [the longest x2 3.27 us: per_device(): (query_raw * query_factor * gain_q).reshape(shape)]
    dot_general x4 -> x2, matrix products: 35.1 us -> 26.3 us  [dot(): return jnp.dot(left, right, preferred_element_type=F32)]
    dot_general x5 -> x0, matrix products: 8.21 us -> none  [the longest x1 3.31 us: per_device(): jnp.einsum('bqhd,bkhd->bhqk', attended_grad, value_low, preferred_element...]
    unnamed x92 -> x55, local copies, waits for them, and re-layouts: 30.4 us -> 23.8 us
    pallas_call x5, Pallas kernels: 384 us -> 390 us  [call(): pl.pallas_call(self.body, out_shape=shapes, in_specs=in_specs, out_specs=...]
  transfers between devices with their start and end apart: 6 -> 6, of which waited for: 0 -> 0; matrix products, arithmetic and copies ran while one was open for 14% -> 4% of each run, Pallas kernels for 51% -> 65%
where the time goes in v5:
time: 597 us; the launch traced here: 587 us
  Pallas kernels  466 us (78%)
  matrix products  69.2 us (12%)
  local copies, waits for them, and re-layouts  25.9 us (4%)
  between operations  14.5 us (2%)
  other arithmetic  8.11 us (1%)
    pallas_call x5, Pallas kernels, call(): pl.pallas_call(self.body, out_shape=shapes, in_specs=in_specs, out_specs=...  390 us
    pallas_call x1, Pallas kernels, attend_back(): pl.pallas_call(functools.partial(attend_back_body, spans), out_shape=[sha...  34.7 us
    dot_general x2, matrix products, dot(): return jnp.dot(left, right, preferred_element_type=F32)  26.3 us
    pallas_call x1, Pallas kernels, attend(): pl.pallas_call(functools.partial(attend_body, spans), out_shape=[shape((t...  26.1 us
    unnamed x55, local copies, waits for them, and re-layouts  23.8 us
    dot_general x2, matrix products, dot_rows(): lax.dot_general(left, right, (((1,), (1,)), ((), ())), preferred_element_...  22.8 us
    dot_general x2, matrix products, dot_first(): lax.dot_general(left, right, (((0,), (0,)), ((), ())), preferred_element_...  20.2 us
  transfers between devices with their start and end apart: 6, of which 0 were waited for; matrix products, arithmetic and copies ran while one was open for 4% of the time, Pallas kernels for 65%

profile of v5, /device:TPU:0, one launch (start us, length us, event | category | flops | bytes accessed | tf_op | source)
XLA Modules:
  0.0 586.7 jit_solution(6741888462340815678)
XLA Ops:
  7.2 1.6 collective-permute-start
  13.3 11.1 %split_columns.1 = (bf16[512,2048]{1,0:T(8,128)(2,1)}, bf16[512,1024]{1,0:T(8,128)(2,1)}) custom-call(bf16[256,2048]{1,0:T(8,128)(2,1)S(1)} %copy-done.3, bf16[256,2048]{1,0:T(8,128)(2,1)S(1)} %copy-done.4, bf16[256,2048]{1,0:T(8,128)(2,1)S(1)} %copy-done.5), custom_call_target="tpu_custom_call" | custom-call | tf_op jit(solution)/shard_map/split_columns/pallas_call | solution.py:491
  26.7 67.5 %gather_tokens.1 = (bf16[2048,768]{1,0:T(8,128)(2,1)S(1)}, s32[64,128]{1,0:T(8,128)S(1)}, bf16[1024,2048]{1,0:T(8,128)(2,1)}) custom-call(bf16[128,2048]{1,0:T(8,128)(2,1)S(1)} %bitcast.29, bf16[8,64,768]{2,1,0:T(8,128)(2,1)S(1)} %reshape.42.refs_1_, s32[8,128]{1,0:T(8,128)S(1)} %broadcast_in_dim.28.refs_2_), custom_call_target="tpu_custom_call" | custom-call | bytes 125829120 | tf_op jit(solution)/shard_map/gather_tokens/pallas_call | solution.py:379
  94.2 1.6 copy-done.15
  98.4 26.1 %attend.1 = (bf16[1024,2048]{1,0:T(8,128)(2,1)}, bf16[1024,256]{1,0:T(8,128)(2,1)}, bf16[1024,256]{1,0:T(8,128)(2,1)}, bf16[1024,256]{1,0:T(8,128)(2,1)}, f32[10...) custom-call(bf16[1024,2048]{1,0:T(8,128)(2,1)} %get-tuple-element.43.tokens, ...), custom_call_target="tpu_custom_call" | custom-call | flops 5368709120 | tf_op jit(solution)/shard_map/attend/pallas_call | solution.py:1061
  124.5 80.2 %sum_projected.1 = (f32[128,2048]{1,0:T(8,128)S(1)}, f32[128,2048]{1,0:T(8,128)S(1)}, bf16[1024,2048]{1,0:T(8,128)(2,1)}) custom-call(bf16[1024,2048]{1,0:T(8,128)(2,1)} %get-tuple-element.46.refs_0_, bf16[128,2048]{1,0:T(8,128)(2,1)S(1)} %bitcast.30, f32[4,2048]{1,0:T(4,128)S(1)} %copy-done.14), custom_call_target="tpu_custom_call" | custom-call | bytes 209715200 | tf_op jit(solution)/shard_map/sum_projected/pallas_call | solution.py:379
  205.7 14.5 %fusion.6 = f32[1024,2048]{1,0:T(8,128)} fusion(bf16[1024,2048]{1,0:T(8,128)(2,1)} %get-tuple-element.47, bf16[2048,2048]{1,0:T(8,128)(2,1)} %all-gather.6.cloned.1.call-done), kind=kOutput, calls=%fused_computation.22 | convolution fusion | flops 8589934592 | bytes 20971520 | tf_op jit(solution)/shard_map/dot_general | solution.py:861
  220.3 6.1 %multiply_convert_fusion.2 = bf16[1024,1024]{1,0:T(8,128)(2,1)} fusion(f32[1024,2048]{1,0:T(8,128)} %fusion.6), kind=kLoop, calls=%fused_computation.4 | loop fusion | flops 6291456 | bytes 10485760 | tf_op jit(solution)/shard_map/convert_element_type | solution.py:1282
  226.4 9.4 %convolution_convert_fusion.3.refs_0_ = bf16[1024,2048]{1,0:T(8,128)(2,1)} fusion(bf16[1024,1024]{1,0:T(8,128)(2,1)} %multiply_convert_fusion.2, bf16[2048,1024]{1,0:T(8,128)(2,1)} %all-gather.8.cloned.1.call-done), kind=kOutput, calls=%fused_computation.9 | convolution fusion | flops 4297064448 | bytes 10485760 | tf_op jit(solution)/shard_map/dot_general | solution.py:865
  235.8 77.9 %sum_feed.1 = (bf16[128,2048]{1,0:T(8,128)(2,1)S(1)}, f32[1,2048]{1,0:T(1,128)S(1)}, bf16[1024,2048]{1,0:T(8,128)(2,1)}) custom-call(bf16[1024,2048]{1,0:T(8,128)(2,1)} %convolution_convert_fusion.3.refs_0_, f32[128,2048]{1,0:T(8,128)S(1)} %get-tuple-element.50.refs_1_, bf16[128,2048]{1,0:T(8,128)(2,1)S(1)} %bitcast.31, f32[4,2048]{1,0:T(4,128)S(1)} %copy-done.14), custom_call_target="tpu_custom_call" | custom-call | bytes 209715200 | tf_op jit(solution)/shard_map/sum_feed/pallas_call | solution.py:379
  313.8 8.4 %convolution_convert_fusion.2 = bf16[2048,1024]{1,0:T(8,128)(2,1)} fusion(bf16[1024,2048]{1,0:T(8,128)(2,1)} %get-tuple-element.52, bf16[1024,1024]{1,0:T(8,128)(2,1)S(1)} %copy-done.17), kind=kOutput, calls=%fused_computation.8 | convolution fusion | flops 4297064448 | bytes 10485760 | tf_op jit(solution)/shard_map/dot_general | solution.py:869
  322.2 11.7 %multiply_convert_fusion.1 = (bf16[1024,1024]{1,0:T(8,128)(2,1)S(1)}, bf16[1024,1024]{1,0:T(8,128)(2,1)S(1)}) fusion(f32[1024,2048]{1,0:T(8,128)} %fusion.6, bf16[1024,2048]{1,0:T(8,128)(2,1)} %get-tuple-element.52, bf16[2048,1024]{1,0:T(8,128)(2,1)} %all-gather.8.cloned.1.call-done), kind=kOutput, calls=%fused_computation.3 | convolution fusion | flops 4308598784 | bytes 20971520 | tf_op jit(solution)/shard_map/dot_general | solution.py:861
  333.9 1.3 copy-done.22
  335.2 11.8 %convolution_convert_fusion = bf16[2048,2048]{1,0:T(8,128)(2,1)} fusion(bf16[1024,2048]{1,0:T(8,128)(2,1)S(1)} %copy-done.21, bf16[1024,1024]{1,0:T(8,128)(2,1)S(1)} %get-tuple-element.79, bf16[1024,1024]{1,0:T(8,128)(2,1)S(1)} %get-tuple-element.78), kind=kOutput, calls=%fused_computation | convolution fusion | flops 8602517504 | bytes 16777216 | tf_op jit(solution)/shard_map/dot_general | solution.py:869
  347.0 13.3 %convolution_convert_fusion.1.refs_0_ = bf16[1024,2048]{1,0:T(8,128)(2,1)} fusion(bf16[2048,2048]{1,0:T(8,128)(2,1)} %all-gather.6.cloned.1.call-done, bf16[1024,1024]{1,0:T(8,128)(2,1)} %copy-done.22, bf16[1024,1024]{1,0:T(8,128)(2,1)S(1)} %get-tuple-element.78), kind=kOutput, calls=%fused_computation.7 | convolution fusion | flops 8600420352 | bytes 16777216 | tf_op jit(solution)/shard_map/dot_general | solution.py:865
  361.6 79.7 %sum_back.1 = (f32[128,2048]{1,0:T(8,128)S(1)}, f32[1,2048]{1,0:T(1,128)S(1)}, bf16[1024,2048]{1,0:T(8,128)(2,1)}) custom-call(bf16[1024,2048]{1,0:T(8,128)(2,1)} %convolution_convert_fusion.1.refs_0_, f32[128,2048]{1,0:T(8,128)S(1)} %copy-done.11, bf16[128,2048]{1,0:T(8,128)(2,1)S(1)} %bitcast.32, f32[4,2048]{1,0:T(4,128)S(1)} %copy-done.14), custom_call_target="tpu_custom_call" | custom-call | bytes 209715200 | tf_op jit(solution)/shard_map/sum_back/pallas_call | solution.py:379
  441.3 34.7 %attend_back.1 = (bf16[1024,2048]{1,0:T(8,128)(2,1)}, bf16[2048,768]{1,0:T(8,128)(2,1)}, bf16[256,2048]{1,0:T(8,128)(2,1)}, f32[8,512]{1,0:T(8,128)}) custom-call(bf16[1024,2048]{1,0:T(8,128)(2,1)} %get-tuple-element.55.grads, bf16[1024,2048]{1,0:T(8,128)(2,1)} %get-tuple-element.43.tokens, bf16[2048,768]{1,0:T(8,128)(2,1)} %copy-done.15, ...), custom_call_target="tpu_custom_call" | custom-call | flops 8589934592 | tf_op jit(solution)/shard_map/attend_back/pallas_call | solution.py:1209
  476.8 1.3 copy-done.7
  478.1 85.0 %sum_input.1 = (f32[128,2048]{1,0:T(8,128)S(1)}, f32[64,6144]{1,0:T(8,128)S(1)}, f32[4,16,128]{2,1,0:T(8,128)S(1)}, f32[64,2048]{1,0:T(8,128)S(1)}) custom-call(bf16[1024,2048]{1,0:T(8,128)(2,1)} %get-tuple-element.62.refs_0_, f32[128,2048]{1,0:T(8,128)S(1)} %get-tuple-element.63.refs_1_, bf16[2048,768]{1,0:T(8,128)(2,1)} %get-tuple-element.64.refs_2_, ...), custom_call_target="tpu_custom_call" | custom-call | bytes 209715200 | tf_op jit(solution)/shard_map/sum_input/pallas_call | solution.py:379
  565.5 1.6 copy-done.1
  568.3 3.7 join_columns.1
  575.7 1.3 copy.41
  577.1 1.3 copy.42
  578.4 1.3 copy.43
  (74 shorter events, 19.7 us)
Async XLA Ops:
  7.2 91.3 %all-gather.4.cloned.1.call-start = ((), (), s32[]{:S(2)}) async-start(), calls=%async_computation.2 | async-start | bytes 1310720 | tf_op jit(solution)/shard_map/all_gather | solution.py:873
  7.2 1.6 collective-permute-start
  9.6 196.2 %all-gather.6.cloned.1.call-start = ((), (), s32[]{:S(2)}) async-start(), calls=%async_computation.3 | async-start | bytes 10485760 | tf_op jit(solution)/shard_map/all_gather | solution.py:873
  9.6 1.2 copy-start.3
  10.8 1.2 copy-start.4
  12.1 1.2 copy-start.5
  13.3 11.9 %copy-start.18 = (bf16[64,6144]{1,0:T(8,128)(2,1)S(1)}, bf16[64,6144]{1,0:T(8,128)(2,1)}, u32[]{:S(2)}) copy-start(bf16[64,6144]{1,0:T(8,128)(2,1)} %param.11) | copy-start | bytes 2359300
  24.3 2.4 copy-start.20
  24.4 2.4 copy-start
  24.4 202.0 %all-gather.8.cloned.1.call-start = ((), (), s32[]{:S(2)}) async-start(), calls=%async_computation.4 | async-start | bytes 5242880 | tf_op jit(solution)/shard_map/all_gather | solution.py:873
  25.1 540.4 %reduce-scatter.5.cloned.1.call-start = ((), (), s32[]{:S(2)}) async-start(), calls=%async_computation.6 | async-start | bytes 5242880 | tf_op jit(solution)/shard_map/reduce_scatter | solution.py:877
  94.2 1.6 copy-start.15
  98.4 26.1 %copy-start.14 = (f32[4,2048]{1,0:T(4,128)S(1)}, f32[4,2048]{1,0:T(4,128)}, u32[]{:S(2)}) copy-start(f32[4,2048]{1,0:T(4,128)} %gains.3) | copy-start | bytes 98308
  226.4 9.4 %copy-start.2 = (bf16[1,128,2048]{2,1,0:T(8,128)(2,1)S(1)}, bf16[1,128,2048]{2,1,0:T(8,128)(2,1)}, u32[]{:S(2)}) copy-start(bf16[1,128,2048]{2,1,0:T(8,128)(2,1)} %param.17) | copy-start | bytes 1572868
  235.8 77.9 %copy-start.17 = (bf16[1024,1024]{1,0:T(8,128)(2,1)S(1)}, bf16[1024,1024]{1,0:T(8,128)(2,1)}, u32[]{:S(2)}) copy-start(bf16[1024,1024]{1,0:T(8,128)(2,1)} %multiply_convert_fusion.2) | copy-start | bytes 6291460
  322.1 13.1 %copy-start.21 = (bf16[1024,2048]{1,0:T(8,128)(2,1)S(1)}, bf16[1024,2048]{1,0:T(8,128)(2,1)}, u32[]{:S(2)}) copy-start(bf16[1024,2048]{1,0:T(8,128)(2,1)} %get-tuple-element.47) | copy-start | bytes 12582916
  333.9 1.3 copy-start.22
  360.4 1.2 copy-start.11
  360.4 205.1 %reduce-scatter.3.cloned.1.call-start = ((), (), s32[]{:S(2)}) async-start(), calls=%async_computation.5 | async-start | bytes 10485760 | tf_op jit(solution)/shard_map/reduce_scatter | solution.py:877
  476.8 1.3 copy-start.7
  565.5 1.6 copy-start.1
  567.1 1.2 copy-start.6
  568.3 4.5 copy-start.9
  568.3 6.6 %copy-start.13 = (f32[64,2048]{1,0:T(8,128)S(1)}, f32[64,2048]{1,0:T(8,128)}, u32[]{:S(2)}) copy-start(f32[64,2048]{1,0:T(8,128)} %copy-done.12) | copy-start | bytes 1572868
  (5 other events, 4.1 us)
Sparse Core Ops, SparseCore 0:
  10.4 53.9 all-gather.3
  66.3 89.7 all-gather.5
  157.9 52.6 all-gather.7
  360.5 52.4 reduce-scatter.4
  416.2 111.6 reduce-scatter.2

commit v6 on v5

--- a/solution.py
+++ b/solution.py
@@ -877,6 +877,412 @@
     return lax.psum_scatter(values, axes, scatter_dimension=0, tiled=True)
 
 
+FF_TILE = 512
+SUM_TILE = 1024
+BATCH_PIECE = 16
+
+
+class Middle:
+    def __init__(self, spans, rows, width, hidden, piece):
+        self.spans, self.rows, self.width, self.hidden, self.piece = spans, rows, width, hidden, piece
+        self.count = rows // piece
+        self.block = spans * piece
+        self.batch = 2 * self.block
+
+    def body(
+        self, chips, partial, tokens, cotangent, gains, gate_up_w, down,
+        output, residual_grad, gain_feed, gain_attn, residual_all, feed_grad_all, gate_up_grad, activated, projected_all,
+        residual, projected, own, near, from_left, from_right, held, wide, act, back, up_weights, down_weights,
+        load_sem, weight_sem, store_sem, act_sem, near_send, near_recv, right_send, right_recv, left_send, left_recv,
+        fwd_send, fwd_recv, bwd_send, bwd_recv, side_send, side_recv, down_send, down_recv,
+    ):
+        spans, rows, piece, count = self.spans, self.rows, self.piece, self.count
+        width, hidden, block, batch = self.width, self.hidden, self.block, self.batch
+        core = lax.axis_index("core")
+        place = lax.axis_index("ctx")
+        other = 1 - core
+        last = spans - 1
+        has_left = place > 0
+        has_right = place < last
+
+        def turn_of(o):
+            return jnp.maximum(o, last - o)
+
+        def at(d, k):
+            return pl.ds(pl.multiple_of((k * spans + d) * piece, piece), piece)
+
+        def at_seq(seq, d, k):
+            return pl.ds(pl.multiple_of(((k * 2 + seq) * spans + d) * piece, piece), piece)
+
+        def batch_at(k):
+            return pl.ds(pl.multiple_of(k * batch, batch), batch)
+
+        def natural(seq, d, k):
+            return pl.ds(pl.multiple_of((seq * spans + d) * rows + k * piece, piece), piece)
+
+        def remote(src, dst, send, recv, **device):
+            return pltpu.make_async_remote_copy(
+                src_ref=src, dst_ref=dst, send_sem=send, recv_sem=recv, device_id=device, device_id_type=MESH_ID
+            )
+
+        barrier = pltpu.get_barrier_semaphore()
+        pl.semaphore_signal(barrier, 1, device_id={"core": other}, device_id_type=MESH_ID)
+
+        @pl.when(has_left)
+        def _():
+            pl.semaphore_signal(barrier, 1, device_id={"ctx": place - 1}, device_id_type=MESH_ID)
+
+        @pl.when(has_right)
+        def _():
+            pl.semaphore_signal(barrier, 1, device_id={"ctx": place + 1}, device_id_type=MESH_ID)
+
+        def near_copy(e, d, k):
+            src = partial.at[natural(other, d, k)] if e == 0 else own.at[at_seq(other, d, k)]
+            return remote(src, near.at[at(d, k)], near_send.at[d, k], near_recv.at[d, k], core=other)
+
+        def right_copy(d, k):
+            return remote(
+                own.at[at_seq(core, d, k)], from_left.at[at(d, k)], right_send.at[d, k], right_recv.at[d, k],
+                ctx=place + 1,
+            )
+
+        def left_copy(d, k):
+            return remote(
+                own.at[at_seq(core, d, k)], from_right.at[at(d, k)], left_send.at[d, k], left_recv.at[d, k],
+                ctx=place - 1,
+            )
+
+        def spread_copy(o, k, send, recv, **device):
+            where = held.at[at_seq(core, o, k)]
+            return remote(where, where, send.at[o, k], recv.at[o, k], **device)
+
+        def fwd_copy(o, k):
+            return spread_copy(o, k, fwd_send, fwd_recv, ctx=place + 1)
+
+        def bwd_copy(o, k):
+            return spread_copy(o, k, bwd_send, bwd_recv, ctx=place - 1)
+
+        def side_copy(o, k):
+            return spread_copy(o, k, side_send, side_recv, core=other)
+
+        def load_own(d, k):
+            return pltpu.make_async_copy(
+                partial.at[natural(core, d, k)], own.at[at_seq(core, d, k)], load_sem.at[d, k]
+            )
+
+        @pl.loop(0, count)
+        def _(k):
+            for d in range(spans):
+                load_own(d, k).start()
+
+        load_up = pltpu.make_async_copy(gate_up_w, up_weights, weight_sem.at[0])
+        chip = lax.axis_index("chip")
+        shard = down.shape[0]
+        here = pl.ds(pl.multiple_of(chip * shard, shard), shard)
+        load_down = pltpu.make_async_copy(down, down_weights.at[here], weight_sem.at[1])
+
+        def down_copy(s):
+            return remote(
+                down, down_weights.at[here], down_send.at[s], down_recv.at[s], chip=lax.rem(chip + s, chips)
+            )
+
+        load_up.start()
+        load_down.start()
+        gain_feed[...] = jnp.zeros_like(gain_feed)
+        gain_attn[...] = jnp.zeros_like(gain_attn)
+        for s in range(1, chips):
+            pl.semaphore_signal(
+                barrier, 1, device_id={"chip": lax.rem(chip + s, chips)}, device_id_type=MESH_ID
+            )
+        pl.semaphore_wait(barrier, chips + has_left.astype(jnp.int32) + has_right.astype(jnp.int32))
+        for s in range(1, chips):
+            down_copy(s).start()
+
+        @pl.loop(0, count)
+        def _(k):
+            for d in range(spans):
+                near_copy(0, d, k).start()
+
+        def base(e, d, k):
+            near_copy(e, d, k).wait_recv()
+            if e == 0:
+                load_own(d, k).wait()
+            return own[at_seq(core, d, k), :].astype(F32) + near[at(d, k), :].astype(F32)
+
+        def pass_on(e, d, k, arrived, copy, later):
+            value = base(e, d, k)
+
+            @pl.when(later)
+            def _():
+                copy(d, k).wait_recv()
+
+            before = arrived[at(d, k), :].astype(F32)
+            value = value + jnp.where(later, before, jnp.zeros_like(before))
+            own[at_seq(core, d, k), :] = value.astype(BF16)
+            copy(d, k).start()
+
+        def pass_right(e, k):
+            for d in range(last, 0, -1):
+
+                @pl.when(d > place)
+                def _():
+                    pass_on(e, d, k, from_left, right_copy, has_left)
+
+        def pass_left(e, k):
+            for d in range(last):
+
+                @pl.when(d < place)
+                def _():
+                    pass_on(e, d, k, from_right, left_copy, has_right)
+
+        def finish(e, k):
+            total = base(e, place, k)
+
+            @pl.when(has_left)
+            def _():
+                right_copy(place, k).wait_recv()
+
+            @pl.when(has_right)
+            def _():
+                left_copy(place, k).wait_recv()
+
+            zero = jnp.zeros_like(total)
+            total = total + jnp.where(has_left, from_left[at(place, k), :].astype(F32), zero)
+            total = total + jnp.where(has_right, from_right[at(place, k), :].astype(F32), zero)
+            mine = pl.ds(pl.multiple_of(k * piece, piece), piece)
+            if e == 0:
+                result = after_projected(total, (tokens, gains), (residual, projected), mine)
+            elif e == 1:
+                result = after_feed(total, (residual, cotangent, gains), (output, gain_feed), mine)
+            else:
+                result = after_back(total, (projected, cotangent, gains), (residual_grad, gain_attn), mine)
+            held[at_seq(core, place, k), :] = result.astype(BF16)
+
+            @pl.when(has_right)
+            def _():
+                fwd_copy(place, k).start()
+
+            @pl.when(has_left)
+            def _():
+                bwd_copy(place, k).start()
+
+            side_copy(place, k).start()
+
+        def relay_right(o, k):
+            fwd_copy(o, k).wait_recv()
+
+            @pl.when(has_right)
+            def _():
+                fwd_copy(o, k).start()
+
+            side_copy(o, k).start()
+
+        def relay_left(o, k):
+            bwd_copy(o, k).wait_recv()
+
+            @pl.when(has_left)
+            def _():
+                bwd_copy(o, k).start()
+
+            side_copy(o, k).start()
+
+        def gathered(k):
+            for o in range(spans):
+                side_copy(o, k).wait_recv()
+
+        def sums_sent(e, k):
+            for d in range(spans):
+                near_copy(e, d, k).wait_send()
+
+                @pl.when(d > place)
+                def _():
+                    right_copy(d, k).wait_send()
+
+                @pl.when(d < place)
+                def _():
+                    left_copy(d, k).wait_send()
+
+        def spread_sent(k):
+            for o in range(spans):
+                side_copy(o, k).wait_send()
+
+                @pl.when(jnp.logical_and(o <= place, has_right))
+                def _():
+                    fwd_copy(o, k).wait_send()
+
+                @pl.when(jnp.logical_and(o >= place, has_left))
+                def _():
+                    bwd_copy(o, k).wait_send()
+
+        def store(src, dst, k, sem):
+            return pltpu.make_async_copy(src, dst.at[batch_at(k)], sem)
+
+        def forward(k):
+            @pl.when(k == 0)
+            def _():
+                load_up.wait()
+                load_down.wait()
+                for s in range(1, chips):
+                    down_copy(s).wait()
+
+            gathered(k)
+            keep = store(held.at[batch_at(k)], residual_all, k, store_sem.at[0])
+            keep.start()
+
+            @pl.loop(0, hidden // FF_TILE)
+            def _(n):
+                low = pl.ds(pl.multiple_of(n * FF_TILE, FF_TILE), FF_TILE)
+                high = pl.ds(pl.multiple_of(hidden + n * FF_TILE, FF_TILE), FF_TILE)
+                gate = dot(held[batch_at(k), :], up_weights[:, low])
+                up = dot(held[batch_at(k), :], up_weights[:, high])
+                wide[batch_at(k), low] = gate
+                wide[batch_at(k), high] = up
+                act[:, low] = (gate * (1.0 / (1.0 + jnp.exp(-gate))) * up).astype(BF16)
+
+            keep_act = store(act, activated, k, act_sem.at[0])
+            keep_act.start()
+            sums_sent(0, k)
+
+            @pl.loop(0, width // SUM_TILE)
+            def _(n):
+                columns = pl.ds(pl.multiple_of(n * SUM_TILE, SUM_TILE), SUM_TILE)
+                own[batch_at(k), columns] = dot_rows(act[...], down_weights[columns, :]).astype(BF16)
+
+            keep_act.wait()
+            keep.wait()
+            spread_sent(k)
+            for d in range(spans):
+                near_copy(1, d, k).start()
+
+        def backward(k):
+            gathered(k)
+            keep = store(held.at[batch_at(k)], feed_grad_all, k, store_sem.at[0])
+            keep.start()
+
+            @pl.loop(0, hidden // FF_TILE)
+            def _(n):
+                low = pl.ds(pl.multiple_of(n * FF_TILE, FF_TILE), FF_TILE)
+                high = pl.ds(pl.multiple_of(hidden + n * FF_TILE, FF_TILE), FF_TILE)
+                act_grad = dot(held[batch_at(k), :], down_weights[:, low])
+                gate = wide[batch_at(k), low]
+                up = wide[batch_at(k), high]
+                sigmoid = 1.0 / (1.0 + jnp.exp(-gate))
+                back[:, low] = (act_grad * up * sigmoid * (1.0 + gate * (1.0 - sigmoid))).astype(BF16)
+                back[:, high] = (act_grad * (gate * sigmoid)).astype(BF16)
+
+            keep_back = store(back, gate_up_grad, k, act_sem.at[1])
+            keep_back.start()
+            sums_sent(1, k)
+
+            @pl.loop(0, width // SUM_TILE)
+            def _(n):
+                columns = pl.ds(pl.multiple_of(n * SUM_TILE, SUM_TILE), SUM_TILE)
+                own[batch_at(k), columns] = dot_rows(back[...], up_weights[columns, :]).astype(BF16)
+
+            keep_back.wait()
+            keep.wait()
+            spread_sent(k)
+            for d in range(spans):
+                near_copy(2, d, k).start()
+
+        def give(seq, d, k):
+            return pltpu.make_async_copy(
+                held.at[at_seq(seq, d, k)], projected_all.at[natural(seq, d, k)], load_sem.at[d, k]
+            )
+
+        def hand_out(k):
+            gathered(k)
+            sums_sent(2, k)
+            for seq in range(2):
+                for d in range(spans):
+                    give(seq, d, k).start()
+                for d in range(spans):
+                    give(seq, d, k).wait()
+            spread_sent(k)
+
+        step = 2 * last + 2
+
+        def due(t, run):
+            @pl.when(jnp.logical_and(t >= 0, t < count))
+            def _():
+                run(t)
+
+        @pl.loop(0, 3 * step + count - 1)
+        def _(t):
+            for e in range(2, -1, -1):
+                now = t - e * step
+                for j in range(1, spans):
+                    o = place - j
+
+                    @pl.when(o >= 0)
+                    def _():
+                        due(now - turn_of(o) - j, functools.partial(relay_right, o))
+
+                    p = place + j
+
+                    @pl.when(p < spans)
+                    def _():
+                        due(now - turn_of(p) - j, functools.partial(relay_left, p))
+
+                due(now - place, functools.partial(pass_right, e))
+                due(now - (last - place), functools.partial(pass_left, e))
+                due(now - turn_of(place), functools.partial(finish, e))
+            for e, run in ((2, hand_out), (1, backward), (0, forward)):
+                due(t - e * step - 2 * last, run)
+
+    def call(self, chips, partial, tokens, cotangent, gains, gate_up_w, down):
+        spans, rows, width, hidden, count = self.spans, self.rows, self.width, self.hidden, self.count
+        total = 2 * spans * rows
+        vmem = pl.BlockSpec(memory_space=pltpu.VMEM)
+        hbm = pl.BlockSpec(memory_space=pl.ANY)
+        shape = jax.ShapeDtypeStruct
+        sems = pltpu.SemaphoreType.DMA((spans, count))
+        two = pltpu.SemaphoreType.DMA((2,))
+        return pl.pallas_call(
+            functools.partial(self.body, chips),
+            out_shape=[
+                shape((rows, width), BF16),
+                shape((rows, width), F32),
+                shape((1, width), F32),
+                shape((1, width), F32),
+                shape((total, width), BF16),
+                shape((total, width), BF16),
+                shape((total, 2 * hidden), BF16),
+                shape((total, hidden), BF16),
+                shape((total, width), BF16),
+            ],
+            in_specs=[hbm, vmem, vmem, vmem, hbm, hbm],
+            out_specs=[vmem] * 4 + [hbm] * 5,
+            scratch_shapes=[
+                pltpu.VMEM((rows, width), F32),
+                pltpu.VMEM((rows, width), F32),
+                pltpu.VMEM((total, width), BF16),
+                pltpu.VMEM((total // 2, width), BF16),
+                pltpu.VMEM((total // 2, width), BF16),
+                pltpu.VMEM((total // 2, width), BF16),
+                pltpu.VMEM((total, width), BF16),
+                pltpu.VMEM((total, 2 * hidden), F32),
+                pltpu.VMEM((self.batch, hidden), BF16),
+                pltpu.VMEM((self.batch, 2 * hidden), BF16),
+                pltpu.VMEM((width, 2 * hidden), BF16),
+                pltpu.VMEM((width, hidden), BF16),
+                sems,
+                two,
+                two,
+                two,
+            ]
+            + [sems] * 12
+            + [pltpu.SemaphoreType.DMA((chips,))] * 2,
+            compiler_params=pltpu.CompilerParams(
+                collective_id=2, has_side_effects=True, vmem_limit_bytes=62 << 20
+            ),
+            cost_estimate=pl.CostEstimate(
+                flops=36 * rows * spans * width * hidden, bytes_accessed=100 * width * width, transcendentals=0
+            ),
+            name="feed_forward",
+        )(partial, tokens, cotangent, gains, gate_up_w, down)
+
+
 def turn(values, cosine, sine):
     return values * cosine + pltpu.roll(values, HEAD_DIM // 2, 1) * sine
 
@@ -972,9 +1378,9 @@
 
 
 def attend_body(
-    spans, tokens, weights, out_w, gains, ids, cosine, sine,
-    partial_out, query_out, key_out, value_out, normed_out, factor_out, attended_out,
-    held, held_w, raw, given, own, arrived, load_sem, store_sem, send, recv,
+    spans, chips, tokens, weights, out_rows, gains, ids, cosine, sine,
+    partial_out, out_w_out, query_out, key_out, value_out, normed_out, factor_out, attended_out,
+    held, held_w, raw, given, out_w, own, arrived, load_sem, store_sem, chip_send, chip_recv, send, recv,
 ):
     part = out_w.shape[0]
     total_rows = raw.shape[0]
@@ -983,6 +1389,21 @@
     tiles = total_rows // ROW_TILE
     stats = Stats(spans, own, arrived, send, recv)
     stats.greet()
+    chip = lax.axis_index("chip")
+    shard = out_rows.shape[0]
+    here = pl.ds(pl.multiple_of(chip * shard, shard), shard)
+
+    def chip_copy(s):
+        return pltpu.make_async_remote_copy(
+            src_ref=out_rows, dst_ref=out_w.at[here], send_sem=chip_send.at[s], recv_sem=chip_recv.at[s],
+            device_id={"chip": lax.rem(chip + s, chips)}, device_id_type=MESH_ID,
+        )
+
+    for s in range(1, chips):
+        pl.semaphore_signal(
+            pltpu.get_barrier_semaphore(), 1, device_id={"chip": lax.rem(chip + s, chips)}, device_id_type=MESH_ID
+        )
+    out_w[here, :] = out_rows[...]
 
     def at(i):
         return pl.ds(pl.multiple_of(i * ROW_TILE, ROW_TILE), ROW_TILE)
@@ -998,6 +1419,9 @@
         load_rows(i).start()
 
     pick = member_rows(part)
+    pl.semaphore_wait(pltpu.get_barrier_semaphore(), 2 * spans - 1 + chips - 1)
+    for s in range(1, chips):
+        chip_copy(s).start()
     load_w.wait()
 
     @pl.loop(0, tiles)
@@ -1008,7 +1432,6 @@
         both = values[:, : 2 * part]
         own[:, at(i)] = row_sums(pick, both * both)
 
-    stats.meet()
     stats.start()
 
     @pl.loop(0, tiles)
@@ -1032,6 +1455,9 @@
             query_out[at(i), head] = turn(scaled[:, head], cosine[place, :], sine[place, :]).astype(BF16)
             key_out[at(i), head] = turn(scaled[:, low], cosine[place, :], sine[place, :]).astype(BF16)
 
+    for s in range(1, chips):
+        chip_copy(s).wait()
+    out_w_out[...] = out_w[...]
     block = QUERY_BLOCK
     for seq in range(2):
         for count in range(length // block):
@@ -1051,17 +1477,18 @@
         pltpu.make_async_copy(given.at[i % 2], partial_out.at[at(i)], store_sem.at[i]).wait()
 
 
-def attend(spans, tokens, weights, out_w, gains, ids, cosine, sine):
+def attend(spans, chips, tokens, weights, out_rows, gains, ids, cosine, sine):
     total_rows, width = tokens.shape
-    part = out_w.shape[0]
+    part = out_rows.shape[0] * chips
     tiles = total_rows // ROW_TILE
     vmem = pl.BlockSpec(memory_space=pltpu.VMEM)
     hbm = pl.BlockSpec(memory_space=pl.ANY)
     shape = jax.ShapeDtypeStruct
     return pl.pallas_call(
-        functools.partial(attend_body, spans),
+        functools.partial(attend_body, spans, chips),
         out_shape=[
             shape((total_rows, width), BF16),
+            shape((part, width), BF16),
             shape((total_rows, part), BF16),
             shape((total_rows, part), BF16),
             shape((total_rows, part), BF16),
@@ -1070,21 +1497,24 @@
             shape((total_rows, part), BF16),
         ],
         in_specs=[hbm, hbm] + [vmem] * 5,
-        out_specs=[hbm] + [vmem] * 6,
+        out_specs=[hbm] + [vmem] * 7,
         scratch_shapes=[
             pltpu.VMEM((total_rows, width), BF16),
             pltpu.VMEM(weights.shape, BF16),
             pltpu.VMEM((total_rows, 3 * part), F32),
             pltpu.VMEM((2, ROW_TILE, width), BF16),
+            pltpu.VMEM((part, width), BF16),
             *stats_scratch(spans, total_rows)[:2],
             pltpu.SemaphoreType.DMA((tiles + 1,)),
             pltpu.SemaphoreType.DMA((tiles,)),
+            pltpu.SemaphoreType.DMA((chips,)),
+            pltpu.SemaphoreType.DMA((chips,)),
             *stats_scratch(spans, total_rows)[2:],
         ],
         compiler_params=pltpu.CompilerParams(collective_id=8, has_side_effects=True, vmem_limit_bytes=56 << 20),
         cost_estimate=pl.CostEstimate(flops=2 * total_rows * width * 5 * part, bytes_accessed=0, transcendentals=0),
         name="attend",
-    )(tokens, weights, out_w, gains, ids, cosine, sine)
+    )(tokens, weights, out_rows, gains, ids, cosine, sine)
 
 
 def attend_back_body(
@@ -1249,12 +1679,7 @@
     qkv_cut = qkv_cut.reshape(members, qkv_rows, 3 * part)
     chips = lax.axis_size("chip")
     assert chips == spans
-    spread = lambda reduce, row_fn, n_in, n_out, gain: Exchange(
-        spans, rows, width, PIECE, reduce, True, row_fn, n_in, n_out, gain
-    )
     own = jax.ShapeDtypeStruct((rows, width), F32)
-    own_low = jax.ShapeDtypeStruct((rows, width), BF16)
-    one = jax.ShapeDtypeStruct((1, width), F32)
     qkv_w, ids, tokens_all = Exchange(
         spans, rows, width, PIECE, False, True, pass_tokens, 1, 0, None,
         QkvWeights(spans, chips, qkv_cut, jnp.broadcast_to(segment, (8, rows))),
@@ -1262,49 +1687,23 @@
     swaps = [
         (m * spans + a, a * members + m) for m in range(members) for a in range(chips)
     ]
-    out_w = gather(lax.ppermute(w_out, ALL, swaps), "chip")
-
-    hidden = w_gate.shape[1] // cores
+    out_rows = lax.ppermute(w_out, ALL, swaps)
+
     gate_up, down = split_columns(w_gate, w_up, w_down_t)
-    gate_up_w, down_w = gather(gate_up, "chip"), gather(down, "chip")
+    gate_up_w = gather(gate_up, "chip")
 
     cosine, sine = rope_tables(jnp.arange(length, dtype=F32))
     half = jnp.arange(HEAD_DIM) < HEAD_DIM // 2
     sine = jnp.where(half[None, :], -sine, sine)
-    out_part, *saved = attend(spans, tokens_all, qkv_w, out_w, gains, ids, cosine, sine)
-    residual, projected, residual_all = spread(True, after_projected, 2, 2, None).call(
-        "sum_projected", 2, out_part, [tokens, gains], [own, own]
+    out_part, out_w, *saved = attend(spans, chips, tokens_all, qkv_w, out_rows, gains, ids, cosine, sine)
+    (
+        output, residual_grad, gain_feed, gain_attn, residual_all, feed_grad_all, gate_up_grad, activated, projected_all
+    ) = Middle(spans, rows, width, w_gate.shape[1] // cores, BATCH_PIECE).call(
+        chips, out_part, tokens, cotangent[0], gains, gate_up_w, down
     )
-
-    gate_up_out = dot(residual_all, gate_up_w)
-    gate, up_part = gate_up_out[:, :hidden], gate_up_out[:, hidden:]
-    sigmoid = 1.0 / (1.0 + jnp.exp(-gate))
-    activated = (gate * sigmoid * up_part).astype(BF16)
-    output, gain_feed, feed_grad_all = spread(True, after_feed, 3, 2, 1).call(
-        "sum_feed",
-        3,
-        dot_rows(activated, down_w).astype(BF16),
-        [residual, cotangent[0], gains],
-        [own_low, one],
-    )
-
-    act_grad = dot(feed_grad_all, down_w)
-    gate_grad = act_grad * up_part * sigmoid * (1.0 + gate * (1.0 - sigmoid))
-    up_grad = act_grad * (gate * sigmoid)
-    gate_up_grad = jnp.concatenate([gate_grad.astype(BF16), up_grad.astype(BF16)], 1)
-    back_part = dot_rows(gate_up_grad, gate_up_w).astype(BF16)
     down_part = dot_first(feed_grad_all, activated).astype(BF16)
     gate_up_part = dot_first(residual_all, gate_up_grad).astype(BF16)
-    back_part, down_part, gate_up_part = lax.optimization_barrier((back_part, down_part, gate_up_part))
     gate_up_sum, down_sum = scatter_sum(gate_up_part, "chip"), scatter_sum(down_part, "chip")
-    residual_grad, gain_attn, projected_all = spread(True, after_back, 3, 2, 1).call(
-        "sum_back",
-        4,
-        back_part,
-        [projected, cotangent[0], gains],
-        [own, one],
-    )
-
     input_part, qkv_part, out_grads, gain_sums = attend_back(
         spans, projected_all, tokens_all, qkv_w, out_w, gains, ids, cosine, sine, saved
     )

time: 597 us -> 581 us (0.973); the launches traced: 587 us -> 581 us
  waiting for transfers between devices: 1.27 us -> 50 us
  matrix products: 69.2 us -> 23.5 us
  other arithmetic: 8.11 us -> 1.99 us
    pallas_call x1 -> x2, Pallas kernels: 26.1 us -> 245 us  [the longest x1 207 us: call(): pl.pallas_call(functools.partial(self.body, chips), out_shape=[shape((row...]
    pallas_call x5 -> x2, Pallas kernels: 390 us -> 179 us  [call(): pl.pallas_call(self.body, out_shape=shapes, in_specs=in_specs, out_specs=...]
    dot_general x4 -> x0, matrix products: 49 us -> none  [the longest x2 26.3 us: dot(): return jnp.dot(left, right, preferred_element_type=F32)]
    reduce_scatter x2, waiting for transfers between devices: 0.01 us -> 29.6 us  [scatter_sum(): return lax.psum_scatter(values, axes, scatter_dimension=0, tiled=True)]
    all_gather x3 -> x1, waiting for transfers between devices: 0.01 us -> 20.4 us  [gather(): return lax.all_gather(values, axes, axis=0, tiled=True)]
    pallas_call x1, Pallas kernels: 11.1 us -> 3.88 us  [split_columns(): pl.pallas_call(split_body, out_shape=[jax.ShapeDtypeStruct((2 * rows, wid...]
    convert_element_type x1 -> x0, other arithmetic: 6.14 us -> none  [per_device(): activated = (gate * sigmoid * up_part).astype(BF16)]
    unnamed x55 -> x45, local copies, waits for them, and re-layouts: 23.8 us -> 20.9 us
  transfers between devices with their start and end apart: 6 -> 4, of which waited for: 0 -> 2; matrix products, arithmetic and copies ran while one was open for 4% -> 3% of each run, Pallas kernels for 65% -> 43%
where the time goes in v6:
time: 581 us
  Pallas kernels  467 us (80%)
  waiting for transfers between devices  50 us (9%)
  matrix products  23.5 us (4%)
  local copies, waits for them, and re-layouts  23 us (4%)
  between operations  14 us (2%)
    pallas_call x1, Pallas kernels, call(): pl.pallas_call(functools.partial(self.body, chips), out_shape=[shape((row...  207 us
    pallas_call x2, Pallas kernels, call(): pl.pallas_call(self.body, out_shape=shapes, in_specs=in_specs, out_specs=...  179 us
    pallas_call x1, Pallas kernels, attend(): pl.pallas_call(functools.partial(attend_body, spans, chips), out_shape=[s...  37.9 us
    pallas_call x1, Pallas kernels, attend_back(): pl.pallas_call(functools.partial(attend_back_body, spans), out_shape=[sha...  35.3 us
    reduce_scatter x2, waiting for transfers between devices, scatter_sum(): return lax.psum_scatter(values, axes, scatter_dimension=0, tiled=True)  29.6 us
    dot_general x2, matrix products, dot_first(): lax.dot_general(left, right, (((0,), (0,)), ((), ())), preferred_element_...  23.5 us
    unnamed x45, local copies, waits for them, and re-layouts  20.9 us
    all_gather x1, waiting for transfers between devices, gather(): return lax.all_gather(values, axes, axis=0, tiled=True)  20.4 us
  transfers between devices with their start and end apart: 4, of which 2 were waited for; matrix products, arithmetic and copies ran while one was open for 3% of the time, Pallas kernels for 43%

profile of v6, /device:TPU:0, one launch (start us, length us, event | category | flops | bytes accessed | tf_op | source)
XLA Modules:
  0.0 580.8 jit_solution(15115093021805116589)
XLA Ops:
  7.2 1.2 copy-done.1
  8.4 1.2 copy-done.2
  9.7 1.2 copy-done.3
  10.9 3.9 split_columns.1
  15.8 1.5 collective-permute-start
  19.9 70.1 %gather_tokens.1 = (bf16[2048,768]{1,0:T(8,128)(2,1)S(1)}, s32[64,128]{1,0:T(8,128)S(1)}, bf16[1024,2048]{1,0:T(8,128)(2,1)}) custom-call(bf16[128,2048]{1,0:T(8,128)(2,1)S(1)} %bitcast.25, bf16[8,64,768]{2,1,0:T(8,128)(2,1)S(1)} %reshape.42.refs_1_, s32[8,128]{1,0:T(8,128)S(1)} %broadcast_in_dim.28.refs_2_), custom_call_target="tpu_custom_call" | custom-call | bytes 125829120 | tf_op jit(solution)/shard_map/gather_tokens/pallas_call | solution.py:379
  90.1 1.6 copy-done.10
  92.7 37.9 %attend.1 = (bf16[1024,2048]{1,0:T(8,128)(2,1)}, bf16[256,2048]{1,0:T(8,128)(2,1)}, bf16[1024,256]{1,0:T(8,128)(2,1)}, bf16[1024,256]{1,0:T(8,128)(2,1)}, bf16[1...) custom-call(bf16[1024,2048]{1,0:T(8,128)(2,1)} %get-tuple-element.41.tokens, ...), custom_call_target="tpu_custom_call" | custom-call | flops 5368709120 | tf_op jit(solution)/shard_map/attend/pallas_call | solution.py:1487
  130.6 20.4 %all-gather.2.cloned.1.call-done.gate_up_w = bf16[2048,2048]{1,0:T(8,128)(2,1)} async-done(((bf16[512,2048]{1,0:T(8,128)(2,1)}), bf16[2048,2048]{1,0:T(8,128)(2,1)}) %all-gather.2.cloned.1.call-update) | async-done | bytes 8388624 | tf_op jit(solution)/shard_map/all_gather | solution.py:873
  151.0 206.7 %feed_forward.1 = (bf16[128,2048]{1,0:T(8,128)(2,1)}, f32[128,2048]{1,0:T(8,128)}, f32[1,2048]{1,0:T(1,128)}, f32[1,2048]{1,0:T(1,128)}, bf16[1024,2048]{1,0:T(8...) custom-call(bf16[1024,2048]{1,0:T(8,128)(2,1)} %get-tuple-element.44, ...), custom_call_target="tpu_custom_call" | custom-call | flops 38654705664 | bytes 419430400 | tf_op jit(solution)/shard_map/feed_forward/pallas_call | solution.py:1241
  357.7 9.4 %convolution_convert_fusion.1 = bf16[2048,1024]{1,0:T(8,128)(2,1)} fusion(bf16[1024,2048]{1,0:T(8,128)(2,1)} %get-tuple-element.68, bf16[1024,1024]{1,0:T(8,128)(2,1)} %get-tuple-element.69), kind=kOutput, calls=%fused_computation.1 | convolution fusion | flops 4297064448 | bytes 10485760 | tf_op jit(solution)/shard_map/dot_general | solution.py:869
  367.4 14.1 %convolution_convert_fusion = bf16[2048,2048]{1,0:T(8,128)(2,1)} fusion(bf16[1024,2048]{1,0:T(8,128)(2,1)} %get-tuple-element.66, bf16[1024,2048]{1,0:T(8,128)(2,1)} %get-tuple-element.67), kind=kOutput, calls=%fused_computation | convolution fusion | flops 8594128896 | bytes 16777216 | tf_op jit(solution)/shard_map/dot_general | solution.py:869
  381.5 35.3 %attend_back.1 = (bf16[1024,2048]{1,0:T(8,128)(2,1)}, bf16[2048,768]{1,0:T(8,128)(2,1)}, bf16[256,2048]{1,0:T(8,128)(2,1)}, f32[8,512]{1,0:T(8,128)}) custom-call(bf16[1024,2048]{1,0:T(8,128)(2,1)} %get-tuple-element.48.grads, bf16[1024,2048]{1,0:T(8,128)(2,1)} %get-tuple-element.41.tokens, bf16[2048,768]{1,0:T(8,128)(2,1)} %copy-done.10, ...), custom_call_target="tpu_custom_call" | custom-call | flops 8589934592 | tf_op jit(solution)/shard_map/attend_back/pallas_call | solution.py:1639
  417.6 1.3 copy-done.6
  418.9 108.9 %sum_input.1 = (f32[128,2048]{1,0:T(8,128)S(1)}, f32[64,6144]{1,0:T(8,128)S(1)}, f32[4,16,128]{2,1,0:T(8,128)S(1)}, f32[64,2048]{1,0:T(8,128)S(1)}) custom-call(bf16[1024,2048]{1,0:T(8,128)(2,1)} %get-tuple-element.56.refs_0_, f32[128,2048]{1,0:T(8,128)S(1)} %copy-done.5, bf16[2048,768]{1,0:T(8,128)(2,1)} %get-tuple-element.58.refs_2_, ...), custom_call_target="tpu_custom_call" | custom-call | bytes 209715200 | tf_op jit(solution)/shard_map/sum_input/pallas_call | solution.py:379
  529.4 29.6 %reduce-scatter.3.cloned.1.call-done.gate_up = bf16[512,2048]{1,0:T(8,128)(2,1)} async-done(((bf16[2048,2048]{1,0:T(8,128)(2,1)}), bf16[512,2048]{1,0:T(8,128)(2,1)}) %reduce-scatter.3.cloned.1.call-update) | async-done | bytes 2097168 | tf_op jit(solution)/shard_map/reduce_scatter | solution.py:877
  559.0 1.6 copy-done
  560.6 1.2 copy-done.4
  561.8 3.7 join_columns.1
  565.5 1.9 copy.32
  568.4 1.1 copy.34
  570.3 1.3 copy.36
  571.6 1.3 copy.37
  572.9 1.3 copy.38
  (51 shorter events, 9.0 us)
Async XLA Ops:
  7.2 143.8 %all-gather.2.cloned.1.call-start = ((), (), s32[]{:S(2)}) async-start(), calls=%async_computation.2 | async-start | bytes 10485760 | tf_op jit(solution)/shard_map/all_gather | solution.py:873
  7.2 1.2 copy-start.1
  8.4 1.2 copy-start.2
  9.7 1.2 copy-start.3
  10.9 4.9 copy-start.17
  10.9 7.5 %copy-start.13 = (bf16[64,6144]{1,0:T(8,128)(2,1)S(1)}, bf16[64,6144]{1,0:T(8,128)(2,1)}, u32[]{:S(2)}) copy-start(bf16[64,6144]{1,0:T(8,128)(2,1)} %param.11) | copy-start | bytes 2359300
  14.8 1.0 copy-start.11
  15.8 4.1 copy-start.16
  15.8 4.1 copy-start.9
  15.8 513.6 %reduce-scatter.5.cloned.1.call-start = ((), (), s32[]{:S(2)}) async-start(), calls=%async_computation.4 | async-start | bytes 5242880 | tf_op jit(solution)/shard_map/reduce_scatter | solution.py:877
  15.8 76.9 %collective-permute-start = (bf16[64,2048]{1,0:T(8,128)(2,1)S(1)}, bf16[64,2048]{1,0:T(8,128)(2,1)}, u32[]{:S(2)}, u32[]{:S(2)}) collective-permute-start(bf16[64,2048]{1,0:T(8,128)(2,1)S(1)} %copy-done.17), channel_id=1, source_target_pairs={{0,0},{1,8},{2,16},{3,24},{4,1},{5,9},{6,17},{7,25},{8,2},{9,10},{... | collective-permute-start | bytes 786440 | tf_op jit(solution)/shard_map/ppermute | solution.py:1690
  90.1 1.6 copy-start.10
  91.7 1.0 copy-start.12
  367.1 191.9 %reduce-scatter.3.cloned.1.call-start = ((), (), s32[]{:S(2)}) async-start(), calls=%async_computation.3 | async-start | bytes 10485760 | tf_op jit(solution)/shard_map/reduce_scatter | solution.py:877
  381.5 36.1 %copy-start.14 = (f32[1,2048]{1,0:T(1,128)S(1)}, f32[1,2048]{1,0:T(1,128)}, u32[]{:S(2)}) copy-start(f32[1,2048]{1,0:T(1,128)} %get-tuple-element.60) | copy-start | bytes 24580
  381.5 36.1 %copy-start.15 = (f32[1,2048]{1,0:T(1,128)S(1)}, f32[1,2048]{1,0:T(1,128)}, u32[]{:S(2)}) copy-start(f32[1,2048]{1,0:T(1,128)} %get-tuple-element.59) | copy-start | bytes 24580
  381.5 36.1 %copy-start.5 = (f32[128,2048]{1,0:T(8,128)S(1)}, f32[128,2048]{1,0:T(8,128)}, u32[]{:S(2)}) copy-start(f32[128,2048]{1,0:T(8,128)} %get-tuple-element.57.refs_1_) | copy-start | bytes 3145732
  417.6 1.3 copy-start.6
  527.8 1.0 copy-start.7
  559.0 1.6 copy-start
  560.6 1.2 copy-start.4
  561.8 5.6 copy-start.8
Sparse Core Ops, SparseCore 0:
  15.9 135.0 all-gather.1
  367.2 51.1 reduce-scatter.4
  421.8 137.1 reduce-scatter.2
